TPU v7x, 128 devices: a whole 4x4x4 slice. The times are simulated.
128 devices in a mesh: prow: 8 (over z, core), pcol: 16 (over y, x).
Axes of the slice: x: 4, y: 4, z: 4, core: 2. Of those that a mesh axis runs over, the one named last changes fastest.
Arguments:
- window_rhs: float32 [64, 8192], P(None, 'prow'), may hold values from -6 to 6
- past_solution: float32 [64, 32768], P(None, 'pcol'), may hold values from -6 to 6
- past_panel: float32 [8192, 32768], P('prow', 'pcol'), may hold values from -0.03125 to 0.03125
- window_panel: float32 [8, 1024, 16, 1024], P('prow', None, 'pcol'), may hold values from -0.09375 to 0.09375
- diag_inverse: float32 [8, 1024, 1024], P('prow'), may hold values from -1 to 1.5, as said below
- tile_list: int32 [128, 2], P(('prow', 'pcol')), may hold values from 0 to 63
- neighbor_list: int32 [128, 2, 8], P(('prow', 'pcol')), may hold values from 0 to 63
- force_constants: float32 [128, 2, 8, 128, 128], P(('prow', 'pcol')), may hold values from -0.1875 to 0.1875
Outputs:
- solution: float32 [64, 8192], P(None, 'prow')
- residual_forces: float32 [128, 2, 64, 128], P(('prow', 'pcol'))
Inputs may be any that keep to these rules, and one draw needn't show every extreme that they name: `diag_inverse`: each block is lower triangular, with diagonal entries from 0.6 to 1.4.
All inputs are finite; a program needn't handle non-finite values.
Results may differ from a plain program's by a relative error of at most 0.00011.
Values sent between devices are 32-bit elements; how exact they have to be, the bound alone decides.
No kernel may reach another device: no remote copies, remote signals or barrier semaphores. Data moves between devices by JAX's collectives and lax.ppermute only.
A program may use at most 128 MiB of HBM per device.

v0:
```python
import jax
import jax.numpy as jnp
from jax import lax
from jax.sharding import Mesh
from jax.sharding import PartitionSpec as P

PROW = ("prow_0", "prow_1")
PCOL = ("pcol_0", "pcol_1")
PROW_PCOL = ("prow_0", "prow_1", "pcol_0", "pcol_1")


def laid_out(pieces, dim):
    dims = list(pieces.shape[1:])
    dims[dim] *= pieces.shape[0]
    return jnp.moveaxis(pieces, 0, dim).reshape(dims)


def from_everyone(x, axis):
    count = lax.axis_size(axis)
    return lax.all_to_all(jnp.broadcast_to(x[None], (count, *x.shape)), axis, 0, 0, tiled=True)


def gather_directly(x, axis, dim):
    return laid_out(from_everyone(x, axis), dim)


def padded_to(lines, count):
    spare = -len(lines) % count
    return jnp.pad(lines, [(0, spare)] + [(0, 0)] * (lines.ndim - 1))


def gather_axes(x, axes, dim):
    far, near = axes
    initial = from_everyone(x, far)
    pieces = jnp.swapaxes(from_everyone(initial, near), 0, 1)
    return laid_out(pieces.reshape(-1, *x.shape), dim)


def cut_along(x, dim, count):
    dims = x.shape
    pieces = x.reshape(*dims[:dim], count, dims[dim] // count, *dims[dim + 1 :])
    return jnp.moveaxis(pieces, dim, 0)


def summed_on_arrival(x, axis, dim):
    pieces = cut_along(x, dim, lax.axis_size(axis))
    arrived = lax.all_to_all(pieces, axis, split_axis=0, concat_axis=0, tiled=True)
    return arrived.sum(axis=0)


def sum_in_two_steps(x, axes, dim):
    far, near = axes
    pieces = cut_along(x, dim, lax.axis_size(far))
    nearer = summed_on_arrival(pieces, near, dim + 1)
    arrived = lax.all_to_all(nearer, far, split_axis=0, concat_axis=0, tiled=True)
    return arrived.sum(axis=0)


def total_of(x, axes):
    lines = x.reshape(-1)
    padded = padded_to(lines, lax.axis_size(axes[0]) * lax.axis_size(axes[1]))
    whole = gather_axes(sum_in_two_steps(padded, axes, 0), axes, 0)
    return lax.slice_in_dim(whole, 0, len(lines)).reshape(x.shape)


def right_product(left, right):
    return lax.dot_general(
        left,
        right,
        (((1,), (1,)), ((), ())),
        precision=lax.Precision.HIGHEST,
        preferred_element_type=jnp.float32,
    )


def per_device(
    window_rhs,
    past_solution,
    past_panel,
    window_panel,
    diag_inverse,
    tile_list,
    neighbor_list,
    force_constants,
):
    row_index = lax.axis_index(PROW)
    col_index = lax.axis_index(PCOL)
    row_count = lax.axis_size(PROW)
    block_order = window_rhs.shape[1]
    full_rhs = gather_directly(window_rhs, PROW, 1)
    partial_value = right_product(past_solution, past_panel)
    block = window_panel[0, :, 0, :]
    inverse = diag_inverse[0]
    zeros_block = jnp.zeros(window_rhs.shape, jnp.float32)
    solved = []
    for step in range(row_count):
        own_rhs = jnp.where(col_index == 0, window_rhs, zeros_block)
        piece = lax.cond(
            row_index == step,
            lambda: right_product(own_rhs - partial_value, inverse),
            lambda: zeros_block,
        )
        current = total_of(piece, (("prow_0", "prow_1", "pcol_0"), "pcol_1"))
        partial_value = lax.cond(
            (col_index == step) & (row_index > step),
            lambda: partial_value + right_product(current, block),
            lambda: partial_value,
        )
        solved.append(current)
    whole_solution = jnp.concatenate(solved, axis=1)
    solution = lax.dynamic_slice_in_dim(whole_solution, row_index * block_order, block_order, 1)
    tile_width = force_constants.shape[-1]
    rhs_count = window_rhs.shape[0]
    tiles = whole_solution.reshape(rhs_count, -1, tile_width)
    rhs_tiles = full_rhs.reshape(rhs_count, -1, tile_width)
    near = tiles[:, neighbor_list[0]]
    term = jnp.einsum("rtnb,tnab->tra", near, force_constants[0], precision=lax.Precision.HIGHEST)
    own = jnp.transpose(rhs_tiles[:, tile_list[0]], (1, 0, 2))
    residual_forces = (own - term)[None]
    return (solution, residual_forces)


def solution(mesh):
    torus = Mesh(mesh.devices.reshape(4, 2, 4, 4), ("prow_0", "prow_1", "pcol_0", "pcol_1"))
    placed = (
        P(None, PROW),
        P(None, PCOL),
        P(PROW, PCOL),
        P(PROW, None, PCOL, None),
        P(PROW, None, None),
        P(PROW_PCOL, None),
        P(PROW_PCOL, None, None),
        P(PROW_PCOL, None, None, None, None),
    )
    return jax.shard_map(
        per_device,
        mesh=torus,
        in_specs=placed,
        out_specs=(P(None, PROW), P(PROW_PCOL, None, None, None)),
        check_vma=False,
    )
```

profile of v0, /device:TPU:1, one launch (start us, length us, event | category | flops | bytes accessed | tf_op | source)
XLA Modules:
  0.0 500.0 jit_solution(1447189618824765781)
XLA Ops:
  1.7 10.6 %fusion.20 = f32[64,1024]{1,0:T(8,128)S(1)} fusion(f32[64,2048]{1,0:T(8,128)} %param.39, f32[1024,2048]{1,0:T(8,128)} %param.40), kind=kOutput, calls=%fused_computation.61 | convolution fusion | flops 1610612736 | bytes 9175040 | tf_op jit(solution)/shard_map/dot_general | solution.py:67
  12.6 9.2 %all_to_all.205 = f32[4,32,512]{2,1,0:T(8,128)S(1)} all-to-all(f32[4,32,512]{2,1,0:T(8,128)S(1)} %copy.38), channel_id=1, replica_groups=mesh['prow_0'=4,'prow_1'=2,'pcol_0'=4,'pcol_1'=4] {'pcol_1'}, dimensions={0} | all-to-all | bytes 524288 | tf_op jit(solution)/shard_map/all_to_all | solution.py:47
  21.9 20.0 %all_to_all.206 = f32[32,1,512]{2,1,0:T(1,128)S(1)} all-to-all(f32[32,1,512]{2,1,0:T(1,128)S(1)} %all_to_all.132), channel_id=1, replica_groups=mesh['prow_0'=4,'prow_1'=2,'pcol_0'=4,'pcol_1'=4] {'prow_0','prow_1','pc..., dimensions={0} | all-to-all | bytes 131072 | tf_op jit(solution)/shard_map/all_to_all | solution.py:55
  42.0 11.0 %all_to_all.207 = f32[32,1,512]{2,1,0:T(1,128)S(1)} all-to-all(f32[32,1,512]{2,1,0:T(1,128)S(1)} %broadcast_in_dim.79), channel_id=1, replica_groups=mesh['prow_0'=4,'prow_1'=2,'pcol_0'=4,'pcol_1'=4] {'prow_0','prow_1','pc..., dimensions={0} | all-to-all | bytes 131072 | tf_op jit(solution)/shard_map/all_to_all | solution.py:20
  53.7 3.4 all-to-all-start.3
  57.1 5.1 %copy.99 = f32[1,1024,1,1024]{3,1,2,0:T(8,128)} copy(f32[1,1024,1,1024]{3,2,1,0:T(1,128)} %param.41) | data formatting | bytes 8388608
  63.5 6.5 %conditional.16 = (f32[64,1024]{1,0:T(8,128)S(1)}) conditional(s32[]{:T(128)} %convert_element_type.47, f32[64,1024]{1,0:T(8,128)S(1)} %fusion.20, (f32[64,1024]{1,0:T(8,128)S(1)}, f32[1024,1024]{1,0:T(8,128)}, f32[64,1024]{1,0:T(8,128)S(1)}) %tuple.161), branch_computations={%region_4.5_spmd, %region_5.6_spmd} | conditional | flops 805371904 | bytes 4980744 | solution.py:104
  63.7 6.3 %convolution_add_fusion = f32[64,1024]{1,0:T(8,128)S(1)} fusion(f32[64,1024]{1,0:T(8,128)S(1)} %get-tuple-element.140, f32[64,1024]{1,0:T(8,128)S(1)} %get-tuple-element.142, f32[1024,1024]{1,0:T(8,128)} %get-tuple-element.143), kind=kOutput, calls=%fused_computation.4 | convolution fusion | flops 805371904 | bytes 4980736 | tf_op jit(solution)/shard_map/cond/branch_1_fun/dot_general | solution.py:67
  70.0 6.3 %conditional.17 = (f32[64,1024]{1,0:T(8,128)S(1)}) conditional(s32[]{:T(128)} %convert_element_type.46, () %tuple.100, (f32[64,1024]{1,0:T(8,128)S(1)}, f32[64,1024]{1,0:T(8,128)S(1)}, f32[1024,1024]{1,0:T(8,128)}) %tuple.154), branch_computations={%region_6.7_spmd, %region_7.8_spmd} | conditional | flops 805371904 | bytes 4980744 | solution.py:98
  70.1 6.3 %fusion.2 = f32[64,1024]{1,0:T(8,128)S(1)} fusion(f32[1024,1024]{1,0:T(8,128)} %get-tuple-element.150, f32[64,1024]{1,0:T(8,128)S(1)} %get-tuple-element.144, f32[64,1024]{1,0:T(8,128)S(1)} %get-tuple-element.145), kind=kOutput, calls=%fused_computation.5 | convolution fusion | flops 805371904 | bytes 4980736 | tf_op jit(solution)/shard_map/cond/branch_1_fun/dot_general | solution.py:67
  76.6 7.9 %all_to_all.208 = f32[4,32,512]{2,1,0:T(8,128)S(1)} all-to-all(f32[4,32,512]{2,1,0:T(8,128)S(1)} %copy.40), channel_id=1, replica_groups=mesh['prow_0'=4,'prow_1'=2,'pcol_0'=4,'pcol_1'=4] {'pcol_1'}, dimensions={0} | all-to-all | bytes 524288 | tf_op jit(solution)/shard_map/all_to_all | solution.py:47
  84.5 9.0 %all_to_all.209 = f32[32,1,512]{2,1,0:T(1,128)S(1)} all-to-all(f32[32,1,512]{2,1,0:T(1,128)S(1)} %all_to_all.137), channel_id=1, replica_groups=mesh['prow_0'=4,'prow_1'=2,'pcol_0'=4,'pcol_1'=4] {'prow_0','prow_1','pc..., dimensions={0} | all-to-all | bytes 131072 | tf_op jit(solution)/shard_map/all_to_all | solution.py:55
  93.7 11.0 %all_to_all.210 = f32[32,1,512]{2,1,0:T(1,128)S(1)} all-to-all(f32[32,1,512]{2,1,0:T(1,128)S(1)} %broadcast_in_dim.82), channel_id=1, replica_groups=mesh['prow_0'=4,'prow_1'=2,'pcol_0'=4,'pcol_1'=4] {'prow_0','prow_1','pc..., dimensions={0} | all-to-all | bytes 131072 | tf_op jit(solution)/shard_map/all_to_all | solution.py:20
  105.4 3.4 all-to-all-start.7
  108.8 6.0 %all-to-all-done.7 = f32[4,32,512]{2,1,0:T(8,128)S(1)} async-done(((f32[4,32,512]{2,1,0:T(8,128)}), f32[4,32,512]{2,1,0:T(8,128)S(1)}, u32[]{:S(2)}, u32[]{:S(2)}) %all-to-all-start.7) | async-done | bytes 262176 | tf_op jit(solution)/shard_map/all_to_all | solution.py:20
  115.7 7.9 %all_to_all.211 = f32[4,32,512]{2,1,0:T(8,128)S(1)} all-to-all(f32[4,32,512]{2,1,0:T(8,128)S(1)} %copy.42), channel_id=1, replica_groups=mesh['prow_0'=4,'prow_1'=2,'pcol_0'=4,'pcol_1'=4] {'pcol_1'}, dimensions={0} | all-to-all | bytes 524288 | tf_op jit(solution)/shard_map/all_to_all | solution.py:47
  123.7 23.6 %all_to_all.212 = f32[32,1,512]{2,1,0:T(1,128)S(1)} all-to-all(f32[32,1,512]{2,1,0:T(1,128)S(1)} %all_to_all.142), channel_id=1, replica_groups=mesh['prow_0'=4,'prow_1'=2,'pcol_0'=4,'pcol_1'=4] {'prow_0','prow_1','pc..., dimensions={0} | all-to-all | bytes 131072 | tf_op jit(solution)/shard_map/all_to_all | solution.py:55
  147.4 11.0 %all_to_all.213 = f32[32,1,512]{2,1,0:T(1,128)S(1)} all-to-all(f32[32,1,512]{2,1,0:T(1,128)S(1)} %broadcast_in_dim.85), channel_id=1, replica_groups=mesh['prow_0'=4,'prow_1'=2,'pcol_0'=4,'pcol_1'=4] {'prow_0','prow_1','pc..., dimensions={0} | all-to-all | bytes 131072 | tf_op jit(solution)/shard_map/all_to_all | solution.py:20
  159.1 3.4 all-to-all-start.11
  162.5 6.0 %all-to-all-done.11 = f32[4,32,512]{2,1,0:T(8,128)S(1)} async-done(((f32[4,32,512]{2,1,0:T(8,128)}), f32[4,32,512]{2,1,0:T(8,128)S(1)}, u32[]{:S(2)}, u32[]{:S(2)}) %all-to-all-start.11) | async-done | bytes 262176 | tf_op jit(solution)/shard_map/all_to_all | solution.py:20
  169.7 7.9 %all_to_all.214 = f32[4,32,512]{2,1,0:T(8,128)S(1)} all-to-all(f32[4,32,512]{2,1,0:T(8,128)S(1)} %copy.44), channel_id=1, replica_groups=mesh['prow_0'=4,'prow_1'=2,'pcol_0'=4,'pcol_1'=4] {'pcol_1'}, dimensions={0} | all-to-all | bytes 524288 | tf_op jit(solution)/shard_map/all_to_all | solution.py:47
  177.7 21.1 %all_to_all.215 = f32[32,1,512]{2,1,0:T(1,128)S(1)} all-to-all(f32[32,1,512]{2,1,0:T(1,128)S(1)} %all_to_all.147), channel_id=1, replica_groups=mesh['prow_0'=4,'prow_1'=2,'pcol_0'=4,'pcol_1'=4] {'prow_0','prow_1','pc..., dimensions={0} | all-to-all | bytes 131072 | tf_op jit(solution)/shard_map/all_to_all | solution.py:55
  198.9 11.0 %all_to_all.216 = f32[32,1,512]{2,1,0:T(1,128)S(1)} all-to-all(f32[32,1,512]{2,1,0:T(1,128)S(1)} %broadcast_in_dim.160), channel_id=1, replica_groups=mesh['prow_0'=4,'prow_1'=2,'pcol_0'=4,'pcol_1'=4] {'prow_0','prow_1','pc..., dimensions={0} | all-to-all | bytes 131072 | tf_op jit(solution)/shard_map/all_to_all | solution.py:20
  210.6 3.4 all-to-all-start.15
  214.0 6.0 %all-to-all-done.15 = f32[4,32,512]{2,1,0:T(8,128)S(1)} async-done(((f32[4,32,512]{2,1,0:T(8,128)}), f32[4,32,512]{2,1,0:T(8,128)S(1)}, u32[]{:S(2)}, u32[]{:S(2)}) %all-to-all-start.15) | async-done | bytes 262176 | tf_op jit(solution)/shard_map/all_to_all | solution.py:20
  222.9 7.9 %all_to_all.217 = f32[4,32,512]{2,1,0:T(8,128)S(1)} all-to-all(f32[4,32,512]{2,1,0:T(8,128)S(1)} %copy.46), channel_id=1, replica_groups=mesh['prow_0'=4,'prow_1'=2,'pcol_0'=4,'pcol_1'=4] {'pcol_1'}, dimensions={0} | all-to-all | bytes 524288 | tf_op jit(solution)/shard_map/all_to_all | solution.py:47
  230.9 24.9 %all_to_all.218 = f32[32,1,512]{2,1,0:T(1,128)S(1)} all-to-all(f32[32,1,512]{2,1,0:T(1,128)S(1)} %all_to_all.152), channel_id=1, replica_groups=mesh['prow_0'=4,'prow_1'=2,'pcol_0'=4,'pcol_1'=4] {'prow_0','prow_1','pc..., dimensions={0} | all-to-all | bytes 131072 | tf_op jit(solution)/shard_map/all_to_all | solution.py:55
  255.9 11.0 %all_to_all.219 = f32[32,1,512]{2,1,0:T(1,128)S(1)} all-to-all(f32[32,1,512]{2,1,0:T(1,128)S(1)} %broadcast_in_dim.163), channel_id=1, replica_groups=mesh['prow_0'=4,'prow_1'=2,'pcol_0'=4,'pcol_1'=4] {'prow_0','prow_1','pc..., dimensions={0} | all-to-all | bytes 131072 | tf_op jit(solution)/shard_map/all_to_all | solution.py:20
  267.6 3.4 all-to-all-start.19
  271.0 6.0 %all-to-all-done.19 = f32[4,32,512]{2,1,0:T(8,128)S(1)} async-done(((f32[4,32,512]{2,1,0:T(8,128)}), f32[4,32,512]{2,1,0:T(8,128)S(1)}, u32[]{:S(2)}, u32[]{:S(2)}) %all-to-all-start.19) | async-done | bytes 262176 | tf_op jit(solution)/shard_map/all_to_all | solution.py:20
  277.9 1.1 reshape_reshape_reshape.28
  280.0 1.8 reshape_reshape.32
  282.8 8.6 %all_to_all.220 = f32[4,32,512]{2,1,0:T(8,128)} all-to-all(f32[4,32,512]{2,1,0:T(8,128)S(1)} %copy.48), channel_id=1, replica_groups=mesh['prow_0'=4,'prow_1'=2,'pcol_0'=4,'pcol_1'=4] {'pcol_1'}, dimensions={0} | all-to-all | bytes 524288 | tf_op jit(solution)/shard_map/all_to_all | solution.py:47
  292.4 22.5 %all_to_all.221 = f32[32,1,512]{2,1,0:T(1,128)S(1)} all-to-all(f32[32,1,512]{2,1,0:T(1,128)S(1)} %all_to_all.157), channel_id=1, replica_groups=mesh['prow_0'=4,'prow_1'=2,'pcol_0'=4,'pcol_1'=4] {'prow_0','prow_1','pc..., dimensions={0} | all-to-all | bytes 131072 | tf_op jit(solution)/shard_map/all_to_all | solution.py:55
  315.0 11.0 %all_to_all.222 = f32[32,1,512]{2,1,0:T(1,128)S(1)} all-to-all(f32[32,1,512]{2,1,0:T(1,128)S(1)} %broadcast_in_dim.166), channel_id=1, replica_groups=mesh['prow_0'=4,'prow_1'=2,'pcol_0'=4,'pcol_1'=4] {'prow_0','prow_1','pc..., dimensions={0} | all-to-all | bytes 131072 | tf_op jit(solution)/shard_map/all_to_all | solution.py:20
  325.9 2.6 broadcast_in_dim.175
  328.5 4.8 all-to-all-start.32
  334.9 1.7 copy_dynamic-update-slice_fusion.7
  339.0 20.7 %all-to-all-done.32 = f32[8,64,1024]{2,1,0:T(8,128)} async-done(((f32[8,64,1024]{2,1,0:T(8,128)}), f32[8,64,1024]{2,1,0:T(8,128)}, u32[]{:S(2)}, u32[]{:S(2)}) %all-to-all-start.32) | async-done | bytes 2097184 | tf_op jit(solution)/shard_map/all_to_all | solution.py:20
  360.5 3.6 all-to-all-start.23
  364.9 4.2 copy.54
  369.1 2.7 reshape_reshape.35
  371.8 4.2 copy.55
  376.0 2.1 gather_fusion
  379.6 1.8 copy.50
  381.3 4.2 all-to-all-start.24
  386.3 4.8 all-to-all-done.24
  391.7 16.2 %all-to-all-start.25 = ((f32[32,1,512]{2,1,0:T(1,128)}), f32[32,1,512]{2,1,0:T(1,128)S(1)}, u32[]{:S(2)}, u32[]{:S(2)}) async-start(f32[32,1,512]{2,1,0:T(1,128)} %all_to_all.162), calls=%async_computation.25 | async-start | bytes 131072 | tf_op jit(solution)/shard_map/all_to_all | solution.py:55
  408.8 6.4 %all-to-all-done.25 = f32[32,1,512]{2,1,0:T(1,128)S(1)} async-done(((f32[32,1,512]{2,1,0:T(1,128)}), f32[32,1,512]{2,1,0:T(1,128)S(1)}, u32[]{:S(2)}, u32[]{:S(2)}) %all-to-all-start.25) | async-done | bytes 65568 | tf_op jit(solution)/shard_map/all_to_all | solution.py:55
  416.0 3.9 all-to-all-start.26
  420.6 6.6 %all-to-all-done.26 = f32[32,1,512]{2,1,0:T(1,128)S(1)} async-done(((f32[32,1,512]{2,1,0:T(1,128)}), f32[32,1,512]{2,1,0:T(1,128)S(1)}, u32[]{:S(2)}, u32[]{:S(2)}) %all-to-all-start.26) | async-done | bytes 65568 | tf_op jit(solution)/shard_map/all_to_all | solution.py:20
  428.0 3.4 all-to-all-start.27
  432.3 5.2 %all-to-all-done.27 = f32[4,32,512]{2,1,0:T(8,128)S(1)} async-done(((f32[4,32,512]{2,1,0:T(8,128)}), f32[4,32,512]{2,1,0:T(8,128)S(1)}, u32[]{:S(2)}, u32[]{:S(2)}) %all-to-all-start.27) | async-done | bytes 262176 | tf_op jit(solution)/shard_map/all_to_all | solution.py:20
  439.1 3.4 all-to-all-start.28
  443.2 4.8 all-to-all-done.28
  448.7 13.7 %all-to-all-start.29 = ((f32[32,1,512]{2,1,0:T(1,128)}), f32[32,1,512]{2,1,0:T(1,128)S(1)}, u32[]{:S(2)}, u32[]{:S(2)}) async-start(f32[32,1,512]{2,1,0:T(1,128)} %all_to_all.167), calls=%async_computation.29 | async-start | bytes 131072 | tf_op jit(solution)/shard_map/all_to_all | solution.py:55
  463.2 6.4 %all-to-all-done.29 = f32[32,1,512]{2,1,0:T(1,128)S(1)} async-done(((f32[32,1,512]{2,1,0:T(1,128)}), f32[32,1,512]{2,1,0:T(1,128)S(1)}, u32[]{:S(2)}, u32[]{:S(2)}) %all-to-all-start.29) | async-done | bytes 65568 | tf_op jit(solution)/shard_map/all_to_all | solution.py:55
  470.4 3.9 all-to-all-start.30
  475.1 6.6 %all-to-all-done.30 = f32[32,1,512]{2,1,0:T(1,128)S(1)} async-done(((f32[32,1,512]{2,1,0:T(1,128)}), f32[32,1,512]{2,1,0:T(1,128)S(1)}, u32[]{:S(2)}, u32[]{:S(2)}) %all-to-all-start.30) | async-done | bytes 65568 | tf_op jit(solution)/shard_map/all_to_all | solution.py:20
  482.4 3.4 all-to-all-start.31
  486.6 5.3 %all-to-all-done.31 = f32[4,32,512]{2,1,0:T(8,128)S(1)} async-done(((f32[4,32,512]{2,1,0:T(8,128)}), f32[4,32,512]{2,1,0:T(8,128)S(1)}, u32[]{:S(2)}, u32[]{:S(2)}) %all-to-all-start.31) | async-done | bytes 262176 | tf_op jit(solution)/shard_map/all_to_all | solution.py:20
  493.1 2.2 gather_fusion.1
  496.0 1.7 constant_dynamic-slice_fusion
  497.7 1.8 fusion.17
  (143 shorter events, 37.7 us)
Async XLA Ops:
  0.6 497.1 %copy-start = (f32[1,2,8,128,128]{4,3,2,1,0:T(8,128)S(1)}, f32[1,2,8,128,128]{4,3,2,1,0:T(8,128)}, u32[]{:S(2)}) copy-start(f32[1,2,8,128,128]{4,3,2,1,0:T(8,128)} %param.45) | copy-start | bytes 3145732
  53.7 9.5 %all-to-all-start.3 = ((f32[4,32,512]{2,1,0:T(8,128)}), f32[4,32,512]{2,1,0:T(8,128)S(1)}, u32[]{:S(2)}, u32[]{:S(2)}) async-start(f32[4,32,512]{2,1,0:T(8,128)} %broadcast_in_dim.81), calls=%async_computation.3 | async-start | bytes 524288 | tf_op jit(solution)/shard_map/all_to_all | solution.py:20
  105.4 9.5 %all-to-all-start.7 = ((f32[4,32,512]{2,1,0:T(8,128)}), f32[4,32,512]{2,1,0:T(8,128)S(1)}, u32[]{:S(2)}, u32[]{:S(2)}) async-start(f32[4,32,512]{2,1,0:T(8,128)} %broadcast_in_dim.84), calls=%async_computation.7 | async-start | bytes 524288 | tf_op jit(solution)/shard_map/all_to_all | solution.py:20
  159.1 9.5 %all-to-all-start.11 = ((f32[4,32,512]{2,1,0:T(8,128)}), f32[4,32,512]{2,1,0:T(8,128)S(1)}, u32[]{:S(2)}, u32[]{:S(2)}) async-start(f32[4,32,512]{2,1,0:T(8,128)} %broadcast_in_dim.87), calls=%async_computation.11 | async-start | bytes 524288 | tf_op jit(solution)/shard_map/all_to_all | solution.py:20
  168.7 0.7 copy-start.1
  210.6 9.5 %all-to-all-start.15 = ((f32[4,32,512]{2,1,0:T(8,128)}), f32[4,32,512]{2,1,0:T(8,128)S(1)}, u32[]{:S(2)}, u32[]{:S(2)}) async-start(f32[4,32,512]{2,1,0:T(8,128)} %broadcast_in_dim.162), calls=%async_computation.15 | async-start | bytes 524288 | tf_op jit(solution)/shard_map/all_to_all | solution.py:20
  220.3 0.7 copy-start.3
  267.6 9.5 %all-to-all-start.19 = ((f32[4,32,512]{2,1,0:T(8,128)}), f32[4,32,512]{2,1,0:T(8,128)S(1)}, u32[]{:S(2)}, u32[]{:S(2)}) async-start(f32[4,32,512]{2,1,0:T(8,128)} %broadcast_in_dim.165), calls=%async_computation.19 | async-start | bytes 524288 | tf_op jit(solution)/shard_map/all_to_all | solution.py:20
  328.5 4.8 copy-start.6
  328.5 4.9 copy-start.7
  328.5 31.2 %all-to-all-start.32 = ((f32[8,64,1024]{2,1,0:T(8,128)}), f32[8,64,1024]{2,1,0:T(8,128)}, u32[]{:S(2)}, u32[]{:S(2)}) async-start(f32[8,64,1024]{2,1,0:T(8,128)} %broadcast_in_dim.175), calls=%async_computation.32 | async-start | bytes 4194304 | tf_op jit(solution)/shard_map/all_to_all | solution.py:20
  334.2 4.0 copy-start.2
  360.5 17.8 %all-to-all-start.23 = ((f32[4,32,512]{2,1,0:T(8,128)}), f32[4,32,512]{2,1,0:T(8,128)S(1)}, u32[]{:S(2)}, u32[]{:S(2)}) async-start(f32[4,32,512]{2,1,0:T(8,128)} %broadcast_in_dim.168), calls=%async_computation.23 | async-start | bytes 524288 | tf_op jit(solution)/shard_map/all_to_all | solution.py:20
  371.8 6.4 %copy-start.4 = (f32[32,4,512]{2,1,0:T(4,128)S(1)}, f32[32,4,512]{2,1,0:T(4,128)}, u32[]{:S(2)}) copy-start(f32[32,4,512]{2,1,0:T(4,128)} %copy-done.3) | copy-start | bytes 786436
  378.7 30.0 %copy-start.5 = (f32[32,4,512]{2,1,0:T(4,128)S(1)}, f32[32,4,512]{2,1,0:T(4,128)}, u32[]{:S(2)}) copy-start(f32[32,4,512]{2,1,0:T(4,128)} %copy.47) | copy-start | bytes 786436
  381.3 9.7 %all-to-all-start.24 = ((f32[4,32,512]{2,1,0:T(8,128)}), f32[4,32,512]{2,1,0:T(8,128)S(1)}, u32[]{:S(2)}, u32[]{:S(2)}) async-start(f32[4,32,512]{2,1,0:T(8,128)} %copy.50), calls=%async_computation.24 | async-start | bytes 524288 | tf_op jit(solution)/shard_map/all_to_all | solution.py:47
  391.7 23.5 %all-to-all-start.25 = ((f32[32,1,512]{2,1,0:T(1,128)}), f32[32,1,512]{2,1,0:T(1,128)S(1)}, u32[]{:S(2)}, u32[]{:S(2)}) async-start(f32[32,1,512]{2,1,0:T(1,128)} %all_to_all.162), calls=%async_computation.25 | async-start | bytes 131072 | tf_op jit(solution)/shard_map/all_to_all | solution.py:55
  416.0 11.3 %all-to-all-start.26 = ((f32[32,1,512]{2,1,0:T(1,128)}), f32[32,1,512]{2,1,0:T(1,128)S(1)}, u32[]{:S(2)}, u32[]{:S(2)}) async-start(f32[32,1,512]{2,1,0:T(1,128)} %broadcast_in_dim.169), calls=%async_computation.26 | async-start | bytes 131072 | tf_op jit(solution)/shard_map/all_to_all | solution.py:20
  428.0 9.5 %all-to-all-start.27 = ((f32[4,32,512]{2,1,0:T(8,128)}), f32[4,32,512]{2,1,0:T(8,128)S(1)}, u32[]{:S(2)}, u32[]{:S(2)}) async-start(f32[4,32,512]{2,1,0:T(8,128)} %broadcast_in_dim.171), calls=%async_computation.27 | async-start | bytes 524288 | tf_op jit(solution)/shard_map/all_to_all | solution.py:20
  439.1 8.9 %all-to-all-start.28 = ((f32[4,32,512]{2,1,0:T(8,128)}), f32[4,32,512]{2,1,0:T(8,128)S(1)}, u32[]{:S(2)}, u32[]{:S(2)}) async-start(f32[4,32,512]{2,1,0:T(8,128)} %copy.52), calls=%async_computation.28 | async-start | bytes 524288 | tf_op jit(solution)/shard_map/all_to_all | solution.py:47
  448.7 21.0 %all-to-all-start.29 = ((f32[32,1,512]{2,1,0:T(1,128)}), f32[32,1,512]{2,1,0:T(1,128)S(1)}, u32[]{:S(2)}, u32[]{:S(2)}) async-start(f32[32,1,512]{2,1,0:T(1,128)} %all_to_all.167), calls=%async_computation.29 | async-start | bytes 131072 | tf_op jit(solution)/shard_map/all_to_all | solution.py:55
  470.4 11.3 %all-to-all-start.30 = ((f32[32,1,512]{2,1,0:T(1,128)}), f32[32,1,512]{2,1,0:T(1,128)S(1)}, u32[]{:S(2)}, u32[]{:S(2)}) async-start(f32[32,1,512]{2,1,0:T(1,128)} %broadcast_in_dim.172), calls=%async_computation.30 | async-start | bytes 131072 | tf_op jit(solution)/shard_map/all_to_all | solution.py:20
  482.4 9.5 %all-to-all-start.31 = ((f32[4,32,512]{2,1,0:T(8,128)}), f32[4,32,512]{2,1,0:T(8,128)S(1)}, u32[]{:S(2)}, u32[]{:S(2)}) async-start(f32[4,32,512]{2,1,0:T(8,128)} %broadcast_in_dim.174), calls=%async_computation.31 | async-start | bytes 524288 | tf_op jit(solution)/shard_map/all_to_all | solution.py:20
where the time goes:
time: 509 us; the launch traced here: 500 us
  blocking collectives  236 us (46%)
  waiting for transfers between devices  92 us (18%)
  starting transfers between devices  77.6 us (15%)
  local copies, waits for them, and re-layouts  63.6 us (12%)
  matrix products  25 us (5%)
    all_to_all x6, blocking collectives, sum_in_two_steps(): lax.all_to_all(nearer, far, split_axis=0, concat_axis=0, tiled=True)  121 us
    all_to_all x11, waiting for transfers between devices, from_everyone(): lax.all_to_all(jnp.broadcast_to(x[None], (count, *x.shape)), axis, 0, 0,...  69.6 us
    all_to_all x6, blocking collectives, from_everyone(): lax.all_to_all(jnp.broadcast_to(x[None], (count, *x.shape)), axis, 0, 0,...  65.7 us
    all_to_all x6, blocking collectives, summed_on_arrival(): lax.all_to_all(pieces, axis, split_axis=0, concat_axis=0, tiled=True)  49.5 us
    all_to_all x11, starting transfers between devices, from_everyone(): lax.all_to_all(jnp.broadcast_to(x[None], (count, *x.shape)), axis, 0, 0,...  40.1 us
    all_to_all x2, starting transfers between devices, sum_in_two_steps(): lax.all_to_all(nearer, far, split_axis=0, concat_axis=0, tiled=True)  30 us
    dot_general x3, matrix products, right_product(): lax.dot_general(left, right, (((1,), (1,)), ((), ())), precision=lax.Prec...  23.1 us
    unnamed x39, local copies, waits for them, and re-layouts  17.6 us
  transfers between devices with their start and end apart: 15, of which 14 were waited for; matrix products, arithmetic and copies ran while one was open for 6% of the time, Pallas kernels for 0%

commit v1 on v0

v1 whole, which is shorter than its diff:
```python
import jax
import jax.numpy as jnp
from jax import lax
from jax.experimental import pallas as pl
from jax.experimental.pallas import tpu as pltpu
from jax.sharding import Mesh
from jax.sharding import PartitionSpec as P

PROW = ("prow_0", "prow_1")
PCOL = ("pcol_0", "pcol_1")
EVERY = ("prow_0", "prow_1", "pcol_0", "pcol_1")
ROWS = 8
COLS = 16
HIGH = lax.Precision.HIGH


def product(left, right, left_dim, right_dim):
    return lax.dot_general(
        left,
        right,
        (((left_dim,), (right_dim,)), ((), ())),
        precision=HIGH,
        preferred_element_type=jnp.float32,
    )


def exchange(pieces, axes):
    return lax.all_to_all(pieces, axes, 0, 0, tiled=True)


def to_everyone(x, axes, count):
    return exchange(jnp.broadcast_to(x[None], (count, *x.shape)), axes)


def place(row, col):
    return row * COLS + col


def send(x, pairs):
    return lax.ppermute(x, EVERY, pairs)


def split_bf16(x):
    high = x.astype(jnp.bfloat16)
    low = (x - high.astype(jnp.float32)).astype(jnp.bfloat16)
    return high, low


def three_pass(left, right):
    dims = (((1,), (1,)), ((), ()))
    left_high, left_low = split_bf16(left)
    right_high, right_low = split_bf16(right)

    def one(a, b):
        return lax.dot_general(a, b, dims, preferred_element_type=jnp.float32)

    return one(left_high, right_high) + (one(left_high, right_low) + one(left_low, right_high))


def finish_kernel(tiles_ref, near_ref, row_ref, pieces_ref, rhs_ref, force_ref, solution_ref, residual_ref):
    row = row_ref[0]
    for group in range(8):
        for half in range(2):
            solution_ref[pl.ds(group * 8, 8), pl.ds(half * 512, 512)] = pieces_ref[row * COLS + group * 2 + half]
    for t in range(2):
        own = tiles_ref[t]
        total = rhs_ref[own // 8, :, pl.ds(pl.multiple_of((own % 8) * 128, 128), 128)]
        for n in range(8):
            tile = near_ref[t, n]
            block = tile // 8
            half = (tile % 8) // 4
            offset = pl.multiple_of((tile % 4) * 128, 128)
            near = jnp.concatenate(
                [pieces_ref[block * COLS + group * 2 + half, :, pl.ds(offset, 128)] for group in range(8)], axis=0
            )
            total = total - three_pass(near, force_ref[t, n])
        residual_ref[t] = total


def finish(tile_list, neighbor_list, row, pieces, rhs, force):
    vmem = pl.BlockSpec(memory_space=pltpu.VMEM)
    smem = pl.BlockSpec(memory_space=pltpu.SMEM)
    return pl.pallas_call(
        finish_kernel,
        out_shape=(
            jax.ShapeDtypeStruct((64, 1024), jnp.float32),
            jax.ShapeDtypeStruct((2, 64, 128), jnp.float32),
        ),
        in_specs=[smem, smem, smem, vmem, vmem, vmem],
        out_specs=(vmem, vmem),
        compiler_params=pltpu.CompilerParams(vmem_limit_bytes=32 * 1024 * 1024),
    )(tile_list, neighbor_list, row, pieces, rhs, force)


def per_device(
    window_rhs,
    past_solution,
    past_panel,
    window_panel,
    diag_inverse,
    tile_list,
    neighbor_list,
    force_constants,
):
    row = lax.axis_index(PROW)
    col = lax.axis_index(PCOL)
    block = window_panel[0, :, 0, :]
    inverse = diag_inverse[0]
    full_rhs = to_everyone(window_rhs, PROW, ROWS)

    past = product(past_solution, past_panel, 1, 1)
    past_rows = exchange(past.reshape(COLS, 4, 1024), PCOL).sum(axis=0)
    rhs_rows = lax.dynamic_slice_in_dim(window_rhs, col * 4, 4, 0)
    start_rows = product(rhs_rows - past_rows, inverse, 1, 1)
    start = to_everyone(start_rows, PCOL, COLS).reshape(64, 1024)

    weight = product(block, inverse, 0, 1)

    carried = start
    arrived = send(start, [(place(0, k - 1), place(k, 0)) for k in range(1, ROWS)])
    current = lax.cond(
        (col == 0) & (row > 0),
        lambda: carried - product(arrived, weight, 1, 0),
        lambda: carried,
    )
    for step in range(1, ROWS - 1):
        source = place(step, step - 1)
        parts = [send(current, [(source, place(k, step))]) for k in range(step + 1, ROWS)]
        partial = send(current, [(place(k, step - 1), place(k, step)) for k in range(step + 1, ROWS)])

        def fire(parts=parts, partial=partial):
            known = parts[0]
            for other in parts[1:]:
                known = known + other
            return partial - product(known, weight, 1, 0)

        current = lax.cond((col == step) & (row > step), fire, lambda current=current: current)

    pieces = current.reshape(8, 8, 2, 512).transpose(0, 2, 1, 3).reshape(COLS, 8, 512)
    spread = exchange(pieces, PCOL)
    own_piece = lax.dynamic_index_in_dim(spread, jnp.maximum(row - 1, 0), 0, keepdims=False)
    everything = to_everyone(own_piece, EVERY, ROWS * COLS)
    solution, residual = finish(
        tile_list[0], neighbor_list[0], row.reshape(1), everything, full_rhs, force_constants[0]
    )
    return (solution, residual[None])


def solution(mesh):
    torus = Mesh(mesh.devices.reshape(4, 2, 4, 4), EVERY)
    placed = (
        P(None, PROW),
        P(None, PCOL),
        P(PROW, PCOL),
        P(PROW, None, PCOL, None),
        P(PROW, None, None),
        P(EVERY, None),
        P(EVERY, None, None),
        P(EVERY, None, None, None, None),
    )
    return jax.shard_map(
        per_device,
        mesh=torus,
        in_specs=placed,
        out_specs=(P(None, PROW), P(EVERY, None, None, None)),
        check_vma=False,
    )
```

time: 509 us -> 241 us (0.47); the launches traced: 500 us -> 240 us
  blocking collectives: 236 us -> 54.2 us
  local copies, waits for them, and re-layouts: 63.6 us -> 3.81 us
  waiting for transfers between devices: 92 us -> 43.3 us
  starting transfers between devices: 77.6 us -> 103 us
  matrix products: 25 us -> 32.5 us
    all_to_all x18 -> x3, blocking collectives: 236 us -> 54.2 us  [exchange(): return lax.all_to_all(pieces, axes, 0, 0, tiled=True)]
    all_to_all x15 -> x2, waiting for transfers between devices: 92 us -> 33.9 us  [exchange(): return lax.all_to_all(pieces, axes, 0, 0, tiled=True)]
    ppermute x0 -> x28, starting transfers between devices: none -> 25.5 us  [send(): return lax.ppermute(x, EVERY, pairs)]
    unnamed x39 -> x10, local copies, waits for them, and re-layouts: 17.6 us -> 1.05 us
    another operation x18 -> x0, local copies, waits for them, and re-layouts: 13.2 us -> none  [the longest x2 6.95 us: per_device(): rhs_tiles = full_rhs.reshape(rhs_count, -1, tile_width)]
    transpose x17 -> x0, local copies, waits for them, and re-layouts: 11.2 us -> none  [the longest x8 4.96 us: cut_along(): return jnp.moveaxis(pieces, dim, 0)]
    ppermute x0 -> x28, waiting for transfers between devices: none -> 9.4 us  [send(): return lax.ppermute(x, EVERY, pairs)]
    broadcast_in_dim x24 -> x4, local copies, waits for them, and re-layouts: 10.8 us -> 1.9 us  [to_everyone(): return exchange(jnp.broadcast_to(x[None], (count, *x.shape)), axes)]
  transfers between devices with their start and end apart: 15 -> 30, of which waited for: 14 -> 6; matrix products, arithmetic and copies ran while one was open for 6% -> 7% of each run, Pallas kernels for 0% -> 0%
where the time goes in v1:
time: 241 us; the launch traced here: 240 us
  starting transfers between devices  103 us (43%)
  blocking collectives  54.2 us (22%)
  waiting for transfers between devices  43.3 us (18%)
  matrix products  32.5 us (13%)
  local copies, waits for them, and re-layouts  3.81 us (2%)
    all_to_all x2, starting transfers between devices, exchange(): return lax.all_to_all(pieces, axes, 0, 0, tiled=True)  77.4 us
    all_to_all x3, blocking collectives, exchange(): return lax.all_to_all(pieces, axes, 0, 0, tiled=True)  54.2 us
    all_to_all x2, waiting for transfers between devices, exchange(): return lax.all_to_all(pieces, axes, 0, 0, tiled=True)  33.9 us
    dot_general x4, matrix products, product(): lax.dot_general(left, right, (((left_dim,), (right_dim,)), ((), ())), pre...  32.5 us
    ppermute x28, starting transfers between devices, send(): return lax.ppermute(x, EVERY, pairs)  25.5 us
    ppermute x28, waiting for transfers between devices, send(): return lax.ppermute(x, EVERY, pairs)  9.4 us
  transfers between devices with their start and end apart: 30, of which 6 were waited for; matrix products, arithmetic and copies ran while one was open for 7% of the time, Pallas kernels for 0%

profile of v1, /device:TPU:1, one launch (start us, length us, event | category | flops | bytes accessed | tf_op | source)
XLA Modules:
  0.0 240.3 jit_solution(8941300578402477600)
XLA Ops:
  0.6 0.0 copy-start
  0.7 1.0 copy-done
  1.7 7.3 %fusion.24 = f32[64,1024]{1,0:T(8,128)S(1)} fusion(f32[64,2048]{1,0:T(8,128)S(1)} %copy-done, f32[1024,2048]{1,0:T(8,128)} %param.24), kind=kOutput, calls=%fused_computation.32 | convolution fusion | flops 805306368 | bytes 9175040 | tf_op jit(solution)/shard_map/dot_general | solution.py:18
  9.0 0.8 reshape.25
  9.8 7.6 %all-to-all-start = ((f32[16,4,1024]{2,1,0:T(4,128)}), f32[16,4,1024]{2,1,0:T(4,128)S(1)}, u32[]{:S(2)}, u32[]{:S(2)}) async-start(f32[16,4,1024]{2,1,0:T(4,128)} %reshape.25), calls=%async_computation | async-start | bytes 524288 | tf_op jit(solution)/shard_map/all_to_all | solution.py:28
  17.4 7.5 %all-to-all-done = f32[16,4,1024]{2,1,0:T(4,128)S(1)} async-done(((f32[16,4,1024]{2,1,0:T(4,128)}), f32[16,4,1024]{2,1,0:T(4,128)S(1)}, u32[]{:S(2)}, u32[]{:S(2)}) %all-to-all-start) | async-done | bytes 262176 | tf_op jit(solution)/shard_map/all_to_all | solution.py:28
  24.9 0.1 reduce_sum.9
  25.0 3.9 %fusion.19 = f32[4,1024]{1,0:T(4,128)S(1)} fusion(f32[1,1024,1024]{2,1,0:T(8,128)} %param.26, f32[4,1024]{1,0:T(4,128)S(1)} %reduce_sum.9, f32[64,1024]{1,0:T(8,128)S(1)} %copy-done.4, s32[]{:T(128)S(6)} %select_n.5), kind=kOutput, calls=%fused_computation.26 | convolution fusion | flops 25169920 | bytes 4243460 | tf_op jit(solution)/shard_map/dot_general | solution.py:18
  28.9 0.1 broadcast_in_dim.10
  29.0 10.5 %all_to_all.25 = f32[16,4,1024]{2,1,0:T(4,128)S(1)} all-to-all(f32[16,4,1024]{2,1,0:T(4,128)S(1)} %broadcast_in_dim.10), channel_id=1, replica_groups=mesh['prow_0'=4,'prow_1'=2,'pcol_0'=4,'pcol_1'=4] {'pcol_0','pcol_1'}, dimensions={0} | all-to-all | bytes 524288 | tf_op jit(solution)/shard_map/all_to_all | solution.py:28
  39.4 0.1 reshape.26
  39.5 1.5 collective-permute-start
  41.0 17.7 %fusion.15 = f32[1024,1024]{1,0:T(8,128)} fusion(f32[1,1024,1,1024]{3,2,1,0:T(1,128)} %param.25, f32[1,1024,1024]{2,1,0:T(8,128)} %param.26), kind=kOutput, calls=%fused_computation.22 | convolution fusion | flops 6442450944 | bytes 12582912 | tf_op jit(solution)/shard_map/dot_general | solution.py:18
  58.6 0.0 collective-permute-done
  58.6 3.6 %conditional.7 = (f32[64,1024]{1,0:T(8,128)S(1)}) conditional(s32[]{:T(128)} %convert_element_type.27, f32[64,1024]{1,0:T(8,128)S(1)} %reshape.26, (f32[64,1024]{1,0:T(8,128)S(1)}, f32[1024,1024]{1,0:T(8,128)}, f32[64,1024]{1,0:T(8,128)S(1)}) %tuple.50), branch_computations={%region_1.0_spmd, %region_2.0_spmd} | conditional | flops 402718720 | bytes 4980744 | solution.py:121
  58.6 3.6 %convolution_subtract_fusion = f32[64,1024]{1,0:T(8,128)S(1)} fusion(f32[64,1024]{1,0:T(8,128)S(1)} %get-tuple-element.100, f32[64,1024]{1,0:T(8,128)S(1)} %get-tuple-element.101, f32[1024,1024]{1,0:T(8,128)} %get-tuple-element.102), kind=kOutput, calls=%fused_computation | convolution fusion | flops 402718720 | bytes 4980736 | tf_op jit(solution)/shard_map/cond/branch_1_fun/dot_general | solution.py:18
  62.3 2.4 %collective-permute-start.1 = (f32[64,1024]{1,0:T(8,128)S(1)}, f32[64,1024]{1,0:T(8,128)S(1)}, u32[]{:S(2)}, u32[]{:S(2)}) collective-permute-start(f32[64,1024]{1,0:T(8,128)S(1)} %get-tuple-element.142), channel_id=1, source_target_pairs={{16,33}} | collective-permute-start | bytes 786440 | tf_op jit(solution)/shard_map/ppermute | solution.py:40
  64.7 1.3 collective-permute-start.2
  66.0 2.0 collective-permute-start.3
  68.0 1.3 collective-permute-start.4
  69.4 1.3 collective-permute-start.5
  70.7 0.0 collective-permute-done.1
  70.7 1.3 collective-permute-start.6
  72.0 0.7 collective-permute-start.7
  72.7 0.9 collective-permute-done.3
  73.6 2.8 %collective-permute-done.4 = f32[64,1024]{1,0:T(8,128)S(1)} collective-permute-done((f32[64,1024]{1,0:T(8,128)S(1)}, f32[64,1024]{1,0:T(8,128)S(1)}, u32[]{:S(2)}, u32[]{:S(2)}) %collective-permute-start.4) | collective-permute-done | bytes 262176 | tf_op jit(solution)/shard_map/ppermute | solution.py:40
  76.4 2.8 %collective-permute-done.5 = f32[64,1024]{1,0:T(8,128)S(1)} collective-permute-done((f32[64,1024]{1,0:T(8,128)S(1)}, f32[64,1024]{1,0:T(8,128)S(1)}, u32[]{:S(2)}, u32[]{:S(2)}) %collective-permute-start.5) | collective-permute-done | bytes 262176 | tf_op jit(solution)/shard_map/ppermute | solution.py:40
  79.2 2.8 %collective-permute-done.6 = f32[64,1024]{1,0:T(8,128)S(1)} collective-permute-done((f32[64,1024]{1,0:T(8,128)S(1)}, f32[64,1024]{1,0:T(8,128)S(1)}, u32[]{:S(2)}, u32[]{:S(2)}) %collective-permute-start.6) | collective-permute-done | bytes 262176 | tf_op jit(solution)/shard_map/ppermute | solution.py:40
  82.0 0.7 collective-permute-start.10
  82.7 0.7 collective-permute-start.11
  83.4 0.7 collective-permute-start.12
  84.1 0.7 collective-permute-start.13
  84.8 0.7 collective-permute-start.8
  85.5 0.7 collective-permute-start.9
  86.2 0.0 collective-permute-done.11
  86.2 0.0 collective-permute-done.8
  86.2 0.7 collective-permute-start.14
  86.9 0.7 collective-permute-start.15
  87.6 0.7 collective-permute-start.16
  88.3 0.9 collective-permute-start.17
  89.2 0.7 collective-permute-start.18
  89.9 0.0 collective-permute-done.15
  89.9 0.0 collective-permute-done.16
  89.9 0.0 collective-permute-done.18
  90.0 0.7 collective-permute-start.19
  90.6 0.7 collective-permute-start.20
  91.3 0.7 collective-permute-start.21
  92.0 0.7 collective-permute-start.22
  92.7 0.0 collective-permute-done.20
  92.7 0.0 collective-permute-done.21
  92.8 0.7 collective-permute-start.23
  93.5 0.7 collective-permute-start.24
  94.1 0.7 collective-permute-start.25
  94.8 0.0 collective-permute-done.23
  94.9 0.7 collective-permute-start.26
  95.6 0.7 collective-permute-start.27
  96.3 0.0 collective-permute-done.26
  96.3 10.1 %all_to_all.26 = f32[16,8,512]{2,1,0:T(8,128)S(1)} all-to-all(f32[16,8,512]{2,1,0:T(8,128)S(1)} %bitcast.34), channel_id=1, replica_groups=mesh['prow_0'=4,'prow_1'=2,'pcol_0'=4,'pcol_1'=4] {'pcol_0','pcol_1'}, dimensions={0} | all-to-all | bytes 524288 | tf_op jit(solution)/shard_map/all_to_all | solution.py:28
  106.4 1.6 broadcast_in_dim.26
  108.0 69.8 %all-to-all-start.4 = ((f32[8,64,1024]{2,1,0:T(8,128)}), f32[8,64,1024]{2,1,0:T(8,128)S(1)}, u32[]{:S(2)}, u32[]{:S(2)}) async-start(f32[8,64,1024]{2,1,0:T(8,128)} %broadcast_in_dim.26), calls=%async_computation.4 | async-start | bytes 4194304 | tf_op jit(solution)/shard_map/all_to_all | solution.py:28
  177.8 26.3 %all-to-all-done.4.rhs_ref = f32[8,64,1024]{2,1,0:T(8,128)S(1)} async-done(((f32[8,64,1024]{2,1,0:T(8,128)}), f32[8,64,1024]{2,1,0:T(8,128)S(1)}, u32[]{:S(2)}, u32[]{:S(2)}) %all-to-all-start.4) | async-done | bytes 2097184 | tf_op jit(solution)/shard_map/all_to_all | solution.py:28
  204.1 0.2 broadcast_in_dim.12
  204.4 33.6 %all_to_all.27.pieces_ref = f32[128,8,512]{2,1,0:T(8,128)S(1)} all-to-all(f32[128,8,512]{2,1,0:T(8,128)S(1)} %broadcast_in_dim.12), channel_id=1, replica_groups=mesh['prow_0'=4,'prow_1'=2,'pcol_0'=4,'pcol_1'=4] {'prow_0','prow_1','pc..., dimensions={0} | all-to-all | bytes 4194304 | tf_op jit(solution)/shard_map/all_to_all | solution.py:28
  238.1 2.3 shard_map.95
  (28 shorter events, 0.1 us)
Async XLA Ops:
  0.6 1.0 copy-start
  0.6 24.3 %copy-start.4 = (f32[64,1024]{1,0:T(8,128)S(1)}, f32[64,1024]{1,0:T(8,128)}, u32[]{:S(2)}) copy-start(f32[64,1024]{1,0:T(8,128)} %param.22) | copy-start | bytes 786436
  9.8 15.1 %all-to-all-start = ((f32[16,4,1024]{2,1,0:T(4,128)}), f32[16,4,1024]{2,1,0:T(4,128)S(1)}, u32[]{:S(2)}, u32[]{:S(2)}) async-start(f32[16,4,1024]{2,1,0:T(4,128)} %reshape.25), calls=%async_computation | async-start | bytes 524288 | tf_op jit(solution)/shard_map/all_to_all | solution.py:28
  39.5 19.1 %collective-permute-start = (f32[64,1024]{1,0:T(8,128)S(1)}, f32[64,1024]{1,0:T(8,128)S(1)}, u32[]{:S(2)}, u32[]{:S(2)}) collective-permute-start(f32[64,1024]{1,0:T(8,128)S(1)} %reshape.26), channel_id=1, source_target_pairs={{0,16},{1,32},{2,48},{3,64},{4,80},{5,96},{6,112}} | collective-permute-start | bytes 786440 | tf_op jit(solution)/shard_map/ppermute | solution.py:40
  62.3 8.4 %collective-permute-start.1 = (f32[64,1024]{1,0:T(8,128)S(1)}, f32[64,1024]{1,0:T(8,128)S(1)}, u32[]{:S(2)}, u32[]{:S(2)}) collective-permute-start(f32[64,1024]{1,0:T(8,128)S(1)} %get-tuple-element.142), channel_id=1, source_target_pairs={{16,33}} | collective-permute-start | bytes 786440 | tf_op jit(solution)/shard_map/ppermute | solution.py:40
  64.7 7.3 %collective-permute-start.2 = (f32[64,1024]{1,0:T(8,128)S(1)}, f32[64,1024]{1,0:T(8,128)S(1)}, u32[]{:S(2)}, u32[]{:S(2)}) collective-permute-start(f32[64,1024]{1,0:T(8,128)S(1)} %get-tuple-element.142), channel_id=1, source_target_pairs={{16,49}} | collective-permute-start | bytes 786440 | tf_op jit(solution)/shard_map/ppermute | solution.py:40
  66.0 7.6 %collective-permute-start.3 = (f32[64,1024]{1,0:T(8,128)S(1)}, f32[64,1024]{1,0:T(8,128)S(1)}, u32[]{:S(2)}, u32[]{:S(2)}) collective-permute-start(f32[64,1024]{1,0:T(8,128)S(1)} %get-tuple-element.142), channel_id=1, source_target_pairs={{16,65}} | collective-permute-start | bytes 786440 | tf_op jit(solution)/shard_map/ppermute | solution.py:40
  68.0 8.4 %collective-permute-start.4 = (f32[64,1024]{1,0:T(8,128)S(1)}, f32[64,1024]{1,0:T(8,128)S(1)}, u32[]{:S(2)}, u32[]{:S(2)}) collective-permute-start(f32[64,1024]{1,0:T(8,128)S(1)} %get-tuple-element.142), channel_id=1, source_target_pairs={{16,81}} | collective-permute-start | bytes 786440 | tf_op jit(solution)/shard_map/ppermute | solution.py:40
  69.4 9.9 %collective-permute-start.5 = (f32[64,1024]{1,0:T(8,128)S(1)}, f32[64,1024]{1,0:T(8,128)S(1)}, u32[]{:S(2)}, u32[]{:S(2)}) collective-permute-start(f32[64,1024]{1,0:T(8,128)S(1)} %get-tuple-element.142), channel_id=1, source_target_pairs={{16,97}} | collective-permute-start | bytes 786440 | tf_op jit(solution)/shard_map/ppermute | solution.py:40
  70.7 11.4 %collective-permute-start.6 = (f32[64,1024]{1,0:T(8,128)S(1)}, f32[64,1024]{1,0:T(8,128)S(1)}, u32[]{:S(2)}, u32[]{:S(2)}) collective-permute-start(f32[64,1024]{1,0:T(8,128)S(1)} %get-tuple-element.142), channel_id=1, source_target_pairs={{16,113}} | collective-permute-start | bytes 786440 | tf_op jit(solution)/shard_map/ppermute | solution.py:40
  72.0 10.0 %collective-permute-start.7 = (f32[64,1024]{1,0:T(8,128)S(1)}, f32[64,1024]{1,0:T(8,128)S(1)}, u32[]{:S(2)}, u32[]{:S(2)}) collective-permute-start(f32[64,1024]{1,0:T(8,128)S(1)} %get-tuple-element.142), channel_id=1, source_target_pairs={{32,33},{48,49},{64,65},{80,81},{96,97},{112,113}} | collective-permute-start | bytes 786440 | tf_op jit(solution)/shard_map/ppermute | solution.py:40
  82.0 3.4 %collective-permute-start.10 = (f32[64,1024]{1,0:T(8,128)S(1)}, f32[64,1024]{1,0:T(8,128)S(1)}, u32[]{:S(2)}, u32[]{:S(2)}) collective-permute-start(f32[64,1024]{1,0:T(8,128)S(1)} %get-tuple-element.143), channel_id=1, source_target_pairs={{33,82}} | collective-permute-start | bytes 786440 | tf_op jit(solution)/shard_map/ppermute | solution.py:40
  82.7 3.5 %collective-permute-start.11 = (f32[64,1024]{1,0:T(8,128)S(1)}, f32[64,1024]{1,0:T(8,128)S(1)}, u32[]{:S(2)}, u32[]{:S(2)}) collective-permute-start(f32[64,1024]{1,0:T(8,128)S(1)} %get-tuple-element.143), channel_id=1, source_target_pairs={{33,98}} | collective-permute-start | bytes 786440 | tf_op jit(solution)/shard_map/ppermute | solution.py:40
  83.4 2.8 %collective-permute-start.12 = (f32[64,1024]{1,0:T(8,128)S(1)}, f32[64,1024]{1,0:T(8,128)S(1)}, u32[]{:S(2)}, u32[]{:S(2)}) collective-permute-start(f32[64,1024]{1,0:T(8,128)S(1)} %get-tuple-element.143), channel_id=1, source_target_pairs={{33,114}} | collective-permute-start | bytes 786440 | tf_op jit(solution)/shard_map/ppermute | solution.py:40
  84.1 2.1 collective-permute-start.13
  84.8 1.4 collective-permute-start.8
  85.5 0.7 collective-permute-start.9
  86.2 3.7 %collective-permute-start.14 = (f32[64,1024]{1,0:T(8,128)S(1)}, f32[64,1024]{1,0:T(8,128)S(1)}, u32[]{:S(2)}, u32[]{:S(2)}) collective-permute-start(f32[64,1024]{1,0:T(8,128)S(1)} %get-tuple-element.144), channel_id=1, source_target_pairs={{50,67}} | collective-permute-start | bytes 786440 | tf_op jit(solution)/shard_map/ppermute | solution.py:40
  86.9 3.0 %collective-permute-start.15 = (f32[64,1024]{1,0:T(8,128)S(1)}, f32[64,1024]{1,0:T(8,128)S(1)}, u32[]{:S(2)}, u32[]{:S(2)}) collective-permute-start(f32[64,1024]{1,0:T(8,128)S(1)} %get-tuple-element.144), channel_id=1, source_target_pairs={{50,83}} | collective-permute-start | bytes 786440 | tf_op jit(solution)/shard_map/ppermute | solution.py:40
  87.6 2.3 collective-permute-start.16
  88.3 1.6 collective-permute-start.17
  89.2 0.7 collective-permute-start.18
  90.0 2.8 %collective-permute-start.19 = (f32[64,1024]{1,0:T(8,128)S(1)}, f32[64,1024]{1,0:T(8,128)S(1)}, u32[]{:S(2)}, u32[]{:S(2)}) collective-permute-start(f32[64,1024]{1,0:T(8,128)S(1)} %get-tuple-element.145), channel_id=1, source_target_pairs={{67,84}} | collective-permute-start | bytes 786440 | tf_op jit(solution)/shard_map/ppermute | solution.py:40
  90.6 2.1 collective-permute-start.20
  91.3 1.4 collective-permute-start.21
  92.0 0.7 collective-permute-start.22
  92.8 2.1 collective-permute-start.23
  93.5 1.4 collective-permute-start.24
  94.1 0.7 collective-permute-start.25
  94.9 1.4 collective-permute-start.26
  95.6 0.7 collective-permute-start.27
  108.0 96.1 %all-to-all-start.4 = ((f32[8,64,1024]{2,1,0:T(8,128)}), f32[8,64,1024]{2,1,0:T(8,128)S(1)}, u32[]{:S(2)}, u32[]{:S(2)}) async-start(f32[8,64,1024]{2,1,0:T(8,128)} %broadcast_in_dim.26), calls=%async_computation.4 | async-start | bytes 4194304 | tf_op jit(solution)/shard_map/all_to_all | solution.py:28
  177.8 60.2 %copy-start.2 = (s32[1,2,8]{2,1,0:T(2,128)S(1)}, s32[1,2,8]{2,1,0:T(2,128)}, u32[]{:S(2)}) copy-start(s32[1,2,8]{2,1,0:T(2,128)} %param.28) | copy-start | bytes 196
  177.8 60.2 %copy-start.3 = (s32[1,2]{1,0:T(1,128)S(1)}, s32[1,2]{1,0:T(1,128)}, u32[]{:S(2)}) copy-start(s32[1,2]{1,0:T(1,128)} %param.27) | copy-start | bytes 28
  204.1 33.9 %copy-start.1 = (f32[1,2,8,128,128]{4,3,2,1,0:T(8,128)S(1)}, f32[1,2,8,128,128]{4,3,2,1,0:T(8,128)}, u32[]{:S(2)}) copy-start(f32[1,2,8,128,128]{4,3,2,1,0:T(8,128)} %param.29) | copy-start | bytes 3145732

commit v2 on v1

--- a/solution.py
+++ b/solution.py
@@ -46,25 +46,116 @@
     return high, low
 
 
-def three_pass(left, right):
+def three_pass(left, right_high, right_low):
     dims = (((1,), (1,)), ((), ()))
     left_high, left_low = split_bf16(left)
-    right_high, right_low = split_bf16(right)
+    rows = left.shape[0]
+    both = lax.dot_general(
+        jnp.concatenate([left_high, left_low], axis=0), right_high, dims, preferred_element_type=jnp.float32
+    )
+    return (both[:rows] + both[rows:]) + lax.dot_general(
+        left_high, right_low, dims, preferred_element_type=jnp.float32
+    )
+
+
+VMEM = pl.BlockSpec(memory_space=pltpu.VMEM)
+SMEM = pl.BlockSpec(memory_space=pltpu.SMEM)
+
+
+def room(mib):
+    return pltpu.CompilerParams(vmem_limit_bytes=mib * 1024 * 1024)
+
+
+def form_kernel(inverse_ref, block_ref, inverse_high_ref, inverse_low_ref, high_ref, low_ref):
+    @pl.when(pl.program_id(0) == 0)
+    def _():
+        inverse_high_ref[...], inverse_low_ref[...] = split_bf16(inverse_ref[...])
+
+    count = block_ref.shape[0] // inverse_ref.shape[0]
+    first = pl.program_id(0) * 2
+    strips = [block_ref[pl.ds(first + i, inverse_ref.shape[0], stride=count), :] for i in range(2)]
+    block_high, block_low = split_bf16(jnp.concatenate(strips, axis=1))
 
     def one(a, b):
-        return lax.dot_general(a, b, dims, preferred_element_type=jnp.float32)
-
-    return one(left_high, right_high) + (one(left_high, right_low) + one(left_low, right_high))
-
-
-def finish_kernel(tiles_ref, near_ref, row_ref, pieces_ref, rhs_ref, force_ref, solution_ref, residual_ref):
+        return jnp.dot(a, b, preferred_element_type=jnp.float32)
+
+    total = one(inverse_high_ref[...], block_high)
+    total = total + one(inverse_high_ref[...], block_low)
+    total = total + one(inverse_low_ref[...], block_high)
+    high_ref[...], low_ref[...] = split_bf16(total)
+
+
+def form(inverse, block):
+    order = inverse.shape[0]
+    width = 256
+    half = jax.ShapeDtypeStruct((order, order), jnp.bfloat16)
+    whole = pl.BlockSpec((order, order), lambda i: (0, 0))
+    strip = pl.BlockSpec((order, width), lambda i: (0, i))
+    return pl.pallas_call(
+        form_kernel,
+        grid=(order // width,),
+        in_specs=[whole, pl.BlockSpec(block.shape, lambda i: (0, 0))],
+        out_specs=(whole, whole, strip, strip),
+        out_shape=(half, half, half, half),
+        compiler_params=room(24),
+    )(inverse, block)
+
+
+def start_kernel(rhs_ref, past_ref, high_ref, low_ref, out_ref):
+    diff = rhs_ref[...] - past_ref[...]
+    out_ref[...] = three_pass(diff, high_ref[...], low_ref[...])
+
+
+def start_product(rhs, past, high, low):
+    return pl.pallas_call(
+        start_kernel,
+        in_specs=[VMEM] * 4,
+        out_specs=VMEM,
+        out_shape=jax.ShapeDtypeStruct(rhs.shape, jnp.float32),
+        compiler_params=room(4),
+    )(rhs, past, high, low)
+
+
+def fire(bases, knowns, high, low):
+    count = len(bases)
+
+    def kernel(*refs):
+        total = refs[0][...]
+        for ref in refs[1:count]:
+            total = total + ref[...]
+        known = refs[count][...]
+        for ref in refs[count + 1 : -3]:
+            known = known + ref[...]
+        refs[-1][...] = total - three_pass(known, refs[-3][...], refs[-2][...])
+
+    return pl.pallas_call(
+        kernel,
+        in_specs=[VMEM] * (count + len(knowns) + 2),
+        out_specs=VMEM,
+        out_shape=jax.ShapeDtypeStruct(knowns[0].shape, jnp.float32),
+        compiler_params=room(8),
+    )(*bases, *knowns, high, low)
+
+
+def finish_kernel(tiles_ref, near_ref, row_ref, pieces_ref, *refs):
+    rhs_refs, (force_ref, solution_ref, residual_ref) = refs[:-3], refs[-3:]
     row = row_ref[0]
     for group in range(8):
         for half in range(2):
             solution_ref[pl.ds(group * 8, 8), pl.ds(half * 512, 512)] = pieces_ref[row * COLS + group * 2 + half]
     for t in range(2):
         own = tiles_ref[t]
-        total = rhs_ref[own // 8, :, pl.ds(pl.multiple_of((own % 8) * 128, 128), 128)]
+        own_row = own // 8
+        behind = (row // 2 - own_row // 2 + 4) % 4
+        core = (row + own_row) % 2
+        for distance in range(4):
+
+            @pl.when(behind == distance)
+            def _():
+                offset = pl.multiple_of((own % 8) * 128, 128)
+                residual_ref[t] = rhs_refs[distance][core, :, pl.ds(offset, 128)]
+
+        total = residual_ref[t]
         for n in range(8):
             tile = near_ref[t, n]
             block = tile // 8
@@ -73,23 +164,21 @@
             near = jnp.concatenate(
                 [pieces_ref[block * COLS + group * 2 + half, :, pl.ds(offset, 128)] for group in range(8)], axis=0
             )
-            total = total - three_pass(near, force_ref[t, n])
+            total = total - three_pass(near, *split_bf16(force_ref[t, n]))
         residual_ref[t] = total
 
 
 def finish(tile_list, neighbor_list, row, pieces, rhs, force):
-    vmem = pl.BlockSpec(memory_space=pltpu.VMEM)
-    smem = pl.BlockSpec(memory_space=pltpu.SMEM)
     return pl.pallas_call(
         finish_kernel,
         out_shape=(
             jax.ShapeDtypeStruct((64, 1024), jnp.float32),
             jax.ShapeDtypeStruct((2, 64, 128), jnp.float32),
         ),
-        in_specs=[smem, smem, smem, vmem, vmem, vmem],
-        out_specs=(vmem, vmem),
-        compiler_params=pltpu.CompilerParams(vmem_limit_bytes=32 * 1024 * 1024),
-    )(tile_list, neighbor_list, row, pieces, rhs, force)
+        in_specs=[SMEM, SMEM, SMEM] + [VMEM] * (2 + len(rhs)),
+        out_specs=(VMEM, VMEM),
+        compiler_params=room(8),
+    )(tile_list, neighbor_list, row, pieces, *rhs, force)
 
 
 def per_device(
@@ -104,37 +193,42 @@
 ):
     row = lax.axis_index(PROW)
     col = lax.axis_index(PCOL)
-    block = window_panel[0, :, 0, :]
+    block = window_panel.reshape(-1, 128)
     inverse = diag_inverse[0]
-    full_rhs = to_everyone(window_rhs, PROW, ROWS)
+
+    other_rhs = lax.ppermute(window_rhs, "prow_1", [(0, 1), (1, 0)])
+    pair = jnp.stack([window_rhs, other_rhs])
+    full_rhs = [pair] + [lax.ppermute(pair, "prow_0", [(i, (i + d) % 4) for i in range(4)]) for d in (1, 2, 3)]
 
     past = product(past_solution, past_panel, 1, 1)
     past_rows = exchange(past.reshape(COLS, 4, 1024), PCOL).sum(axis=0)
+    inverse_high, inverse_low, high, low = form(inverse, block)
     rhs_rows = lax.dynamic_slice_in_dim(window_rhs, col * 4, 4, 0)
-    start_rows = product(rhs_rows - past_rows, inverse, 1, 1)
+    start_rows = start_product(rhs_rows, past_rows, inverse_high, inverse_low)
     start = to_everyone(start_rows, PCOL, COLS).reshape(64, 1024)
-
-    weight = product(block, inverse, 0, 1)
-
-    carried = start
+    start, *full_rhs = lax.optimization_barrier((start, *full_rhs))
+
+    total = jnp.where(row == col + 1, start, jnp.zeros_like(start))
     arrived = send(start, [(place(0, k - 1), place(k, 0)) for k in range(1, ROWS)])
     current = lax.cond(
         (col == 0) & (row > 0),
-        lambda: carried - product(arrived, weight, 1, 0),
-        lambda: carried,
+        lambda: fire([total], [arrived], high, low),
+        lambda: start,
     )
     for step in range(1, ROWS - 1):
         source = place(step, step - 1)
-        parts = [send(current, [(source, place(k, step))]) for k in range(step + 1, ROWS)]
-        partial = send(current, [(place(k, step - 1), place(k, step)) for k in range(step + 1, ROWS)])
-
-        def fire(parts=parts, partial=partial):
-            known = parts[0]
-            for other in parts[1:]:
-                known = known + other
-            return partial - product(known, weight, 1, 0)
-
-        current = lax.cond((col == step) & (row > step), fire, lambda current=current: current)
+        beside = place(step ^ 1, step - 1)
+        knowns = [send(current, [(source, place(step + 1, step))])]
+        if step + 2 < ROWS:
+            relayed = send(current, [(source, beside)])
+            knowns += [send(relayed, [(beside, place(k, step))]) for k in range(step + 2, ROWS)]
+        extra = send(current, [(place(k, step - 1), place(k, k - 1)) for k in range(step + 1, ROWS)])
+        current = lax.cond(
+            (col == step) & (row > step),
+            lambda: fire([total, extra], knowns, high, low),
+            lambda: current,
+        )
+        total = total + extra
 
     pieces = current.reshape(8, 8, 2, 512).transpose(0, 2, 1, 3).reshape(COLS, 8, 512)
     spread = exchange(pieces, PCOL)

time: 241 us -> 236 us (0.979)
  blocking collectives: 54.2 us -> 124 us
  starting transfers between devices: 103 us -> 58.2 us
  waiting for transfers between devices: 43.3 us -> 15.2 us
  matrix products: 32.5 us -> 7.31 us
  Pallas kernels: 2.27 us -> 17.7 us
  local copies, waits for them, and re-layouts: 3.81 us -> 9.3 us
    all_to_all x3 -> x2, blocking collectives: 54.2 us -> 124 us  [exchange(): return lax.all_to_all(pieces, axes, 0, 0, tiled=True)]
    all_to_all x2, starting transfers between devices: 77.4 us -> 10.4 us  [exchange(): return lax.all_to_all(pieces, axes, 0, 0, tiled=True)]
    all_to_all x2, waiting for transfers between devices: 33.9 us -> 7.5 us  [exchange(): return lax.all_to_all(pieces, axes, 0, 0, tiled=True)]
    dot_general x4 -> x1, matrix products: 32.5 us -> 7.31 us  [product(): lax.dot_general(left, right, (((left_dim,), (right_dim,)), ((), ())), pre...]
    ppermute x0 -> x4, starting transfers between devices: none -> 21.5 us  [the longest x3 20 us: per_device(): lax.ppermute(pair, 'prow_0', [(i, (i + d) % 4) for i in range(4)])]
    pallas_call x0 -> x3, Pallas kernels: none -> 14.8 us  [the longest x1 9.21 us: form(): pl.pallas_call(form_kernel, grid=(order // width,), in_specs=[whole, pl.B...]
    unnamed x10 -> x16, local copies, waits for them, and re-layouts: 1.05 us -> 7.35 us
    ppermute x28 -> x33, waiting for transfers between devices: 9.4 us -> 6.36 us  [send(): return lax.ppermute(x, EVERY, pairs)]
  transfers between devices with their start and end apart: 30 -> 39, of which waited for: 6 -> 4; matrix products, arithmetic and copies ran while one was open for 7% -> 4% of each run, Pallas kernels for 0% -> 4%
where the time goes in v2:
time: 236 us; the launch traced here: 235 us
  blocking collectives  124 us (53%)
  starting transfers between devices  58.2 us (25%)
  Pallas kernels  17.7 us (8%)
  waiting for transfers between devices  15.2 us (6%)
  local copies, waits for them, and re-layouts  9.3 us (4%)
  matrix products  7.31 us (3%)
    all_to_all x2, blocking collectives, exchange(): return lax.all_to_all(pieces, axes, 0, 0, tiled=True)  124 us
    ppermute x33, starting transfers between devices, send(): return lax.ppermute(x, EVERY, pairs)  26.3 us
    ppermute x3, starting transfers between devices, per_device(): lax.ppermute(pair, 'prow_0', [(i, (i + d) % 4) for i in range(4)])  20 us
    all_to_all x2, starting transfers between devices, exchange(): return lax.all_to_all(pieces, axes, 0, 0, tiled=True)  10.4 us
    pallas_call x1, Pallas kernels, form(): pl.pallas_call(form_kernel, grid=(order // width,), in_specs=[whole, pl.B...  9.21 us
    all_to_all x2, waiting for transfers between devices, exchange(): return lax.all_to_all(pieces, axes, 0, 0, tiled=True)  7.5 us
    unnamed x16, local copies, waits for them, and re-layouts  7.35 us
    dot_general x1, matrix products, product(): lax.dot_general(left, right, (((left_dim,), (right_dim,)), ((), ())), pre...  7.31 us
  transfers between devices with their start and end apart: 39, of which 4 were waited for; matrix products, arithmetic and copies ran while one was open for 4% of the time, Pallas kernels for 4%

profile of v2, /device:TPU:1, one launch (start us, length us, event | category | flops | bytes accessed | tf_op | source)
XLA Modules:
  0.0 234.7 jit_solution(2277632760034749509)
XLA Ops:
  0.6 1.5 collective-permute-start
  2.1 1.4 collective-permute-done
  3.5 1.0 pad_maximum_fusion.refs_0_
  4.5 1.8 collective-permute-start.1
  6.3 9.3 %collective-permute-start.2 = (f32[2,64,1024]{2,1,0:T(8,128)S(1)}, f32[2,64,1024]{2,1,0:T(8,128)}, u32[]{:S(2)}, u32[]{:S(2)}) collective-permute-start(f32[2,64,1024]{2,1,0:T(8,128)S(1)} %pad_maximum_fusion.refs_0_), channel_id=1, source_target_pairs={{0,64},{32,96},{64,0},{96,32},{1,65},{33,97},{65,1},{97,33},{2,66}... | collective-permute-start | bytes 1572872 | tf_op jit(solution)/shard_map/ppermute | solution.py:201
  15.6 8.9 %collective-permute-start.3 = (f32[2,64,1024]{2,1,0:T(8,128)S(1)}, f32[2,64,1024]{2,1,0:T(8,128)}, u32[]{:S(2)}, u32[]{:S(2)}) collective-permute-start(f32[2,64,1024]{2,1,0:T(8,128)S(1)} %pad_maximum_fusion.refs_0_), channel_id=1, source_target_pairs={{0,96},{32,0},{64,32},{96,64},{1,97},{33,1},{65,33},{97,65},{2,98}... | collective-permute-start | bytes 1572872 | tf_op jit(solution)/shard_map/ppermute | solution.py:201
  24.5 7.3 %fusion.2 = f32[64,1024]{1,0:T(8,128)S(1)} fusion(f32[64,2048]{1,0:T(8,128)S(1)} %copy-done, f32[1024,2048]{1,0:T(8,128)} %param.24), kind=kOutput, calls=%fused_computation.6 | convolution fusion | flops 805306368 | bytes 9175040 | tf_op jit(solution)/shard_map/dot_general | solution.py:18
  31.8 0.8 reshape.24
  32.6 6.7 %all-to-all-start = ((f32[16,4,1024]{2,1,0:T(4,128)}), f32[16,4,1024]{2,1,0:T(4,128)S(1)}, u32[]{:S(2)}, u32[]{:S(2)}) async-start(f32[16,4,1024]{2,1,0:T(4,128)} %reshape.24), calls=%async_computation | async-start | bytes 524288 | tf_op jit(solution)/shard_map/all_to_all | solution.py:28
  39.3 2.2 copy-done.1
  41.5 2.2 copy-done.2
  43.7 9.2 %shard_map.95 = (bf16[1024,1024]{1,0:T(8,128)(2,1)S(1)}, bf16[1024,1024]{1,0:T(8,128)(2,1)S(1)}, bf16[1024,1024]{1,0:T(8,128)(2,1)}, bf16[1024,1024]{1,0:T(8,128)(2,1)}) custom-call(f32[1024,1024]{1,0:T(8,128)S(1)} %bitcast.18, f32[8192,128]{1,0:T(8,128)S(1)} %bitcast.19), custom_call_target="tpu_custom_call" | custom-call | tf_op jit(solution)/shard_map/pallas_call | solution.py:94
  52.9 1.4 copy-done.3
  54.3 0.8 constant_dynamic-slice_fusion.rhs_ref
  55.1 0.1 reduce_sum.9.past_ref
  55.1 1.6 copy-done.4
  56.7 1.2 shard_map.96
  57.9 0.1 broadcast_in_dim.20
  58.0 14.1 %all_to_all.20 = f32[16,4,1024]{2,1,0:T(4,128)S(1)} all-to-all(f32[16,4,1024]{2,1,0:T(4,128)S(1)} %broadcast_in_dim.20), channel_id=1, replica_groups=mesh['prow_0'=4,'prow_1'=2,'pcol_0'=4,'pcol_1'=4] {'pcol_0','pcol_1'}, dimensions={0} | all-to-all | bytes 524288 | tf_op jit(solution)/shard_map/all_to_all | solution.py:28
  72.1 0.1 reshape.26
  72.2 1.3 collective-permute-start.4
  73.5 3.2 %collective-permute-done.4 = f32[64,1024]{1,0:T(8,128)S(1)} collective-permute-done((f32[64,1024]{1,0:T(8,128)S(1)}, f32[64,1024]{1,0:T(8,128)S(1)}, u32[]{:S(2)}, u32[]{:S(2)}) %collective-permute-start.4) | collective-permute-done | bytes 262176 | tf_op jit(solution)/shard_map/ppermute | solution.py:40
  76.7 4.4 %conditional.7 = (f32[64,1024]{1,0:T(8,128)}) conditional(s32[]{:T(128)} %convert_element_type.27, f32[64,1024]{1,0:T(8,128)S(1)} %reshape.26, (f32[64,1024]{1,0:T(8,128)S(1)}, f32[64,1024]{1,0:T(8,128)S(1)}, bf16[1024,1024]{1,0:T(8,128)(2,1)}, bf16[1024,1024]{1,0:T(8,128)(2,1)}) %tuple.52), branch_computations={%region_1.2_spmd, %region_2.3_spmd} | conditional | bytes 524296 | solution.py:213
  76.7 4.4 %branch_1_fun.7 = f32[64,1024]{1,0:T(8,128)} custom-call(f32[64,1024]{1,0:T(8,128)S(1)} %get-tuple-element.129.refs_0_, f32[64,1024]{1,0:T(8,128)S(1)} %get-tuple-element.130.refs_1_, bf16[1024,1024]{1,0:T(8,128)(2,1)} %get-tuple-element.131.refs_2_, bf16[1024,1024]{1,0:T(8,128)(2,1)} %get-tuple-element.132.refs_3_), custom_call_target="tpu_custom_call" | custom-call | tf_op jit(solution)/shard_map/cond/branch_1_fun/pallas_call | solution.py:131
  81.1 2.0 collective-permute-start.7
  83.1 0.7 collective-permute-start.5
  83.8 1.3 collective-permute-start.6
  85.1 0.7 collective-permute-start.10
  85.8 0.7 collective-permute-start.11
  86.5 0.7 collective-permute-start.12
  87.2 0.7 collective-permute-start.8
  87.9 3.1 %collective-permute-done.6 = f32[64,1024]{1,0:T(8,128)S(1)} collective-permute-done((f32[64,1024]{1,0:T(8,128)}, f32[64,1024]{1,0:T(8,128)S(1)}, u32[]{:S(2)}, u32[]{:S(2)}) %collective-permute-start.6) | collective-permute-done | bytes 262176 | tf_op jit(solution)/shard_map/ppermute | solution.py:40
  90.9 0.7 collective-permute-start.9
  91.7 1.4 collective-permute-start.15
  93.1 0.7 collective-permute-start.13
  93.7 0.7 collective-permute-start.14
  94.4 0.7 collective-permute-start.16
  95.1 0.7 collective-permute-start.17
  95.8 0.7 collective-permute-start.18
  96.5 1.4 collective-permute-start.19
  98.0 0.2 conditional.9
  98.2 0.7 collective-permute-start.22
  98.9 0.7 collective-permute-start.20
  99.6 0.7 collective-permute-start.21
  100.3 0.7 collective-permute-start.23
  101.0 0.7 collective-permute-start.24
  101.6 0.7 collective-permute-start.25
  102.4 0.7 collective-permute-start.28
  103.1 0.7 collective-permute-start.26
  103.8 0.7 collective-permute-start.27
  104.5 0.7 collective-permute-start.29
  105.2 0.7 collective-permute-start.30
  105.9 0.1 fusion
  106.0 0.7 collective-permute-start.33
  106.7 0.7 collective-permute-start.31
  107.3 0.7 collective-permute-start.32
  108.0 0.7 collective-permute-start.34
  108.8 0.7 collective-permute-start.35
  109.5 0.7 collective-permute-start.36
  110.2 3.7 %all-to-all-start.2 = ((f32[16,8,512]{2,1,0:T(8,128)}), f32[16,8,512]{2,1,0:T(8,128)S(1)}, u32[]{:S(2)}, u32[]{:S(2)}) async-start(f32[16,8,512]{2,1,0:T(8,128)} %bitcast.9), calls=%async_computation.2 | async-start | bytes 524288 | tf_op jit(solution)/shard_map/all_to_all | solution.py:28
  113.9 7.5 %all-to-all-done.2 = f32[16,8,512]{2,1,0:T(8,128)S(1)} async-done(((f32[16,8,512]{2,1,0:T(8,128)}), f32[16,8,512]{2,1,0:T(8,128)S(1)}, u32[]{:S(2)}, u32[]{:S(2)}) %all-to-all-start.2) | async-done | bytes 262176 | tf_op jit(solution)/shard_map/all_to_all | solution.py:28
  121.4 0.3 broadcast_in_dim.23
  121.7 110.0 %all_to_all.21.pieces_ref = f32[128,8,512]{2,1,0:T(8,128)S(1)} all-to-all(f32[128,8,512]{2,1,0:T(8,128)S(1)} %broadcast_in_dim.23), channel_id=1, replica_groups=mesh['prow_0'=4,'prow_1'=2,'pcol_0'=4,'pcol_1'=4] {'prow_0','prow_1','pc..., dimensions={0} | all-to-all | bytes 4194304 | tf_op jit(solution)/shard_map/all_to_all | solution.py:28
  231.7 3.0 %shard_map.97 = (f32[64,1024]{1,0:T(8,128)}, f32[2,64,128]{2,1,0:T(8,128)}) custom-call(s32[2]{0:T(128)S(1)} %bitcast.22, s32[2,8]{1,0:T(2,128)S(1)} %bitcast.21, s32[1]{0:T(128)} %bitcast.2.row_ref, f32[128,8,512]{2,1,0:T(8,128)S(1)} %all_to_all.21.pieces_ref, f32[2,64,1024]{2,1,0:T(8,128)S(1)} %pad_maximum_fusion.refs_0_, ...), custom_call_target="tpu_custom_call" | custom-call | tf_op jit(solution)/shard_map/pallas_call | solution.py:172
  (55 shorter events, 0.2 us)
Async XLA Ops:
  0.6 23.9 %copy-start = (f32[64,2048]{1,0:T(8,128)S(1)}, f32[64,2048]{1,0:T(8,128)}, u32[]{:S(2)}) copy-start(f32[64,2048]{1,0:T(8,128)} %param.23) | copy-start | bytes 1572868
  0.6 2.9 %collective-permute-start = (f32[64,1024]{1,0:T(8,128)}, f32[64,1024]{1,0:T(8,128)S(1)}, u32[]{:S(2)}, u32[]{:S(2)}) collective-permute-start(f32[64,1024]{1,0:T(8,128)} %param.22), channel_id=1, source_target_pairs={{0,16},{16,0},{1,17},{17,1},{2,18},{18,2},{3,19},{19,3},{4,20},{20... | collective-permute-start | bytes 786440 | tf_op jit(solution)/shard_map/ppermute | solution.py:199
  4.5 67.6 %collective-permute-start.1 = (f32[2,64,1024]{2,1,0:T(8,128)S(1)}, f32[2,64,1024]{2,1,0:T(8,128)}, u32[]{:S(2)}, u32[]{:S(2)}) collective-permute-start(f32[2,64,1024]{2,1,0:T(8,128)S(1)} %pad_maximum_fusion.refs_0_), channel_id=1, source_target_pairs={{0,32},{32,64},{64,96},{96,0},{1,33},{33,65},{65,97},{97,1},{2,34}... | collective-permute-start | bytes 1572872 | tf_op jit(solution)/shard_map/ppermute | solution.py:201
  6.3 65.9 %collective-permute-start.2 = (f32[2,64,1024]{2,1,0:T(8,128)S(1)}, f32[2,64,1024]{2,1,0:T(8,128)}, u32[]{:S(2)}, u32[]{:S(2)}) collective-permute-start(f32[2,64,1024]{2,1,0:T(8,128)S(1)} %pad_maximum_fusion.refs_0_), channel_id=1, source_target_pairs={{0,64},{32,96},{64,0},{96,32},{1,65},{33,97},{65,1},{97,33},{2,66}... | collective-permute-start | bytes 1572872 | tf_op jit(solution)/shard_map/ppermute | solution.py:201
  15.6 56.5 %collective-permute-start.3 = (f32[2,64,1024]{2,1,0:T(8,128)S(1)}, f32[2,64,1024]{2,1,0:T(8,128)}, u32[]{:S(2)}, u32[]{:S(2)}) collective-permute-start(f32[2,64,1024]{2,1,0:T(8,128)S(1)} %pad_maximum_fusion.refs_0_), channel_id=1, source_target_pairs={{0,96},{32,0},{64,32},{96,64},{1,97},{33,1},{65,33},{97,65},{2,98}... | collective-permute-start | bytes 1572872 | tf_op jit(solution)/shard_map/ppermute | solution.py:201
  32.6 22.4 %all-to-all-start = ((f32[16,4,1024]{2,1,0:T(4,128)}), f32[16,4,1024]{2,1,0:T(4,128)S(1)}, u32[]{:S(2)}, u32[]{:S(2)}) async-start(f32[16,4,1024]{2,1,0:T(4,128)} %reshape.24), calls=%async_computation | async-start | bytes 524288 | tf_op jit(solution)/shard_map/all_to_all | solution.py:28
  39.3 2.2 copy-start.1
  41.5 2.2 copy-start.2
  52.9 1.4 copy-start.3
  55.1 1.6 copy-start.4
  72.2 4.6 %collective-permute-start.4 = (f32[64,1024]{1,0:T(8,128)S(1)}, f32[64,1024]{1,0:T(8,128)S(1)}, u32[]{:S(2)}, u32[]{:S(2)}) collective-permute-start(f32[64,1024]{1,0:T(8,128)S(1)} %reshape.26), channel_id=1, source_target_pairs={{0,16},{1,32},{2,48},{3,64},{4,80},{5,96},{6,112}} | collective-permute-start | bytes 786440 | tf_op jit(solution)/shard_map/ppermute | solution.py:40
  81.1 4.0 %collective-permute-start.7 = (f32[64,1024]{1,0:T(8,128)}, f32[64,1024]{1,0:T(8,128)}, u32[]{:S(2)}, u32[]{:S(2)}) collective-permute-start(f32[64,1024]{1,0:T(8,128)} %get-tuple-element.207), channel_id=1, source_target_pairs={{16,0}} | collective-permute-start | bytes 786440 | tf_op jit(solution)/shard_map/ppermute | solution.py:40
  83.1 4.1 %collective-permute-start.5 = (f32[64,1024]{1,0:T(8,128)}, f32[64,1024]{1,0:T(8,128)S(1)}, u32[]{:S(2)}, u32[]{:S(2)}) collective-permute-start(f32[64,1024]{1,0:T(8,128)} %get-tuple-element.207), channel_id=1, source_target_pairs={{32,33},{48,50},{64,67},{80,84},{96,101},{112,118}} | collective-permute-start | bytes 786440 | tf_op jit(solution)/shard_map/ppermute | solution.py:40
  83.8 7.1 %collective-permute-start.6 = (f32[64,1024]{1,0:T(8,128)}, f32[64,1024]{1,0:T(8,128)S(1)}, u32[]{:S(2)}, u32[]{:S(2)}) collective-permute-start(f32[64,1024]{1,0:T(8,128)} %get-tuple-element.207), channel_id=1, source_target_pairs={{16,33}} | collective-permute-start | bytes 786440 | tf_op jit(solution)/shard_map/ppermute | solution.py:40
  85.1 6.5 %collective-permute-start.10 = (f32[64,1024]{1,0:T(8,128)}, f32[64,1024]{1,0:T(8,128)S(1)}, u32[]{:S(2)}, u32[]{:S(2)}) collective-permute-start(f32[64,1024]{1,0:T(8,128)} %collective-permute-done.7), channel_id=1, source_target_pairs={{0,81}} | collective-permute-start | bytes 786440 | tf_op jit(solution)/shard_map/ppermute | solution.py:40
  85.8 5.8 %collective-permute-start.11 = (f32[64,1024]{1,0:T(8,128)}, f32[64,1024]{1,0:T(8,128)S(1)}, u32[]{:S(2)}, u32[]{:S(2)}) collective-permute-start(f32[64,1024]{1,0:T(8,128)} %collective-permute-done.7), channel_id=1, source_target_pairs={{0,97}} | collective-permute-start | bytes 786440 | tf_op jit(solution)/shard_map/ppermute | solution.py:40
  86.5 5.2 %collective-permute-start.12 = (f32[64,1024]{1,0:T(8,128)}, f32[64,1024]{1,0:T(8,128)S(1)}, u32[]{:S(2)}, u32[]{:S(2)}) collective-permute-start(f32[64,1024]{1,0:T(8,128)} %collective-permute-done.7), channel_id=1, source_target_pairs={{0,113}} | collective-permute-start | bytes 786440 | tf_op jit(solution)/shard_map/ppermute | solution.py:40
  87.2 4.5 %collective-permute-start.8 = (f32[64,1024]{1,0:T(8,128)}, f32[64,1024]{1,0:T(8,128)S(1)}, u32[]{:S(2)}, u32[]{:S(2)}) collective-permute-start(f32[64,1024]{1,0:T(8,128)} %collective-permute-done.7), channel_id=1, source_target_pairs={{0,49}} | collective-permute-start | bytes 786440 | tf_op jit(solution)/shard_map/ppermute | solution.py:40
  90.9 0.7 collective-permute-start.9
  91.7 2.8 %collective-permute-start.15 = (f32[64,1024]{1,0:T(8,128)}, f32[64,1024]{1,0:T(8,128)}, u32[]{:S(2)}, u32[]{:S(2)}) collective-permute-start(f32[64,1024]{1,0:T(8,128)} %get-tuple-element.208), channel_id=1, source_target_pairs={{33,49}} | collective-permute-start | bytes 786440 | tf_op jit(solution)/shard_map/ppermute | solution.py:40
  93.1 3.4 %collective-permute-start.13 = (f32[64,1024]{1,0:T(8,128)}, f32[64,1024]{1,0:T(8,128)S(1)}, u32[]{:S(2)}, u32[]{:S(2)}) collective-permute-start(f32[64,1024]{1,0:T(8,128)} %get-tuple-element.208), channel_id=1, source_target_pairs={{49,50},{65,67},{81,84},{97,101},{113,118}} | collective-permute-start | bytes 786440 | tf_op jit(solution)/shard_map/ppermute | solution.py:40
  93.7 4.2 %collective-permute-start.14 = (f32[64,1024]{1,0:T(8,128)}, f32[64,1024]{1,0:T(8,128)S(1)}, u32[]{:S(2)}, u32[]{:S(2)}) collective-permute-start(f32[64,1024]{1,0:T(8,128)} %get-tuple-element.208), channel_id=1, source_target_pairs={{33,50}} | collective-permute-start | bytes 786440 | tf_op jit(solution)/shard_map/ppermute | solution.py:40
  94.4 3.5 %collective-permute-start.16 = (f32[64,1024]{1,0:T(8,128)}, f32[64,1024]{1,0:T(8,128)S(1)}, u32[]{:S(2)}, u32[]{:S(2)}) collective-permute-start(f32[64,1024]{1,0:T(8,128)} %collective-permute-done.15), channel_id=1, source_target_pairs={{49,66}} | collective-permute-start | bytes 786440 | tf_op jit(solution)/shard_map/ppermute | solution.py:40
  95.1 2.9 %collective-permute-start.17 = (f32[64,1024]{1,0:T(8,128)}, f32[64,1024]{1,0:T(8,128)S(1)}, u32[]{:S(2)}, u32[]{:S(2)}) collective-permute-start(f32[64,1024]{1,0:T(8,128)} %collective-permute-done.15), channel_id=1, source_target_pairs={{49,82}} | collective-permute-start | bytes 786440 | tf_op jit(solution)/shard_map/ppermute | solution.py:40
  95.8 2.2 collective-permute-start.18
  96.5 1.5 collective-permute-start.19
  98.2 2.1 collective-permute-start.22
  98.9 3.5 %collective-permute-start.20 = (f32[64,1024]{1,0:T(8,128)}, f32[64,1024]{1,0:T(8,128)S(1)}, u32[]{:S(2)}, u32[]{:S(2)}) collective-permute-start(f32[64,1024]{1,0:T(8,128)} %get-tuple-element.209), channel_id=1, source_target_pairs={{66,67},{82,84},{98,101},{114,118}} | collective-permute-start | bytes 786440 | tf_op jit(solution)/shard_map/ppermute | solution.py:40
  99.6 2.8 %collective-permute-start.21 = (f32[64,1024]{1,0:T(8,128)}, f32[64,1024]{1,0:T(8,128)S(1)}, u32[]{:S(2)}, u32[]{:S(2)}) collective-permute-start(f32[64,1024]{1,0:T(8,128)} %get-tuple-element.209), channel_id=1, source_target_pairs={{50,67}} | collective-permute-start | bytes 786440 | tf_op jit(solution)/shard_map/ppermute | solution.py:40
  100.3 2.1 collective-permute-start.23
  101.0 1.4 collective-permute-start.24
  101.6 0.7 collective-permute-start.25
  102.4 2.1 collective-permute-start.28
  103.1 2.8 %collective-permute-start.26 = (f32[64,1024]{1,0:T(8,128)}, f32[64,1024]{1,0:T(8,128)S(1)}, u32[]{:S(2)}, u32[]{:S(2)}) collective-permute-start(f32[64,1024]{1,0:T(8,128)} %get-tuple-element.210), channel_id=1, source_target_pairs={{83,84},{99,101},{115,118}} | collective-permute-start | bytes 786440 | tf_op jit(solution)/shard_map/ppermute | solution.py:40
  103.8 2.2 collective-permute-start.27
  104.5 1.5 collective-permute-start.29
  105.2 0.8 collective-permute-start.30
  106.0 2.1 collective-permute-start.33
  106.7 2.1 collective-permute-start.31
  107.3 1.4 collective-permute-start.32
  108.0 0.7 collective-permute-start.34
  108.8 1.4 collective-permute-start.35
  109.5 0.7 collective-permute-start.36
  110.2 121.5 %copy-start.5 = (f32[1,2,8,128,128]{4,3,2,1,0:T(8,128)S(1)}, f32[1,2,8,128,128]{4,3,2,1,0:T(8,128)}, u32[]{:S(2)}) copy-start(f32[1,2,8,128,128]{4,3,2,1,0:T(8,128)} %param.29) | copy-start | bytes 3145732
  110.2 121.5 %copy-start.6 = (s32[1,2,8]{2,1,0:T(2,128)S(1)}, s32[1,2,8]{2,1,0:T(2,128)}, u32[]{:S(2)}) copy-start(s32[1,2,8]{2,1,0:T(2,128)} %param.28) | copy-start | bytes 196
  110.2 121.5 %copy-start.7 = (s32[1,2]{1,0:T(1,128)S(1)}, s32[1,2]{1,0:T(1,128)}, u32[]{:S(2)}) copy-start(s32[1,2]{1,0:T(1,128)} %param.27) | copy-start | bytes 28
  110.2 11.2 %all-to-all-start.2 = ((f32[16,8,512]{2,1,0:T(8,128)}), f32[16,8,512]{2,1,0:T(8,128)S(1)}, u32[]{:S(2)}, u32[]{:S(2)}) async-start(f32[16,8,512]{2,1,0:T(8,128)} %bitcast.9), calls=%async_computation.2 | async-start | bytes 524288 | tf_op jit(solution)/shard_map/all_to_all | solution.py:28

commit v3 on v2

--- a/solution.py
+++ b/solution.py
@@ -46,16 +46,24 @@
     return high, low
 
 
-def three_pass(left, right_high, right_low):
-    dims = (((1,), (1,)), ((), ()))
+ACROSS = (((1,), (1,)), ((), ()))
+
+
+def high_passes(left, right_high):
     left_high, left_low = split_bf16(left)
     rows = left.shape[0]
     both = lax.dot_general(
-        jnp.concatenate([left_high, left_low], axis=0), right_high, dims, preferred_element_type=jnp.float32
-    )
-    return (both[:rows] + both[rows:]) + lax.dot_general(
-        left_high, right_low, dims, preferred_element_type=jnp.float32
-    )
+        jnp.concatenate([left_high, left_low], axis=0), right_high, ACROSS, preferred_element_type=jnp.float32
+    )
+    return both[:rows] + both[rows:]
+
+
+def low_pass(left, right_low):
+    return lax.dot_general(left.astype(jnp.bfloat16), right_low, ACROSS, preferred_element_type=jnp.float32)
+
+
+def three_pass(left, right_high, right_low):
+    return high_passes(left, right_high) + low_pass(left, right_low)
 
 
 VMEM = pl.BlockSpec(memory_space=pltpu.VMEM)
@@ -66,75 +74,141 @@
     return pltpu.CompilerParams(vmem_limit_bytes=mib * 1024 * 1024)
 
 
-def form_kernel(inverse_ref, block_ref, inverse_high_ref, inverse_low_ref, high_ref, low_ref):
-    @pl.when(pl.program_id(0) == 0)
-    def _():
-        inverse_high_ref[...], inverse_low_ref[...] = split_bf16(inverse_ref[...])
-
-    count = block_ref.shape[0] // inverse_ref.shape[0]
-    first = pl.program_id(0) * 2
-    strips = [block_ref[pl.ds(first + i, inverse_ref.shape[0], stride=count), :] for i in range(2)]
-    block_high, block_low = split_bf16(jnp.concatenate(strips, axis=1))
+def in_hbm(x):
+    return pltpu.with_memory_space_constraint(x, pltpu.HBM)
+
+
+def in_vmem(x):
+    return pltpu.with_memory_space_constraint(x, pltpu.VMEM)
+
+
+PARTS = 4
+
+
+def form_kernel(
+    inverse_hbm,
+    block_hbm,
+    high_ref,
+    low_ref,
+    inverse_buffer,
+    block_buffer,
+    block_high_ref,
+    block_low_ref,
+    inverse_sems,
+    block_sems,
+):
+    order = inverse_buffer.shape[0]
+    part = order // PARTS
+    lines = block_buffer.shape[0] // PARTS
+    count = lines // part
+
+    def block_copy(i):
+        span = pl.ds(i * lines, lines)
+        return pltpu.make_async_copy(block_hbm.at[span], block_buffer.at[span], block_sems.at[i])
+
+    def inverse_copy(i):
+        span = pl.ds(i * part, part)
+        return pltpu.make_async_copy(inverse_hbm.at[span], inverse_buffer.at[span], inverse_sems.at[i])
+
+    for i in range(PARTS):
+        block_copy(i).start()
+    for i in range(PARTS):
+        inverse_copy(i).start()
+    for i in range(PARTS):
+        block_copy(i).wait()
+        span = pl.ds(i * part, part)
+        for j in range(count):
+            lanes = pl.ds(j * 128, 128)
+            strip = block_buffer[pl.ds(i * lines + j, part, stride=count), :]
+            block_high_ref[span, lanes], block_low_ref[span, lanes] = split_bf16(strip)
 
     def one(a, b):
         return jnp.dot(a, b, preferred_element_type=jnp.float32)
 
-    total = one(inverse_high_ref[...], block_high)
-    total = total + one(inverse_high_ref[...], block_low)
-    total = total + one(inverse_low_ref[...], block_high)
-    high_ref[...], low_ref[...] = split_bf16(total)
+    for i in range(PARTS):
+        inverse_copy(i).wait()
+        span = pl.ds(i * part, part)
+        inverse_high, inverse_low = split_bf16(inverse_buffer[span, :])
+        total = one(inverse_high, block_high_ref[...])
+        total = total + one(inverse_high, block_low_ref[...])
+        total = total + one(inverse_low, block_high_ref[...])
+        high_ref[span, :], low_ref[span, :] = split_bf16(total)
 
 
 def form(inverse, block):
     order = inverse.shape[0]
-    width = 256
     half = jax.ShapeDtypeStruct((order, order), jnp.bfloat16)
-    whole = pl.BlockSpec((order, order), lambda i: (0, 0))
-    strip = pl.BlockSpec((order, width), lambda i: (0, i))
+    hbm = pl.BlockSpec(memory_space=pltpu.HBM)
     return pl.pallas_call(
         form_kernel,
-        grid=(order // width,),
-        in_specs=[whole, pl.BlockSpec(block.shape, lambda i: (0, 0))],
-        out_specs=(whole, whole, strip, strip),
-        out_shape=(half, half, half, half),
+        in_specs=[hbm, hbm],
+        out_specs=(VMEM,) * 2,
+        out_shape=(half,) * 2,
+        scratch_shapes=[
+            pltpu.VMEM(inverse.shape, jnp.float32),
+            pltpu.VMEM(block.shape, jnp.float32),
+            pltpu.VMEM((order, order), jnp.bfloat16),
+            pltpu.VMEM((order, order), jnp.bfloat16),
+            pltpu.SemaphoreType.DMA((PARTS,)),
+            pltpu.SemaphoreType.DMA((PARTS,)),
+        ],
         compiler_params=room(24),
-    )(inverse, block)
-
-
-def start_kernel(rhs_ref, past_ref, high_ref, low_ref, out_ref):
+    )(in_hbm(inverse), in_hbm(block))
+
+
+def start_kernel(rhs_ref, past_ref, inverse_hbm, out_ref, buffer, sems):
+    part = buffer.shape[0] // PARTS
+
+    def copy(i):
+        span = pl.ds(i * part, part)
+        return pltpu.make_async_copy(inverse_hbm.at[span], buffer.at[span], sems.at[i])
+
+    for i in range(PARTS):
+        copy(i).start()
     diff = rhs_ref[...] - past_ref[...]
-    out_ref[...] = three_pass(diff, high_ref[...], low_ref[...])
-
-
-def start_product(rhs, past, high, low):
+    for i in range(PARTS):
+        copy(i).wait()
+        span = pl.ds(i * part, part)
+        out_ref[:, span] = three_pass(diff, *split_bf16(buffer[span, :]))
+
+
+def start_product(rhs, past, inverse):
     return pl.pallas_call(
         start_kernel,
-        in_specs=[VMEM] * 4,
+        in_specs=[VMEM, VMEM, pl.BlockSpec(memory_space=pltpu.HBM)],
         out_specs=VMEM,
         out_shape=jax.ShapeDtypeStruct(rhs.shape, jnp.float32),
-        compiler_params=room(4),
-    )(rhs, past, high, low)
+        scratch_shapes=[pltpu.VMEM(inverse.shape, jnp.float32), pltpu.SemaphoreType.DMA((PARTS,))],
+        compiler_params=room(12),
+    )(rhs, past, in_hbm(inverse))
 
 
 def fire(bases, knowns, high, low):
     count = len(bases)
 
     def kernel(*refs):
-        total = refs[0][...]
-        for ref in refs[1:count]:
+        base_refs, known_refs = refs[:count], refs[count:-5]
+        high_ref, low_hbm, out_ref, low_buffer, sem = refs[-5:]
+        copy = pltpu.make_async_copy(low_hbm, low_buffer, sem)
+        copy.start()
+        total = base_refs[0][...]
+        for ref in base_refs[1:]:
             total = total + ref[...]
-        known = refs[count][...]
-        for ref in refs[count + 1 : -3]:
+        known = known_refs[0][...]
+        for ref in known_refs[1:]:
             known = known + ref[...]
-        refs[-1][...] = total - three_pass(known, refs[-3][...], refs[-2][...])
+        total = total - high_passes(known, high_ref[...])
+        copy.wait()
+        out_ref[...] = total - low_pass(known, low_buffer[...])
 
     return pl.pallas_call(
         kernel,
-        in_specs=[VMEM] * (count + len(knowns) + 2),
+        in_specs=[VMEM] * (count + len(knowns) + 1) + [pl.BlockSpec(memory_space=pltpu.HBM)],
         out_specs=VMEM,
         out_shape=jax.ShapeDtypeStruct(knowns[0].shape, jnp.float32),
-        compiler_params=room(8),
-    )(*bases, *knowns, high, low)
+        scratch_shapes=[pltpu.VMEM(low.shape, low.dtype), pltpu.SemaphoreType.DMA],
+        compiler_params=room(10),
+    )(*bases, *knowns, high, in_hbm(low))
 
 
 def finish_kernel(tiles_ref, near_ref, row_ref, pieces_ref, *refs):
@@ -198,15 +272,24 @@
 
     other_rhs = lax.ppermute(window_rhs, "prow_1", [(0, 1), (1, 0)])
     pair = jnp.stack([window_rhs, other_rhs])
-    full_rhs = [pair] + [lax.ppermute(pair, "prow_0", [(i, (i + d) % 4) for i in range(4)]) for d in (1, 2, 3)]
-
+
+    def around(x, distance):
+        return lax.ppermute(x, "prow_0", [(i, (i + distance) % 4) for i in range(4)])
+
+    next_rhs = around(pair, 1)
     past = product(past_solution, past_panel, 1, 1)
+    past, pair, next_rhs = lax.optimization_barrier((past, pair, next_rhs))
+    last_rhs = around(pair, 3)
     past_rows = exchange(past.reshape(COLS, 4, 1024), PCOL).sum(axis=0)
-    inverse_high, inverse_low, high, low = form(inverse, block)
+    high, low = form(inverse, block)
+    high = in_vmem(high)
+    past_rows, pair, last_rhs, high = lax.optimization_barrier((past_rows, pair, last_rhs, high))
+    far_rhs = around(pair, 2)
     rhs_rows = lax.dynamic_slice_in_dim(window_rhs, col * 4, 4, 0)
-    start_rows = start_product(rhs_rows, past_rows, inverse_high, inverse_low)
+    start_rows = start_product(rhs_rows, past_rows, inverse)
     start = to_everyone(start_rows, PCOL, COLS).reshape(64, 1024)
-    start, *full_rhs = lax.optimization_barrier((start, *full_rhs))
+    start, far_rhs = lax.optimization_barrier((start, far_rhs))
+    full_rhs = [pair, next_rhs, far_rhs, last_rhs]
 
     total = jnp.where(row == col + 1, start, jnp.zeros_like(start))
     arrived = send(start, [(place(0, k - 1), place(k, 0)) for k in range(1, ROWS)])

time: 236 us -> 251 us (1.064)
  starting transfers between devices: 58.2 us -> 77.8 us
  blocking collectives: 124 us -> 115 us
  local copies, waits for them, and re-layouts: 9.3 us -> 2.92 us
  Pallas kernels: 17.7 us -> 22.4 us
  other arithmetic: 1.18 us -> 5.51 us
  waiting for transfers between devices: 15.2 us -> 17.8 us
    ppermute x33, starting transfers between devices: 26.3 us -> 46.9 us  [send(): return lax.ppermute(x, EVERY, pairs)]
    all_to_all x2, blocking collectives: 124 us -> 115 us  [exchange(): return lax.all_to_all(pieces, axes, 0, 0, tiled=True)]
    unnamed x16, local copies, waits for them, and re-layouts: 7.35 us -> 0.04 us
    ppermute x3, waiting for transfers between devices: 0.01 us -> 6.81 us  [around(): lax.ppermute(x, 'prow_0', [(i, (i + distance) % 4) for i in range(4)])]
    pallas_call x3, Pallas kernels: 14.8 us -> 19.6 us  [the longest x1 12.1 us: form(): pl.pallas_call(form_kernel, in_specs=[hbm, hbm], out_specs=(VMEM,) * 2, o...]
    ppermute x33, waiting for transfers between devices: 6.36 us -> 2.16 us  [send(): return lax.ppermute(x, EVERY, pairs)]
    add x2, other arithmetic: 0.11 us -> 3.73 us  [per_device(): total = total + extra]
  transfers between devices with their start and end apart: 39 -> 39, of which waited for: 4 -> 5; matrix products, arithmetic and copies ran while one was open for 4% -> 6% of each run, Pallas kernels for 4% -> 6%
where the time goes in v3:
time: 251 us; the launch traced here: 250 us
  blocking collectives  115 us (46%)
  starting transfers between devices  77.8 us (31%)
  Pallas kernels  22.4 us (9%)
  waiting for transfers between devices  17.8 us (7%)
  matrix products  7.31 us (3%)
  other arithmetic  5.51 us (2%)
  local copies, waits for them, and re-layouts  2.92 us (1%)
    all_to_all x2, blocking collectives, exchange(): return lax.all_to_all(pieces, axes, 0, 0, tiled=True)  115 us
    ppermute x33, starting transfers between devices, send(): return lax.ppermute(x, EVERY, pairs)  46.9 us
    ppermute x3, starting transfers between devices, around(): lax.ppermute(x, 'prow_0', [(i, (i + distance) % 4) for i in range(4)])  19 us
    pallas_call x1, Pallas kernels, form(): pl.pallas_call(form_kernel, in_specs=[hbm, hbm], out_specs=(VMEM,) * 2, o...  12.1 us
    all_to_all x2, starting transfers between devices, exchange(): return lax.all_to_all(pieces, axes, 0, 0, tiled=True)  10.4 us
    all_to_all x2, waiting for transfers between devices, exchange(): return lax.all_to_all(pieces, axes, 0, 0, tiled=True)  7.5 us
    dot_general x1, matrix products, product(): lax.dot_general(left, right, (((left_dim,), (right_dim,)), ((), ())), pre...  7.31 us
    ppermute x3, waiting for transfers between devices, around(): lax.ppermute(x, 'prow_0', [(i, (i + distance) % 4) for i in range(4)])  6.81 us
  transfers between devices with their start and end apart: 39, of which 5 were waited for; matrix products, arithmetic and copies ran while one was open for 6% of the time, Pallas kernels for 6%

profile of v3, /device:TPU:1, one launch (start us, length us, event | category | flops | bytes accessed | tf_op | source)
XLA Modules:
  0.0 250.2 jit_solution(13730629594409056685)
XLA Ops:
  0.6 0.0 copy-start
  0.6 1.5 collective-permute-start
  2.1 1.4 collective-permute-done
  3.5 1.0 pad_maximum_fusion.refs_0_
  4.5 1.8 collective-permute-start.1
  6.3 7.3 %fusion.2 = f32[64,1024]{1,0:T(8,128)S(1)} fusion(f32[64,2048]{1,0:T(8,128)S(1)} %copy-done, f32[1024,2048]{1,0:T(8,128)} %param.24), kind=kOutput, calls=%fused_computation.6 | convolution fusion | flops 805306368 | bytes 9175040 | tf_op jit(solution)/shard_map/dot_general | solution.py:18
  13.6 6.8 %collective-permute-done.1.refs_1_ = f32[2,64,1024]{2,1,0:T(8,128)S(1)} collective-permute-done((f32[2,64,1024]{2,1,0:T(8,128)S(1)}, f32[2,64,1024]{2,1,0:T(8,128)S(1)}, u32[]{:S(2)}, u32[]{:S(2)}) %collective-permute-start.1) | collective-permute-done | bytes 524320 | tf_op jit(solution)/shard_map/ppermute | solution.py:277
  20.4 7.7 %collective-permute-start.2 = (f32[2,64,1024]{2,1,0:T(8,128)S(1)}, f32[2,64,1024]{2,1,0:T(8,128)}, u32[]{:S(2)}, u32[]{:S(2)}) collective-permute-start(f32[2,64,1024]{2,1,0:T(8,128)S(1)} %pad_maximum_fusion.refs_0_), channel_id=1, source_target_pairs={{0,96},{32,0},{64,32},{96,64},{1,97},{33,1},{65,33},{97,65},{2,98}... | collective-permute-start | bytes 1572872 | tf_op jit(solution)/shard_map/ppermute | solution.py:277
  28.1 0.8 reshape.24
  28.9 6.7 %all-to-all-start = ((f32[16,4,1024]{2,1,0:T(4,128)}), f32[16,4,1024]{2,1,0:T(4,128)S(1)}, u32[]{:S(2)}, u32[]{:S(2)}) async-start(f32[16,4,1024]{2,1,0:T(4,128)} %reshape.24), calls=%async_computation | async-start | bytes 524288 | tf_op jit(solution)/shard_map/all_to_all | solution.py:28
  35.6 12.1 %shard_map.95 = (bf16[1024,1024]{1,0:T(8,128)(2,1)S(1)}, bf16[1024,1024]{1,0:T(8,128)(2,1)}) custom-call(f32[1024,1024]{1,0:T(8,128)} %bitcast.21, f32[8192,128]{1,0:T(8,128)} %bitcast.23), custom_call_target="tpu_custom_call" | custom-call | tf_op jit(solution)/shard_map/pallas_call | solution.py:142
  47.7 0.1 reduce_sum.9.past_ref
  47.8 9.5 %collective-permute-start.3 = (f32[2,64,1024]{2,1,0:T(8,128)S(1)}, f32[2,64,1024]{2,1,0:T(8,128)}, u32[]{:S(2)}, u32[]{:S(2)}) collective-permute-start(f32[2,64,1024]{2,1,0:T(8,128)S(1)} %pad_maximum_fusion.refs_0_), channel_id=1, source_target_pairs={{0,64},{32,96},{64,0},{96,32},{1,65},{33,97},{65,1},{97,33},{2,66}... | collective-permute-start | bytes 1572872 | tf_op jit(solution)/shard_map/ppermute | solution.py:277
  57.3 0.8 constant_dynamic-slice_fusion.rhs_ref
  58.0 2.8 %shard_map.96 = f32[4,1024]{1,0:T(4,128)S(1)} custom-call(f32[4,1024]{1,0:T(4,128)S(1)} %constant_dynamic-slice_fusion.rhs_ref, f32[4,1024]{1,0:T(4,128)S(1)} %reduce_sum.9.past_ref, f32[1024,1024]{1,0:T(8,128)} %bitcast.22), custom_call_target="tpu_custom_call" | custom-call | tf_op jit(solution)/shard_map/pallas_call | solution.py:176
  60.9 14.7 %all_to_all.20 = f32[16,4,1024]{2,1,0:T(4,128)} all-to-all(f32[16,4,1024]{2,1,0:T(4,128)S(1)} %broadcast_in_dim.20), channel_id=1, replica_groups=mesh['prow_0'=4,'prow_1'=2,'pcol_0'=4,'pcol_1'=4] {'pcol_0','pcol_1'}, dimensions={0} | all-to-all | bytes 524288 | tf_op jit(solution)/shard_map/all_to_all | solution.py:28
  75.7 1.0 reshape.26
  76.7 1.3 collective-permute-start.4
  78.0 0.7 broadcast_select_fusion
  78.8 1.9 collective-permute-done.4
  80.7 4.7 %conditional.7 = (f32[64,1024]{1,0:T(8,128)}) conditional(s32[]{:T(128)} %convert_element_type.27, f32[64,1024]{1,0:T(8,128)S(1)} %reshape.26, (f32[64,1024]{1,0:T(8,128)}, f32[64,1024]{1,0:T(8,128)}, bf16[1024,1024]{1,0:T(8,128)(2,1)S(1)}, bf16[1024,1024]{1,0:T(8,128)(2,1)}) %tuple.56), branch_computations={%region_1.2_spmd, %region_2.3_spmd} | conditional | bytes 524296 | solution.py:296
  80.7 4.7 %branch_1_fun.7 = f32[64,1024]{1,0:T(8,128)} custom-call(f32[64,1024]{1,0:T(8,128)} %get-tuple-element.129.refs_0_, f32[64,1024]{1,0:T(8,128)} %get-tuple-element.130.refs_1_, bf16[1024,1024]{1,0:T(8,128)(2,1)S(1)} %get-tuple-element.131.refs_2_, bf16[1024,1024]{1,0:T(8,128)(2,1)} %get-tuple-element.132.refs_3_), custom_call_target="tpu_custom_call" | custom-call | tf_op jit(solution)/shard_map/cond/branch_1_fun/pallas_call | solution.py:204
  85.4 2.0 collective-permute-start.7
  87.4 1.4 collective-permute-start.5
  88.8 2.0 collective-permute-start.6
  90.8 1.4 collective-permute-start.10
  92.2 1.4 collective-permute-start.11
  93.5 1.4 collective-permute-start.12
  94.9 1.4 collective-permute-start.8
  96.3 0.2 collective-permute-done.6
  96.5 1.4 collective-permute-start.9
  97.9 1.4 collective-permute-start.15
  99.3 1.4 collective-permute-start.13
  100.7 1.4 collective-permute-start.14
  102.1 1.4 collective-permute-start.16
  103.4 1.4 collective-permute-start.17
  104.8 1.4 collective-permute-start.18
  106.2 1.4 collective-permute-start.19
  107.6 1.9 fusion.1
  109.5 1.5 collective-permute-start.22
  111.0 1.4 collective-permute-start.20
  112.4 1.4 collective-permute-start.21
  113.8 1.4 collective-permute-start.23
  115.1 1.4 collective-permute-start.24
  116.5 1.4 collective-permute-start.25
  118.0 1.4 collective-permute-start.28
  119.3 1.4 collective-permute-start.26
  120.7 1.4 collective-permute-start.27
  122.1 1.4 collective-permute-start.29
  123.5 1.4 collective-permute-start.30
  124.9 1.9 fusion
  126.8 1.5 collective-permute-start.33
  128.3 1.4 collective-permute-start.31
  129.7 1.4 collective-permute-start.32
  131.0 1.4 collective-permute-start.34
  132.4 1.4 collective-permute-start.35
  133.8 1.4 collective-permute-start.36
  135.2 0.0 copy-start.4
  135.2 0.0 copy-start.5
  135.3 3.7 %all-to-all-start.2 = ((f32[16,8,512]{2,1,0:T(8,128)}), f32[16,8,512]{2,1,0:T(8,128)S(1)}, u32[]{:S(2)}, u32[]{:S(2)}) async-start(f32[16,8,512]{2,1,0:T(8,128)} %bitcast.24), calls=%async_computation.2 | async-start | bytes 524288 | tf_op jit(solution)/shard_map/all_to_all | solution.py:28
  138.9 7.5 %all-to-all-done.2 = f32[16,8,512]{2,1,0:T(8,128)S(1)} async-done(((f32[16,8,512]{2,1,0:T(8,128)}), f32[16,8,512]{2,1,0:T(8,128)S(1)}, u32[]{:S(2)}, u32[]{:S(2)}) %all-to-all-start.2) | async-done | bytes 262176 | tf_op jit(solution)/shard_map/all_to_all | solution.py:28
  146.4 0.3 broadcast_in_dim.23
  146.7 100.7 %all_to_all.21.pieces_ref = f32[128,8,512]{2,1,0:T(8,128)S(1)} all-to-all(f32[128,8,512]{2,1,0:T(8,128)S(1)} %broadcast_in_dim.23), channel_id=1, replica_groups=mesh['prow_0'=4,'prow_1'=2,'pcol_0'=4,'pcol_1'=4] {'prow_0','prow_1','pc..., dimensions={0} | all-to-all | bytes 4194304 | tf_op jit(solution)/shard_map/all_to_all | solution.py:28
  247.4 2.8 %shard_map.97 = (f32[64,1024]{1,0:T(8,128)}, f32[2,64,128]{2,1,0:T(8,128)}) custom-call(s32[2]{0:T(128)S(1)} %bitcast.20, s32[2,8]{1,0:T(2,128)S(1)} %bitcast.19, s32[1]{0:T(128)} %bitcast.2.row_ref, f32[128,8,512]{2,1,0:T(8,128)S(1)} %all_to_all.21.pieces_ref, f32[2,64,1024]{2,1,0:T(8,128)S(1)} %pad_maximum_fusion.refs_0_, f32[2,64,1024]{2,1,0:T(8,128)S(1)} %copy-done.3, ...), custom_call_target="tpu_custom_call" | custom-call | tf_op jit(solution)/shard_map/pallas_call | solution.py:246
  (55 shorter events, 0.2 us)
Async XLA Ops:
  0.6 5.7 %copy-start = (f32[64,2048]{1,0:T(8,128)S(1)}, f32[64,2048]{1,0:T(8,128)}, u32[]{:S(2)}) copy-start(f32[64,2048]{1,0:T(8,128)} %param.23) | copy-start | bytes 1572868
  0.6 2.9 %collective-permute-start = (f32[64,1024]{1,0:T(8,128)}, f32[64,1024]{1,0:T(8,128)S(1)}, u32[]{:S(2)}, u32[]{:S(2)}) collective-permute-start(f32[64,1024]{1,0:T(8,128)} %param.22), channel_id=1, source_target_pairs={{0,16},{16,0},{1,17},{17,1},{2,18},{18,2},{3,19},{19,3},{4,20},{20... | collective-permute-start | bytes 786440 | tf_op jit(solution)/shard_map/ppermute | solution.py:273
  4.5 15.9 %collective-permute-start.1 = (f32[2,64,1024]{2,1,0:T(8,128)S(1)}, f32[2,64,1024]{2,1,0:T(8,128)S(1)}, u32[]{:S(2)}, u32[]{:S(2)}) collective-permute-start(f32[2,64,1024]{2,1,0:T(8,128)S(1)} %pad_maximum_fusion.refs_0_), channel_id=1, source_target_pairs={{0,32},{32,64},{64,96},{96,0},{1,33},{33,65},{65,97},{97,1},{2,34}... | collective-permute-start | bytes 1572872 | tf_op jit(solution)/shard_map/ppermute | solution.py:277
  20.4 15.2 %copy-start.2 = (f32[2,64,1024]{2,1,0:T(8,128)}, f32[2,64,1024]{2,1,0:T(8,128)S(1)}, u32[]{:S(2)}) copy-start(f32[2,64,1024]{2,1,0:T(8,128)S(1)} %collective-permute-done.1.refs_1_) | copy-start | bytes 1572868
  20.4 27.3 %collective-permute-start.2 = (f32[2,64,1024]{2,1,0:T(8,128)S(1)}, f32[2,64,1024]{2,1,0:T(8,128)}, u32[]{:S(2)}, u32[]{:S(2)}) collective-permute-start(f32[2,64,1024]{2,1,0:T(8,128)S(1)} %pad_maximum_fusion.refs_0_), channel_id=1, source_target_pairs={{0,96},{32,0},{64,32},{96,64},{1,97},{33,1},{65,33},{97,65},{2,98}... | collective-permute-start | bytes 1572872 | tf_op jit(solution)/shard_map/ppermute | solution.py:277
  28.9 18.8 %all-to-all-start = ((f32[16,4,1024]{2,1,0:T(4,128)}), f32[16,4,1024]{2,1,0:T(4,128)S(1)}, u32[]{:S(2)}, u32[]{:S(2)}) async-start(f32[16,4,1024]{2,1,0:T(4,128)} %reshape.24), calls=%async_computation | async-start | bytes 524288 | tf_op jit(solution)/shard_map/all_to_all | solution.py:28
  47.8 28.9 %collective-permute-start.3 = (f32[2,64,1024]{2,1,0:T(8,128)S(1)}, f32[2,64,1024]{2,1,0:T(8,128)}, u32[]{:S(2)}, u32[]{:S(2)}) collective-permute-start(f32[2,64,1024]{2,1,0:T(8,128)S(1)} %pad_maximum_fusion.refs_0_), channel_id=1, source_target_pairs={{0,64},{32,96},{64,0},{96,32},{1,65},{33,97},{65,1},{97,33},{2,66}... | collective-permute-start | bytes 1572872 | tf_op jit(solution)/shard_map/ppermute | solution.py:277
  76.7 3.9 %collective-permute-start.4 = (f32[64,1024]{1,0:T(8,128)S(1)}, f32[64,1024]{1,0:T(8,128)}, u32[]{:S(2)}, u32[]{:S(2)}) collective-permute-start(f32[64,1024]{1,0:T(8,128)S(1)} %reshape.26), channel_id=1, source_target_pairs={{0,16},{1,32},{2,48},{3,64},{4,80},{5,96},{6,112}} | collective-permute-start | bytes 786440 | tf_op jit(solution)/shard_map/ppermute | solution.py:40
  85.4 5.4 %collective-permute-start.7 = (f32[64,1024]{1,0:T(8,128)}, f32[64,1024]{1,0:T(8,128)}, u32[]{:S(2)}, u32[]{:S(2)}) collective-permute-start(f32[64,1024]{1,0:T(8,128)} %get-tuple-element.211), channel_id=1, source_target_pairs={{16,0}} | collective-permute-start | bytes 786440 | tf_op jit(solution)/shard_map/ppermute | solution.py:40
  87.4 7.5 %collective-permute-start.5 = (f32[64,1024]{1,0:T(8,128)}, f32[64,1024]{1,0:T(8,128)}, u32[]{:S(2)}, u32[]{:S(2)}) collective-permute-start(f32[64,1024]{1,0:T(8,128)} %get-tuple-element.211), channel_id=1, source_target_pairs={{32,33},{48,50},{64,67},{80,84},{96,101},{112,118}} | collective-permute-start | bytes 786440 | tf_op jit(solution)/shard_map/ppermute | solution.py:40
  88.8 7.7 %collective-permute-start.6 = (f32[64,1024]{1,0:T(8,128)}, f32[64,1024]{1,0:T(8,128)}, u32[]{:S(2)}, u32[]{:S(2)}) collective-permute-start(f32[64,1024]{1,0:T(8,128)} %get-tuple-element.211), channel_id=1, source_target_pairs={{16,33}} | collective-permute-start | bytes 786440 | tf_op jit(solution)/shard_map/ppermute | solution.py:40
  90.8 7.1 %collective-permute-start.10 = (f32[64,1024]{1,0:T(8,128)}, f32[64,1024]{1,0:T(8,128)}, u32[]{:S(2)}, u32[]{:S(2)}) collective-permute-start(f32[64,1024]{1,0:T(8,128)} %collective-permute-done.7), channel_id=1, source_target_pairs={{0,81}} | collective-permute-start | bytes 786440 | tf_op jit(solution)/shard_map/ppermute | solution.py:40
  92.2 5.7 %collective-permute-start.11 = (f32[64,1024]{1,0:T(8,128)}, f32[64,1024]{1,0:T(8,128)}, u32[]{:S(2)}, u32[]{:S(2)}) collective-permute-start(f32[64,1024]{1,0:T(8,128)} %collective-permute-done.7), channel_id=1, source_target_pairs={{0,97}} | collective-permute-start | bytes 786440 | tf_op jit(solution)/shard_map/ppermute | solution.py:40
  93.5 4.3 %collective-permute-start.12 = (f32[64,1024]{1,0:T(8,128)}, f32[64,1024]{1,0:T(8,128)}, u32[]{:S(2)}, u32[]{:S(2)}) collective-permute-start(f32[64,1024]{1,0:T(8,128)} %collective-permute-done.7), channel_id=1, source_target_pairs={{0,113}} | collective-permute-start | bytes 786440 | tf_op jit(solution)/shard_map/ppermute | solution.py:40
  94.9 3.0 %collective-permute-start.8 = (f32[64,1024]{1,0:T(8,128)}, f32[64,1024]{1,0:T(8,128)}, u32[]{:S(2)}, u32[]{:S(2)}) collective-permute-start(f32[64,1024]{1,0:T(8,128)} %collective-permute-done.7), channel_id=1, source_target_pairs={{0,49}} | collective-permute-start | bytes 786440 | tf_op jit(solution)/shard_map/ppermute | solution.py:40
  96.5 1.4 collective-permute-start.9
  97.9 4.1 %collective-permute-start.15 = (f32[64,1024]{1,0:T(8,128)}, f32[64,1024]{1,0:T(8,128)}, u32[]{:S(2)}, u32[]{:S(2)}) collective-permute-start(f32[64,1024]{1,0:T(8,128)} %get-tuple-element.212), channel_id=1, source_target_pairs={{33,49}} | collective-permute-start | bytes 786440 | tf_op jit(solution)/shard_map/ppermute | solution.py:40
  99.3 6.9 %collective-permute-start.13 = (f32[64,1024]{1,0:T(8,128)}, f32[64,1024]{1,0:T(8,128)}, u32[]{:S(2)}, u32[]{:S(2)}) collective-permute-start(f32[64,1024]{1,0:T(8,128)} %get-tuple-element.212), channel_id=1, source_target_pairs={{49,50},{65,67},{81,84},{97,101},{113,118}} | collective-permute-start | bytes 786440 | tf_op jit(solution)/shard_map/ppermute | solution.py:40
  100.7 8.8 %collective-permute-start.14 = (f32[64,1024]{1,0:T(8,128)}, f32[64,1024]{1,0:T(8,128)}, u32[]{:S(2)}, u32[]{:S(2)}) collective-permute-start(f32[64,1024]{1,0:T(8,128)} %get-tuple-element.212), channel_id=1, source_target_pairs={{33,50}} | collective-permute-start | bytes 786440 | tf_op jit(solution)/shard_map/ppermute | solution.py:40
  102.1 7.4 %collective-permute-start.16 = (f32[64,1024]{1,0:T(8,128)}, f32[64,1024]{1,0:T(8,128)}, u32[]{:S(2)}, u32[]{:S(2)}) collective-permute-start(f32[64,1024]{1,0:T(8,128)} %collective-permute-done.15), channel_id=1, source_target_pairs={{49,66}} | collective-permute-start | bytes 786440 | tf_op jit(solution)/shard_map/ppermute | solution.py:40
  103.4 6.0 %collective-permute-start.17 = (f32[64,1024]{1,0:T(8,128)}, f32[64,1024]{1,0:T(8,128)}, u32[]{:S(2)}, u32[]{:S(2)}) collective-permute-start(f32[64,1024]{1,0:T(8,128)} %collective-permute-done.15), channel_id=1, source_target_pairs={{49,82}} | collective-permute-start | bytes 786440 | tf_op jit(solution)/shard_map/ppermute | solution.py:40
  104.8 4.6 %collective-permute-start.18 = (f32[64,1024]{1,0:T(8,128)}, f32[64,1024]{1,0:T(8,128)}, u32[]{:S(2)}, u32[]{:S(2)}) collective-permute-start(f32[64,1024]{1,0:T(8,128)} %collective-permute-done.15), channel_id=1, source_target_pairs={{49,98}} | collective-permute-start | bytes 786440 | tf_op jit(solution)/shard_map/ppermute | solution.py:40
  106.2 3.3 %collective-permute-start.19 = (f32[64,1024]{1,0:T(8,128)}, f32[64,1024]{1,0:T(8,128)}, u32[]{:S(2)}, u32[]{:S(2)}) collective-permute-start(f32[64,1024]{1,0:T(8,128)} %collective-permute-done.15), channel_id=1, source_target_pairs={{49,114}} | collective-permute-start | bytes 786440 | tf_op jit(solution)/shard_map/ppermute | solution.py:40
  109.4 8.5 %copy-start.6 = (f32[64,1024]{1,0:T(8,128)S(1)}, f32[64,1024]{1,0:T(8,128)}, u32[]{:S(2)}) copy-start(f32[64,1024]{1,0:T(8,128)} %get-tuple-element.209) | copy-start | bytes 786436
  109.5 4.3 %collective-permute-start.22 = (f32[64,1024]{1,0:T(8,128)}, f32[64,1024]{1,0:T(8,128)}, u32[]{:S(2)}, u32[]{:S(2)}) collective-permute-start(f32[64,1024]{1,0:T(8,128)} %get-tuple-element.213), channel_id=1, source_target_pairs={{50,34}} | collective-permute-start | bytes 786440 | tf_op jit(solution)/shard_map/ppermute | solution.py:40
  111.0 6.9 %collective-permute-start.20 = (f32[64,1024]{1,0:T(8,128)}, f32[64,1024]{1,0:T(8,128)}, u32[]{:S(2)}, u32[]{:S(2)}) collective-permute-start(f32[64,1024]{1,0:T(8,128)} %get-tuple-element.213), channel_id=1, source_target_pairs={{66,67},{82,84},{98,101},{114,118}} | collective-permute-start | bytes 786440 | tf_op jit(solution)/shard_map/ppermute | solution.py:40
  112.4 5.5 %collective-permute-start.21 = (f32[64,1024]{1,0:T(8,128)}, f32[64,1024]{1,0:T(8,128)}, u32[]{:S(2)}, u32[]{:S(2)}) collective-permute-start(f32[64,1024]{1,0:T(8,128)} %get-tuple-element.213), channel_id=1, source_target_pairs={{50,67}} | collective-permute-start | bytes 786440 | tf_op jit(solution)/shard_map/ppermute | solution.py:40
  113.8 4.2 %collective-permute-start.23 = (f32[64,1024]{1,0:T(8,128)}, f32[64,1024]{1,0:T(8,128)}, u32[]{:S(2)}, u32[]{:S(2)}) collective-permute-start(f32[64,1024]{1,0:T(8,128)} %collective-permute-done.22), channel_id=1, source_target_pairs={{34,83}} | collective-permute-start | bytes 786440 | tf_op jit(solution)/shard_map/ppermute | solution.py:40
  115.1 2.8 %collective-permute-start.24 = (f32[64,1024]{1,0:T(8,128)}, f32[64,1024]{1,0:T(8,128)}, u32[]{:S(2)}, u32[]{:S(2)}) collective-permute-start(f32[64,1024]{1,0:T(8,128)} %collective-permute-done.22), channel_id=1, source_target_pairs={{34,99}} | collective-permute-start | bytes 786440 | tf_op jit(solution)/shard_map/ppermute | solution.py:40
  116.5 1.4 collective-permute-start.25
  118.0 4.1 %collective-permute-start.28 = (f32[64,1024]{1,0:T(8,128)}, f32[64,1024]{1,0:T(8,128)}, u32[]{:S(2)}, u32[]{:S(2)}) collective-permute-start(f32[64,1024]{1,0:T(8,128)} %get-tuple-element.214), channel_id=1, source_target_pairs={{67,83}} | collective-permute-start | bytes 786440 | tf_op jit(solution)/shard_map/ppermute | solution.py:40
  119.3 5.5 %collective-permute-start.26 = (f32[64,1024]{1,0:T(8,128)}, f32[64,1024]{1,0:T(8,128)}, u32[]{:S(2)}, u32[]{:S(2)}) collective-permute-start(f32[64,1024]{1,0:T(8,128)} %get-tuple-element.214), channel_id=1, source_target_pairs={{83,84},{99,101},{115,118}} | collective-permute-start | bytes 786440 | tf_op jit(solution)/shard_map/ppermute | solution.py:40
  120.7 6.0 %collective-permute-start.27 = (f32[64,1024]{1,0:T(8,128)}, f32[64,1024]{1,0:T(8,128)}, u32[]{:S(2)}, u32[]{:S(2)}) collective-permute-start(f32[64,1024]{1,0:T(8,128)} %get-tuple-element.214), channel_id=1, source_target_pairs={{67,84}} | collective-permute-start | bytes 786440 | tf_op jit(solution)/shard_map/ppermute | solution.py:40
  122.1 4.6 %collective-permute-start.29 = (f32[64,1024]{1,0:T(8,128)}, f32[64,1024]{1,0:T(8,128)}, u32[]{:S(2)}, u32[]{:S(2)}) collective-permute-start(f32[64,1024]{1,0:T(8,128)} %collective-permute-done.28), channel_id=1, source_target_pairs={{83,100}} | collective-permute-start | bytes 786440 | tf_op jit(solution)/shard_map/ppermute | solution.py:40
  123.5 3.3 %collective-permute-start.30 = (f32[64,1024]{1,0:T(8,128)}, f32[64,1024]{1,0:T(8,128)}, u32[]{:S(2)}, u32[]{:S(2)}) collective-permute-start(f32[64,1024]{1,0:T(8,128)} %collective-permute-done.28), channel_id=1, source_target_pairs={{83,116}} | collective-permute-start | bytes 786440 | tf_op jit(solution)/shard_map/ppermute | solution.py:40
  126.7 5.7 %copy-start.7 = (f32[64,1024]{1,0:T(8,128)S(1)}, f32[64,1024]{1,0:T(8,128)}, u32[]{:S(2)}) copy-start(f32[64,1024]{1,0:T(8,128)} %get-tuple-element.207) | copy-start | bytes 786436
  126.8 4.3 %collective-permute-start.33 = (f32[64,1024]{1,0:T(8,128)}, f32[64,1024]{1,0:T(8,128)}, u32[]{:S(2)}, u32[]{:S(2)}) collective-permute-start(f32[64,1024]{1,0:T(8,128)} %get-tuple-element.215), channel_id=1, source_target_pairs={{84,68}} | collective-permute-start | bytes 786440 | tf_op jit(solution)/shard_map/ppermute | solution.py:40
  128.3 4.1 %collective-permute-start.31 = (f32[64,1024]{1,0:T(8,128)}, f32[64,1024]{1,0:T(8,128)}, u32[]{:S(2)}, u32[]{:S(2)}) collective-permute-start(f32[64,1024]{1,0:T(8,128)} %get-tuple-element.215), channel_id=1, source_target_pairs={{100,101},{116,118}} | collective-permute-start | bytes 786440 | tf_op jit(solution)/shard_map/ppermute | solution.py:40
  129.7 2.8 %collective-permute-start.32 = (f32[64,1024]{1,0:T(8,128)}, f32[64,1024]{1,0:T(8,128)}, u32[]{:S(2)}, u32[]{:S(2)}) collective-permute-start(f32[64,1024]{1,0:T(8,128)} %get-tuple-element.215), channel_id=1, source_target_pairs={{84,101}} | collective-permute-start | bytes 786440 | tf_op jit(solution)/shard_map/ppermute | solution.py:40
  131.0 1.4 collective-permute-start.34
  132.4 2.8 %collective-permute-start.35 = (f32[64,1024]{1,0:T(8,128)}, f32[64,1024]{1,0:T(8,128)}, u32[]{:S(2)}, u32[]{:S(2)}) collective-permute-start(f32[64,1024]{1,0:T(8,128)} %get-tuple-element.216), channel_id=1, source_target_pairs={{117,118}} | collective-permute-start | bytes 786440 | tf_op jit(solution)/shard_map/ppermute | solution.py:40
  133.8 1.4 collective-permute-start.36
  135.2 112.2 %copy-start.1 = (f32[1,2,8,128,128]{4,3,2,1,0:T(8,128)S(1)}, f32[1,2,8,128,128]{4,3,2,1,0:T(8,128)}, u32[]{:S(2)}) copy-start(f32[1,2,8,128,128]{4,3,2,1,0:T(8,128)} %param.29) | copy-start | bytes 3145732
  135.2 112.2 %copy-start.3 = (f32[2,64,1024]{2,1,0:T(8,128)S(1)}, f32[2,64,1024]{2,1,0:T(8,128)}, u32[]{:S(2)}) copy-start(f32[2,64,1024]{2,1,0:T(8,128)} %copy-done.2) | copy-start | bytes 1572868
  135.2 112.2 %copy-start.4 = (s32[1,2,8]{2,1,0:T(2,128)S(1)}, s32[1,2,8]{2,1,0:T(2,128)}, u32[]{:S(2)}) copy-start(s32[1,2,8]{2,1,0:T(2,128)} %param.28) | copy-start | bytes 196
  135.2 112.2 %copy-start.5 = (s32[1,2]{1,0:T(1,128)S(1)}, s32[1,2]{1,0:T(1,128)}, u32[]{:S(2)}) copy-start(s32[1,2]{1,0:T(1,128)} %param.27) | copy-start | bytes 28
  135.3 11.2 %all-to-all-start.2 = ((f32[16,8,512]{2,1,0:T(8,128)}), f32[16,8,512]{2,1,0:T(8,128)S(1)}, u32[]{:S(2)}, u32[]{:S(2)}) async-start(f32[16,8,512]{2,1,0:T(8,128)} %bitcast.24), calls=%async_computation.2 | async-start | bytes 524288 | tf_op jit(solution)/shard_map/all_to_all | solution.py:28

commit v4 on v3

--- a/solution.py
+++ b/solution.py
@@ -47,23 +47,24 @@
 
 
 ACROSS = (((1,), (1,)), ((), ()))
-
-
-def high_passes(left, right_high):
+ALONG = (((1,), (0,)), ((), ()))
+
+
+def high_passes(left, right_high, dims):
     left_high, left_low = split_bf16(left)
     rows = left.shape[0]
     both = lax.dot_general(
-        jnp.concatenate([left_high, left_low], axis=0), right_high, ACROSS, preferred_element_type=jnp.float32
+        jnp.concatenate([left_high, left_low], axis=0), right_high, dims, preferred_element_type=jnp.float32
     )
     return both[:rows] + both[rows:]
 
 
-def low_pass(left, right_low):
-    return lax.dot_general(left.astype(jnp.bfloat16), right_low, ACROSS, preferred_element_type=jnp.float32)
-
-
-def three_pass(left, right_high, right_low):
-    return high_passes(left, right_high) + low_pass(left, right_low)
+def low_pass(left, right_low, dims):
+    return lax.dot_general(left.astype(jnp.bfloat16), right_low, dims, preferred_element_type=jnp.float32)
+
+
+def three_pass(left, right_high, right_low, dims=ACROSS):
+    return high_passes(left, right_high, dims) + low_pass(left, right_low, dims)
 
 
 VMEM = pl.BlockSpec(memory_space=pltpu.VMEM)
@@ -132,7 +133,7 @@
         total = one(inverse_high, block_high_ref[...])
         total = total + one(inverse_high, block_low_ref[...])
         total = total + one(inverse_low, block_high_ref[...])
-        high_ref[span, :], low_ref[span, :] = split_bf16(total)
+        high_ref[:, span], low_ref[:, span] = split_bf16(total.T)
 
 
 def form(inverse, block):
@@ -183,53 +184,48 @@
     )(rhs, past, in_hbm(inverse))
 
 
-def fire(bases, knowns, high, low):
-    count = len(bases)
-
-    def kernel(*refs):
-        base_refs, known_refs = refs[:count], refs[count:-5]
-        high_ref, low_hbm, out_ref, low_buffer, sem = refs[-5:]
-        copy = pltpu.make_async_copy(low_hbm, low_buffer, sem)
-        copy.start()
-        total = base_refs[0][...]
-        for ref in base_refs[1:]:
-            total = total + ref[...]
-        known = known_refs[0][...]
-        for ref in known_refs[1:]:
-            known = known + ref[...]
-        total = total - high_passes(known, high_ref[...])
-        copy.wait()
-        out_ref[...] = total - low_pass(known, low_buffer[...])
-
+def fire(step, where, before, total, extra, knowns, high, low):
+    def kernel(where_ref, before_ref, total_ref, *refs):
+        row, col = where_ref[0], where_ref[1]
+        turn = jnp.logical_and(col == step, row > step)
+        known_refs = refs[: len(knowns)]
+        extra_refs = refs[len(knowns) : -4]
+        high_ref, low_ref, out_ref, sum_ref = refs[-4:]
+        if extra_refs:
+            sum_ref[...] = total_ref[...] + extra_refs[0][...]
+        else:
+            sum_ref[...] = jnp.where(row == col + 1, total_ref[...], 0.0)
+
+        @pl.when(jnp.logical_not(turn))
+        def _():
+            out_ref[...] = before_ref[...]
+
+        @pl.when(turn)
+        def _():
+            known = known_refs[0][...]
+            for ref in known_refs[1:]:
+                known = known + ref[...]
+            out_ref[...] = sum_ref[...] - three_pass(known, high_ref[...], low_ref[...], ALONG)
+
+    extras = [] if extra is None else [extra]
+    like = jax.ShapeDtypeStruct(before.shape, jnp.float32)
     return pl.pallas_call(
         kernel,
-        in_specs=[VMEM] * (count + len(knowns) + 1) + [pl.BlockSpec(memory_space=pltpu.HBM)],
-        out_specs=VMEM,
-        out_shape=jax.ShapeDtypeStruct(knowns[0].shape, jnp.float32),
-        scratch_shapes=[pltpu.VMEM(low.shape, low.dtype), pltpu.SemaphoreType.DMA],
-        compiler_params=room(10),
-    )(*bases, *knowns, high, in_hbm(low))
-
-
-def finish_kernel(tiles_ref, near_ref, row_ref, pieces_ref, *refs):
-    rhs_refs, (force_ref, solution_ref, residual_ref) = refs[:-3], refs[-3:]
+        in_specs=[SMEM] + [VMEM] * (len(knowns) + len(extras) + 4),
+        out_specs=(VMEM, VMEM),
+        out_shape=(like, like),
+        compiler_params=room(3),
+    )(where, before, total, *knowns, *extras, high, low)
+
+
+def finish_kernel(tiles_ref, near_ref, row_ref, pieces_ref, rhs_ref, force_ref, solution_ref, residual_ref):
     row = row_ref[0]
     for group in range(8):
         for half in range(2):
             solution_ref[pl.ds(group * 8, 8), pl.ds(half * 512, 512)] = pieces_ref[row * COLS + group * 2 + half]
     for t in range(2):
         own = tiles_ref[t]
-        own_row = own // 8
-        behind = (row // 2 - own_row // 2 + 4) % 4
-        core = (row + own_row) % 2
-        for distance in range(4):
-
-            @pl.when(behind == distance)
-            def _():
-                offset = pl.multiple_of((own % 8) * 128, 128)
-                residual_ref[t] = rhs_refs[distance][core, :, pl.ds(offset, 128)]
-
-        total = residual_ref[t]
+        total = rhs_ref[own // 8, :, pl.ds(pl.multiple_of((own % 8) * 128, 128), 128)]
         for n in range(8):
             tile = near_ref[t, n]
             block = tile // 8
@@ -249,10 +245,10 @@
             jax.ShapeDtypeStruct((64, 1024), jnp.float32),
             jax.ShapeDtypeStruct((2, 64, 128), jnp.float32),
         ),
-        in_specs=[SMEM, SMEM, SMEM] + [VMEM] * (2 + len(rhs)),
+        in_specs=[SMEM, SMEM, SMEM] + [VMEM] * 3,
         out_specs=(VMEM, VMEM),
         compiler_params=room(8),
-    )(tile_list, neighbor_list, row, pieces, *rhs, force)
+    )(tile_list, neighbor_list, row, pieces, rhs, force)
 
 
 def per_device(
@@ -268,36 +264,20 @@
     row = lax.axis_index(PROW)
     col = lax.axis_index(PCOL)
     block = window_panel.reshape(-1, 128)
+    where = jnp.stack([row, col]).astype(jnp.int32)
     inverse = diag_inverse[0]
 
-    other_rhs = lax.ppermute(window_rhs, "prow_1", [(0, 1), (1, 0)])
-    pair = jnp.stack([window_rhs, other_rhs])
-
-    def around(x, distance):
-        return lax.ppermute(x, "prow_0", [(i, (i + distance) % 4) for i in range(4)])
-
-    next_rhs = around(pair, 1)
+    full_rhs = lax.all_gather(window_rhs, PROW, axis=0, tiled=False)
     past = product(past_solution, past_panel, 1, 1)
-    past, pair, next_rhs = lax.optimization_barrier((past, pair, next_rhs))
-    last_rhs = around(pair, 3)
     past_rows = exchange(past.reshape(COLS, 4, 1024), PCOL).sum(axis=0)
-    high, low = form(inverse, block)
-    high = in_vmem(high)
-    past_rows, pair, last_rhs, high = lax.optimization_barrier((past_rows, pair, last_rhs, high))
-    far_rhs = around(pair, 2)
+    high, low = (in_vmem(x) for x in form(inverse, block))
+    past_rows, high = lax.optimization_barrier((past_rows, high))
     rhs_rows = lax.dynamic_slice_in_dim(window_rhs, col * 4, 4, 0)
     start_rows = start_product(rhs_rows, past_rows, inverse)
     start = to_everyone(start_rows, PCOL, COLS).reshape(64, 1024)
-    start, far_rhs = lax.optimization_barrier((start, far_rhs))
-    full_rhs = [pair, next_rhs, far_rhs, last_rhs]
-
-    total = jnp.where(row == col + 1, start, jnp.zeros_like(start))
+
     arrived = send(start, [(place(0, k - 1), place(k, 0)) for k in range(1, ROWS)])
-    current = lax.cond(
-        (col == 0) & (row > 0),
-        lambda: fire([total], [arrived], high, low),
-        lambda: start,
-    )
+    current, total = fire(0, where, start, start, None, [arrived], high, low)
     for step in range(1, ROWS - 1):
         source = place(step, step - 1)
         beside = place(step ^ 1, step - 1)
@@ -306,19 +286,14 @@
             relayed = send(current, [(source, beside)])
             knowns += [send(relayed, [(beside, place(k, step))]) for k in range(step + 2, ROWS)]
         extra = send(current, [(place(k, step - 1), place(k, k - 1)) for k in range(step + 1, ROWS)])
-        current = lax.cond(
-            (col == step) & (row > step),
-            lambda: fire([total, extra], knowns, high, low),
-            lambda: current,
-        )
-        total = total + extra
+        current, total = fire(step, where, current, total, extra, knowns, high, low)
 
     pieces = current.reshape(8, 8, 2, 512).transpose(0, 2, 1, 3).reshape(COLS, 8, 512)
     spread = exchange(pieces, PCOL)
     own_piece = lax.dynamic_index_in_dim(spread, jnp.maximum(row - 1, 0), 0, keepdims=False)
     everything = to_everyone(own_piece, EVERY, ROWS * COLS)
     solution, residual = finish(
-        tile_list[0], neighbor_list[0], row.reshape(1), everything, full_rhs, force_constants[0]
+        tile_list[0], neighbor_list[0], where, everything, full_rhs, force_constants[0]
     )
     return (solution, residual[None])
 

time: 251 us -> 218 us (0.87)
  blocking collectives: 115 us -> 14 us
  starting transfers between devices: 77.8 us -> 104 us
  waiting for transfers between devices: 17.8 us -> 42.5 us
  between operations: 0.98 us -> 14.7 us
  local copies, waits for them, and re-layouts: 2.92 us -> 11.7 us
  other arithmetic: 5.51 us -> 0.14 us
    all_to_all x2 -> x1, blocking collectives: 115 us -> 14 us  [exchange(): return lax.all_to_all(pieces, axes, 0, 0, tiled=True)]
    all_to_all x2 -> x3, starting transfers between devices: 10.4 us -> 79.6 us  [exchange(): return lax.all_to_all(pieces, axes, 0, 0, tiled=True)]
    all_to_all x2 -> x3, waiting for transfers between devices: 7.5 us -> 37.2 us  [exchange(): return lax.all_to_all(pieces, axes, 0, 0, tiled=True)]
    ppermute x33, starting transfers between devices: 46.9 us -> 24.2 us  [send(): return lax.ppermute(x, EVERY, pairs)]
    ppermute x4 -> x0, starting transfers between devices: 20.5 us -> none  [the longest x3 19 us: around(): lax.ppermute(x, 'prow_0', [(i, (i + distance) % 4) for i in range(4)])]
    unnamed x16, local copies, waits for them, and re-layouts: 0.04 us -> 8.38 us
    ppermute x4 -> x0, waiting for transfers between devices: 8.18 us -> none  [the longest x3 6.81 us: around(): lax.ppermute(x, 'prow_0', [(i, (i + distance) % 4) for i in range(4)])]
    add x2 -> x0, other arithmetic: 3.73 us -> none  [per_device(): total = total + extra]
  transfers between devices with their start and end apart: 39 -> 37, of which waited for: 5 -> 4; matrix products, arithmetic and copies ran while one was open for 6% -> 1% of each run, Pallas kernels for 6% -> 6%
where the time goes in v4:
time: 218 us; the launch traced here: 216 us
  starting transfers between devices  104 us (48%)
  waiting for transfers between devices  42.5 us (19%)
  Pallas kernels  22.1 us (10%)
  between operations  14.7 us (7%)
  blocking collectives  14 us (6%)
  local copies, waits for them, and re-layouts  11.7 us (5%)
  matrix products  7.31 us (3%)
    all_to_all x3, starting transfers between devices, exchange(): return lax.all_to_all(pieces, axes, 0, 0, tiled=True)  79.6 us
    all_to_all x3, waiting for transfers between devices, exchange(): return lax.all_to_all(pieces, axes, 0, 0, tiled=True)  37.2 us
    ppermute x33, starting transfers between devices, send(): return lax.ppermute(x, EVERY, pairs)  24.2 us
    all_to_all x1, blocking collectives, exchange(): return lax.all_to_all(pieces, axes, 0, 0, tiled=True)  14 us
    pallas_call x1, Pallas kernels, form(): pl.pallas_call(form_kernel, in_specs=[hbm, hbm], out_specs=(VMEM,) * 2, o...  11.4 us
    unnamed x16, local copies, waits for them, and re-layouts  8.38 us
    dot_general x1, matrix products, product(): lax.dot_general(left, right, (((left_dim,), (right_dim,)), ((), ())), pre...  7.31 us
    pallas_call x7, Pallas kernels, fire(): pl.pallas_call(kernel, in_specs=[SMEM] + [VMEM] * (len(knowns) + len(extr...  5.93 us
  transfers between devices with their start and end apart: 37, of which 4 were waited for; matrix products, arithmetic and copies ran while one was open for 1% of the time, Pallas kernels for 6%

profile of v4, /device:TPU:1, one launch (start us, length us, event | category | flops | bytes accessed | tf_op | source)
XLA Modules:
  0.0 216.5 jit_solution(13972988859727192157)
XLA Ops:
  7.2 1.0 copy-done
  8.2 7.3 %fusion = f32[64,1024]{1,0:T(8,128)S(1)} fusion(f32[64,2048]{1,0:T(8,128)S(1)} %copy-done, f32[1024,2048]{1,0:T(8,128)} %param.10), kind=kOutput, calls=%fused_computation.3 | convolution fusion | flops 805306368 | bytes 9175040 | tf_op jit(solution)/shard_map/dot_general | solution.py:18
  15.5 0.8 reshape.20
  16.3 7.6 %all-to-all-start = ((f32[16,4,1024]{2,1,0:T(4,128)}), f32[16,4,1024]{2,1,0:T(4,128)S(1)}, u32[]{:S(2)}, u32[]{:S(2)}) async-start(f32[16,4,1024]{2,1,0:T(4,128)} %reshape.20), calls=%async_computation | async-start | bytes 524288 | tf_op jit(solution)/shard_map/all_to_all | solution.py:28
  23.9 0.2 all-gather.3.cloned.1.call-start
  24.1 11.4 %shard_map.95 = (bf16[1024,1024]{1,0:T(8,128)(2,1)S(1)}, bf16[1024,1024]{1,0:T(8,128)(2,1)S(1)}) custom-call(f32[1024,1024]{1,0:T(8,128)} %bitcast.22, f32[8192,128]{1,0:T(8,128)} %bitcast.24), custom_call_target="tpu_custom_call" | custom-call | tf_op jit(solution)/shard_map/pallas_call | solution.py:143
  35.5 1.3 copy-done.1
  36.9 0.8 constant_dynamic-slice_fusion.rhs_ref
  37.7 2.8 %shard_map.96 = f32[4,1024]{1,0:T(4,128)S(1)} custom-call(f32[4,1024]{1,0:T(4,128)S(1)} %constant_dynamic-slice_fusion.rhs_ref, f32[4,1024]{1,0:T(4,128)S(1)} %reduce_sum.9.past_ref, f32[1024,1024]{1,0:T(8,128)} %bitcast.23), custom_call_target="tpu_custom_call" | custom-call | tf_op jit(solution)/shard_map/pallas_call | solution.py:177
  40.6 14.0 %all_to_all.20 = f32[16,4,1024]{2,1,0:T(4,128)S(1)} all-to-all(f32[16,4,1024]{2,1,0:T(4,128)S(1)} %broadcast_in_dim.8), channel_id=1, replica_groups=mesh['prow_0'=4,'prow_1'=2,'pcol_0'=4,'pcol_1'=4] {'pcol_0','pcol_1'}, dimensions={0} | all-to-all | bytes 524288 | tf_op jit(solution)/shard_map/all_to_all | solution.py:28
  54.6 0.1 reshape.22.before_ref.total_ref
  54.7 1.3 collective-permute-start
  56.0 0.1 pad_add_fusion.where_ref.row_ref
  56.1 3.6 %collective-permute-done.refs_0_ = f32[64,1024]{1,0:T(8,128)S(1)} collective-permute-done((f32[64,1024]{1,0:T(8,128)S(1)}, f32[64,1024]{1,0:T(8,128)S(1)}, u32[]{:S(2)}, u32[]{:S(2)}) %collective-permute-start) | collective-permute-done | bytes 262176 | tf_op jit(solution)/shard_map/ppermute | solution.py:40
  59.6 1.6 copy-done.2
  61.2 1.4 shard_map.97
  62.6 1.3 collective-permute-start.2
  63.9 1.3 collective-permute-start.1
  65.2 0.7 collective-permute-start.8
  65.9 0.7 collective-permute-start.3
  66.6 0.7 collective-permute-start.4
  67.3 0.7 collective-permute-start.5
  68.0 1.6 collective-permute-done.1.refs_0_
  69.6 0.7 collective-permute-start.6
  70.3 0.7 collective-permute-start.7
  71.0 0.6 shard_map.98
  71.6 0.7 collective-permute-start.10
  72.3 0.7 collective-permute-start.15
  73.0 0.7 collective-permute-start.9
  73.7 0.7 collective-permute-start.11
  74.4 0.7 collective-permute-start.12
  75.0 0.7 collective-permute-start.13
  75.7 0.7 collective-permute-start.14
  76.5 0.8 shard_map.99
  77.3 0.7 collective-permute-start.17
  78.0 0.7 collective-permute-start.16
  78.7 0.7 collective-permute-start.21
  79.4 0.7 collective-permute-start.18
  80.0 0.7 collective-permute-start.19
  80.7 0.7 collective-permute-start.20
  81.5 0.6 shard_map.100
  82.1 0.7 collective-permute-start.23
  82.8 0.7 collective-permute-start.22
  83.5 0.7 collective-permute-start.26
  84.2 0.7 collective-permute-start.24
  84.8 0.7 collective-permute-start.25
  85.6 1.6 copy-done.3
  87.2 0.6 shard_map.101
  87.8 0.7 collective-permute-start.28
  88.4 0.7 collective-permute-start.27
  89.1 0.7 collective-permute-start.30
  89.8 0.7 collective-permute-start.29
  90.5 0.6 shard_map.102
  91.1 0.7 collective-permute-start.31
  91.8 0.7 collective-permute-start.32
  92.5 1.4 shard_map.103
  93.9 3.7 %all-to-all-start.2 = ((f32[16,8,512]{2,1,0:T(8,128)}), f32[16,8,512]{2,1,0:T(8,128)S(1)}, u32[]{:S(2)}, u32[]{:S(2)}) async-start(f32[16,8,512]{2,1,0:T(8,128)} %bitcast.8), calls=%async_computation.2 | async-start | bytes 524288 | tf_op jit(solution)/shard_map/all_to_all | solution.py:28
  97.6 7.5 %all-to-all-done.2 = f32[16,8,512]{2,1,0:T(8,128)S(1)} async-done(((f32[16,8,512]{2,1,0:T(8,128)}), f32[16,8,512]{2,1,0:T(8,128)S(1)}, u32[]{:S(2)}, u32[]{:S(2)}) %all-to-all-start.2) | async-done | bytes 262176 | tf_op jit(solution)/shard_map/all_to_all | solution.py:28
  105.1 1.6 broadcast_in_dim.19
  106.7 68.4 %all-to-all-start.3 = ((f32[128,8,512]{2,1,0:T(8,128)}), f32[128,8,512]{2,1,0:T(8,128)S(1)}, u32[]{:S(2)}, u32[]{:S(2)}) async-start(f32[128,8,512]{2,1,0:T(8,128)} %broadcast_in_dim.19), calls=%async_computation.3 | async-start | bytes 4194304 | tf_op jit(solution)/shard_map/all_to_all | solution.py:28
  175.2 29.7 %all-to-all-done.3.pieces_ref = f32[128,8,512]{2,1,0:T(8,128)S(1)} async-done(((f32[128,8,512]{2,1,0:T(8,128)}), f32[128,8,512]{2,1,0:T(8,128)S(1)}, u32[]{:S(2)}, u32[]{:S(2)}) %all-to-all-start.3) | async-done | bytes 2097184 | tf_op jit(solution)/shard_map/all_to_all | solution.py:28
  204.8 1.6 copy-done.4
  206.4 1.2 copy-done.5
  207.7 2.0 shard_map.104
  (47 shorter events, 0.2 us)
Async XLA Ops:
  7.2 1.0 copy-start
  16.3 21.3 %all-to-all-start = ((f32[16,4,1024]{2,1,0:T(4,128)}), f32[16,4,1024]{2,1,0:T(4,128)S(1)}, u32[]{:S(2)}, u32[]{:S(2)}) async-start(f32[16,4,1024]{2,1,0:T(4,128)} %reshape.20), calls=%async_computation | async-start | bytes 524288 | tf_op jit(solution)/shard_map/all_to_all | solution.py:28
  23.9 151.3 %all-gather.3.cloned.1.call-start = ((), (), s32[]{:S(2)}) async-start(), calls=%async_computation.4 | async-start | bytes 2359296 | tf_op jit(solution)/shard_map/all_gather | solution.py:270
  35.5 1.4 copy-start.1
  54.7 5.0 %collective-permute-start = (f32[64,1024]{1,0:T(8,128)S(1)}, f32[64,1024]{1,0:T(8,128)S(1)}, u32[]{:S(2)}, u32[]{:S(2)}) collective-permute-start(f32[64,1024]{1,0:T(8,128)S(1)} %reshape.22.before_ref.total_ref), channel_id=1, source_target_pairs={{0,16},{1,32},{2,48},{3,64},{4,80},{5,96},{6,112}} | collective-permute-start | bytes 786440 | tf_op jit(solution)/shard_map/ppermute | solution.py:40
  59.6 1.6 copy-start.2
  62.6 3.3 %collective-permute-start.2 = (f32[64,1024]{1,0:T(8,128)S(1)}, f32[64,1024]{1,0:T(8,128)S(1)}, u32[]{:S(2)}, u32[]{:S(2)}) collective-permute-start(f32[64,1024]{1,0:T(8,128)S(1)} %get-tuple-element.25.before_ref), channel_id=1, source_target_pairs={{16,0}} | collective-permute-start | bytes 786440 | tf_op jit(solution)/shard_map/ppermute | solution.py:40
  63.9 5.7 %collective-permute-start.1 = (f32[64,1024]{1,0:T(8,128)S(1)}, f32[64,1024]{1,0:T(8,128)S(1)}, u32[]{:S(2)}, u32[]{:S(2)}) collective-permute-start(f32[64,1024]{1,0:T(8,128)S(1)} %get-tuple-element.25.before_ref), channel_id=1, source_target_pairs={{16,33}} | collective-permute-start | bytes 786440 | tf_op jit(solution)/shard_map/ppermute | solution.py:40
  65.2 5.0 %collective-permute-start.8 = (f32[64,1024]{1,0:T(8,128)S(1)}, f32[64,1024]{1,0:T(8,128)S(1)}, u32[]{:S(2)}, u32[]{:S(2)}) collective-permute-start(f32[64,1024]{1,0:T(8,128)S(1)} %get-tuple-element.25.before_ref), channel_id=1, source_target_pairs={{32,33},{48,50},{64,67},{80,84},{96,101},{112,118}} | collective-permute-start | bytes 786440 | tf_op jit(solution)/shard_map/ppermute | solution.py:40
  65.9 5.0 %collective-permute-start.3 = (f32[64,1024]{1,0:T(8,128)S(1)}, f32[64,1024]{1,0:T(8,128)S(1)}, u32[]{:S(2)}, u32[]{:S(2)}) collective-permute-start(f32[64,1024]{1,0:T(8,128)S(1)} %collective-permute-done.2), channel_id=1, source_target_pairs={{0,49}} | collective-permute-start | bytes 786440 | tf_op jit(solution)/shard_map/ppermute | solution.py:40
  66.6 4.4 %collective-permute-start.4 = (f32[64,1024]{1,0:T(8,128)S(1)}, f32[64,1024]{1,0:T(8,128)S(1)}, u32[]{:S(2)}, u32[]{:S(2)}) collective-permute-start(f32[64,1024]{1,0:T(8,128)S(1)} %collective-permute-done.2), channel_id=1, source_target_pairs={{0,65}} | collective-permute-start | bytes 786440 | tf_op jit(solution)/shard_map/ppermute | solution.py:40
  67.3 3.7 %collective-permute-start.5 = (f32[64,1024]{1,0:T(8,128)S(1)}, f32[64,1024]{1,0:T(8,128)S(1)}, u32[]{:S(2)}, u32[]{:S(2)}) collective-permute-start(f32[64,1024]{1,0:T(8,128)S(1)} %collective-permute-done.2), channel_id=1, source_target_pairs={{0,81}} | collective-permute-start | bytes 786440 | tf_op jit(solution)/shard_map/ppermute | solution.py:40
  69.6 1.4 collective-permute-start.6
  70.3 0.7 collective-permute-start.7
  71.6 2.1 collective-permute-start.10
  72.3 3.4 %collective-permute-start.15 = (f32[64,1024]{1,0:T(8,128)S(1)}, f32[64,1024]{1,0:T(8,128)S(1)}, u32[]{:S(2)}, u32[]{:S(2)}) collective-permute-start(f32[64,1024]{1,0:T(8,128)S(1)} %get-tuple-element.27.before_ref), channel_id=1, source_target_pairs={{49,50},{65,67},{81,84},{97,101},{113,118}} | collective-permute-start | bytes 786440 | tf_op jit(solution)/shard_map/ppermute | solution.py:40
  73.0 3.5 %collective-permute-start.9 = (f32[64,1024]{1,0:T(8,128)S(1)}, f32[64,1024]{1,0:T(8,128)S(1)}, u32[]{:S(2)}, u32[]{:S(2)}) collective-permute-start(f32[64,1024]{1,0:T(8,128)S(1)} %get-tuple-element.27.before_ref), channel_id=1, source_target_pairs={{33,50}} | collective-permute-start | bytes 786440 | tf_op jit(solution)/shard_map/ppermute | solution.py:40
  73.7 2.8 %collective-permute-start.11 = (f32[64,1024]{1,0:T(8,128)S(1)}, f32[64,1024]{1,0:T(8,128)S(1)}, u32[]{:S(2)}, u32[]{:S(2)}) collective-permute-start(f32[64,1024]{1,0:T(8,128)S(1)} %collective-permute-done.10), channel_id=1, source_target_pairs={{49,66}} | collective-permute-start | bytes 786440 | tf_op jit(solution)/shard_map/ppermute | solution.py:40
  74.4 2.1 collective-permute-start.12
  75.0 1.4 collective-permute-start.13
  75.7 0.7 collective-permute-start.14
  77.3 2.1 collective-permute-start.17
  78.0 3.4 %collective-permute-start.16 = (f32[64,1024]{1,0:T(8,128)S(1)}, f32[64,1024]{1,0:T(8,128)S(1)}, u32[]{:S(2)}, u32[]{:S(2)}) collective-permute-start(f32[64,1024]{1,0:T(8,128)S(1)} %get-tuple-element.29.before_ref), channel_id=1, source_target_pairs={{50,67}} | collective-permute-start | bytes 786440 | tf_op jit(solution)/shard_map/ppermute | solution.py:40
  78.7 2.8 %collective-permute-start.21 = (f32[64,1024]{1,0:T(8,128)S(1)}, f32[64,1024]{1,0:T(8,128)S(1)}, u32[]{:S(2)}, u32[]{:S(2)}) collective-permute-start(f32[64,1024]{1,0:T(8,128)S(1)} %get-tuple-element.29.before_ref), channel_id=1, source_target_pairs={{66,67},{82,84},{98,101},{114,118}} | collective-permute-start | bytes 786440 | tf_op jit(solution)/shard_map/ppermute | solution.py:40
  79.4 2.1 collective-permute-start.18
  80.0 1.4 collective-permute-start.19
  80.7 0.7 collective-permute-start.20
  82.1 2.1 collective-permute-start.23
  82.8 2.8 %collective-permute-start.22 = (f32[64,1024]{1,0:T(8,128)S(1)}, f32[64,1024]{1,0:T(8,128)S(1)}, u32[]{:S(2)}, u32[]{:S(2)}) collective-permute-start(f32[64,1024]{1,0:T(8,128)S(1)} %get-tuple-element.31.before_ref), channel_id=1, source_target_pairs={{67,84}} | collective-permute-start | bytes 786440 | tf_op jit(solution)/shard_map/ppermute | solution.py:40
  83.5 2.1 collective-permute-start.26
  84.2 1.4 collective-permute-start.24
  84.8 0.7 collective-permute-start.25
  85.6 1.6 copy-start.3
  87.8 2.1 collective-permute-start.28
  88.4 2.1 collective-permute-start.27
  89.1 1.4 collective-permute-start.30
  89.8 0.7 collective-permute-start.29
  91.1 1.4 collective-permute-start.31
  91.8 0.7 collective-permute-start.32
  93.9 110.9 %copy-start.6 = (s32[1,2,8]{2,1,0:T(2,128)S(1)}, s32[1,2,8]{2,1,0:T(2,128)}, u32[]{:S(2)}) copy-start(s32[1,2,8]{2,1,0:T(2,128)} %param.14) | copy-start | bytes 196
  93.9 110.9 %copy-start.7 = (s32[1,2]{1,0:T(1,128)S(1)}, s32[1,2]{1,0:T(1,128)}, u32[]{:S(2)}) copy-start(s32[1,2]{1,0:T(1,128)} %param.13) | copy-start | bytes 28
  93.9 11.2 %all-to-all-start.2 = ((f32[16,8,512]{2,1,0:T(8,128)}), f32[16,8,512]{2,1,0:T(8,128)S(1)}, u32[]{:S(2)}, u32[]{:S(2)}) async-start(f32[16,8,512]{2,1,0:T(8,128)} %bitcast.8), calls=%async_computation.2 | async-start | bytes 524288 | tf_op jit(solution)/shard_map/all_to_all | solution.py:28
  106.7 98.1 %all-to-all-start.3 = ((f32[128,8,512]{2,1,0:T(8,128)}), f32[128,8,512]{2,1,0:T(8,128)S(1)}, u32[]{:S(2)}, u32[]{:S(2)}) async-start(f32[128,8,512]{2,1,0:T(8,128)} %broadcast_in_dim.19), calls=%async_computation.3 | async-start | bytes 4194304 | tf_op jit(solution)/shard_map/all_to_all | solution.py:28
  204.8 1.6 copy-start.4
  206.4 1.2 copy-start.5
Sparse Core Ops, SparseCore 0:
  82.9 57.6 all-gather.2

commit v5 on v4

--- a/solution.py
+++ b/solution.py
@@ -184,7 +184,7 @@
     )(rhs, past, in_hbm(inverse))
 
 
-def fire(step, where, before, total, extra, knowns, high, low):
+def fire(step, where, before, total, extras, knowns, high, low):
     def kernel(where_ref, before_ref, total_ref, *refs):
         row, col = where_ref[0], where_ref[1]
         turn = jnp.logical_and(col == step, row > step)
@@ -192,7 +192,10 @@
         extra_refs = refs[len(knowns) : -4]
         high_ref, low_ref, out_ref, sum_ref = refs[-4:]
         if extra_refs:
-            sum_ref[...] = total_ref[...] + extra_refs[0][...]
+            total = total_ref[...]
+            for ref in extra_refs:
+                total = total + ref[...]
+            sum_ref[...] = total
         else:
             sum_ref[...] = jnp.where(row == col + 1, total_ref[...], 0.0)
 
@@ -200,14 +203,21 @@
         def _():
             out_ref[...] = before_ref[...]
 
-        @pl.when(turn)
+        @pl.when(jnp.logical_and(turn, row == step + 1))
+        def _():
+            out_ref[...] = known_refs[0][...]
+
+        @pl.when(jnp.logical_and(turn, row > step + 1))
         def _():
             known = known_refs[0][...]
             for ref in known_refs[1:]:
                 known = known + ref[...]
-            out_ref[...] = sum_ref[...] - three_pass(known, high_ref[...], low_ref[...], ALONG)
-
-    extras = [] if extra is None else [extra]
+            out_ref[...] = known
+
+        @pl.when(turn)
+        def _():
+            out_ref[...] = sum_ref[...] - three_pass(out_ref[...], high_ref[...], low_ref[...], ALONG)
+
     like = jax.ShapeDtypeStruct(before.shape, jnp.float32)
     return pl.pallas_call(
         kernel,
@@ -218,14 +228,40 @@
     )(where, before, total, *knowns, *extras, high, low)
 
 
-def finish_kernel(tiles_ref, near_ref, row_ref, pieces_ref, rhs_ref, force_ref, solution_ref, residual_ref):
+def assemble_kernel(pieces_ref, out_ref):
+    for i in range(COLS):
+        out_ref[pl.ds(i * 4, 4), :] = pieces_ref[i]
+
+
+def assemble(pieces):
+    return pl.pallas_call(
+        assemble_kernel,
+        in_specs=[VMEM],
+        out_specs=VMEM,
+        out_shape=jax.ShapeDtypeStruct((64, 1024), jnp.float32),
+        compiler_params=room(2),
+    )(pieces)
+
+
+def finish_kernel(tiles_ref, near_ref, row_ref, pieces_ref, *refs):
+    rhs_refs, (force_ref, solution_ref, residual_ref) = refs[:4], refs[4:]
     row = row_ref[0]
     for group in range(8):
         for half in range(2):
             solution_ref[pl.ds(group * 8, 8), pl.ds(half * 512, 512)] = pieces_ref[row * COLS + group * 2 + half]
     for t in range(2):
         own = tiles_ref[t]
-        total = rhs_ref[own // 8, :, pl.ds(pl.multiple_of((own % 8) * 128, 128), 128)]
+        own_row = own // 8
+        behind = (row // 2 - own_row // 2 + 4) % 4
+        core = (row + own_row) % 2
+        offset_own = pl.multiple_of((own % 8) * 128, 128)
+        for distance in range(4):
+
+            @pl.when(behind == distance)
+            def _(distance=distance):
+                residual_ref[t] = rhs_refs[distance][core, :, pl.ds(offset_own, 128)]
+
+        total = residual_ref[t]
         for n in range(8):
             tile = near_ref[t, n]
             block = tile // 8
@@ -245,10 +281,10 @@
             jax.ShapeDtypeStruct((64, 1024), jnp.float32),
             jax.ShapeDtypeStruct((2, 64, 128), jnp.float32),
         ),
-        in_specs=[SMEM, SMEM, SMEM] + [VMEM] * 3,
+        in_specs=[SMEM, SMEM, SMEM] + [VMEM] * 6,
         out_specs=(VMEM, VMEM),
         compiler_params=room(8),
-    )(tile_list, neighbor_list, row, pieces, rhs, force)
+    )(tile_list, neighbor_list, row, pieces, *rhs, force)
 
 
 def per_device(
@@ -267,17 +303,31 @@
     where = jnp.stack([row, col]).astype(jnp.int32)
     inverse = diag_inverse[0]
 
-    full_rhs = lax.all_gather(window_rhs, PROW, axis=0, tiled=False)
+    def onward(x):
+        return lax.ppermute(x, "prow_0", [(i, (i + 1) % 4) for i in range(4)])
+
+    other_rhs = lax.ppermute(window_rhs, "prow_1", [(0, 1), (1, 0)])
+    pair = jnp.stack([window_rhs, other_rhs])
+    next_rhs = onward(pair)
     past = product(past_solution, past_panel, 1, 1)
-    past_rows = exchange(past.reshape(COLS, 4, 1024), PCOL).sum(axis=0)
-    high, low = (in_vmem(x) for x in form(inverse, block))
-    past_rows, high = lax.optimization_barrier((past_rows, high))
+    past_rows = exchange(past.reshape(COLS, 4, 1024), PCOL)
+    _, next_rhs = lax.optimization_barrier((past, next_rhs))
+    far_rhs = onward(next_rhs)
+    high, low = form(inverse, block)
+    past_rows, high, far_rhs = lax.optimization_barrier((past_rows, high, far_rhs))
+    last_rhs = onward(far_rhs)
+    past_rows = past_rows.sum(axis=0)
     rhs_rows = lax.dynamic_slice_in_dim(window_rhs, col * 4, 4, 0)
     start_rows = start_product(rhs_rows, past_rows, inverse)
-    start = to_everyone(start_rows, PCOL, COLS).reshape(64, 1024)
-
-    arrived = send(start, [(place(0, k - 1), place(k, 0)) for k in range(1, ROWS)])
-    current, total = fire(0, where, start, start, None, [arrived], high, low)
+    start_rows = to_everyone(start_rows, PCOL, COLS)
+    start_rows, last_rhs = lax.optimization_barrier((start_rows, last_rhs))
+    full_rhs = [pair, next_rhs, far_rhs, last_rhs]
+    start = assemble(start_rows)
+
+    arrived = send(start, [(place(0, i), place(k, 0)) for i, k in ((0, 1), (1, 2), (3, 6), (4, 4))])
+    relayed = send(arrived, [(place(k, 0), place(k + 1, 0)) for k in (2, 4, 6)])
+    current, total = fire(0, where, start, start, [], [arrived, relayed], high, low)
+    late = []
     for step in range(1, ROWS - 1):
         source = place(step, step - 1)
         beside = place(step ^ 1, step - 1)
@@ -285,8 +335,11 @@
         if step + 2 < ROWS:
             relayed = send(current, [(source, beside)])
             knowns += [send(relayed, [(beside, place(k, step))]) for k in range(step + 2, ROWS)]
-        extra = send(current, [(place(k, step - 1), place(k, k - 1)) for k in range(step + 1, ROWS)])
-        current, total = fire(step, where, current, total, extra, knowns, high, low)
+        extras = late + [send(current, [(place(step + 1, step - 1), place(step + 1, step))])]
+        late = []
+        if step + 2 < ROWS:
+            late = [send(current, [(place(k, step - 1), place(k, k - 1)) for k in range(step + 2, ROWS)])]
+        current, total = fire(step, where, current, total, extras, knowns, high, low)
 
     pieces = current.reshape(8, 8, 2, 512).transpose(0, 2, 1, 3).reshape(COLS, 8, 512)
     spread = exchange(pieces, PCOL)

time: 218 us -> 273 us (1.25)
  blocking collectives: 14 us -> 72.4 us
  starting transfers between devices: 104 us -> 139 us
  waiting for transfers between devices: 42.5 us -> 20.7 us
  between operations: 14.7 us -> 1.34 us
  local copies, waits for them, and re-layouts: 11.7 us -> 5.49 us
    ppermute x33 -> x39, starting transfers between devices: 24.2 us -> 113 us  [send(): return lax.ppermute(x, EVERY, pairs)]
    all_to_all x3 -> x2, starting transfers between devices: 79.6 us -> 13.6 us  [exchange(): return lax.all_to_all(pieces, axes, 0, 0, tiled=True)]
    all_to_all x1 -> x2, blocking collectives: 14 us -> 72.4 us  [exchange(): return lax.all_to_all(pieces, axes, 0, 0, tiled=True)]
    all_to_all x3 -> x2, waiting for transfers between devices: 37.2 us -> 8.12 us  [exchange(): return lax.all_to_all(pieces, axes, 0, 0, tiled=True)]
    ppermute x0 -> x4, starting transfers between devices: none -> 12.6 us  [the longest x1 10.7 us: per_device(): other_rhs = lax.ppermute(window_rhs, 'prow_1', [(0, 1), (1, 0)])]
    ppermute x0 -> x4, waiting for transfers between devices: none -> 8.66 us  [the longest x3 6.49 us: onward(): return lax.ppermute(x, 'prow_0', [(i, (i + 1) % 4) for i in range(4)])]
    unnamed x16 -> x14, local copies, waits for them, and re-layouts: 8.38 us -> 3.65 us
  transfers between devices with their start and end apart: 37 -> 45, of which waited for: 4 -> 5; matrix products, arithmetic and copies ran while one was open for 1% -> 4% of each run, Pallas kernels for 6% -> 5%
where the time goes in v5:
time: 273 us; the launch traced here: 272 us
  starting transfers between devices  139 us (51%)
  blocking collectives  72.4 us (27%)
  Pallas kernels  23.5 us (9%)
  waiting for transfers between devices  20.7 us (8%)
  matrix products  7.31 us (3%)
  local copies, waits for them, and re-layouts  5.49 us (2%)
    ppermute x39, starting transfers between devices, send(): return lax.ppermute(x, EVERY, pairs)  113 us
    all_to_all x2, blocking collectives, exchange(): return lax.all_to_all(pieces, axes, 0, 0, tiled=True)  72.4 us
    all_to_all x2, starting transfers between devices, exchange(): return lax.all_to_all(pieces, axes, 0, 0, tiled=True)  13.6 us
    pallas_call x1, Pallas kernels, form(): pl.pallas_call(form_kernel, in_specs=[hbm, hbm], out_specs=(VMEM,) * 2, o...  11.4 us
    ppermute x1, starting transfers between devices, per_device(): other_rhs = lax.ppermute(window_rhs, 'prow_1', [(0, 1), (1, 0)])  10.7 us
    all_to_all x2, waiting for transfers between devices, exchange(): return lax.all_to_all(pieces, axes, 0, 0, tiled=True)  8.12 us
    dot_general x1, matrix products, product(): lax.dot_general(left, right, (((left_dim,), (right_dim,)), ((), ())), pre...  7.31 us
    ppermute x3, waiting for transfers between devices, onward(): return lax.ppermute(x, 'prow_0', [(i, (i + 1) % 4) for i in range(4)])  6.49 us
  transfers between devices with their start and end apart: 45, of which 5 were waited for; matrix products, arithmetic and copies ran while one was open for 4% of the time, Pallas kernels for 5%

profile of v5, /device:TPU:1, one launch (start us, length us, event | category | flops | bytes accessed | tf_op | source)
XLA Modules:
  0.0 271.6 jit_solution(6037154645172693721)
XLA Ops:
  0.6 10.7 %collective-permute-start = (f32[64,1024]{1,0:T(8,128)}, f32[64,1024]{1,0:T(8,128)S(1)}, u32[]{:S(2)}, u32[]{:S(2)}) collective-permute-start(f32[64,1024]{1,0:T(8,128)} %param.8), channel_id=1, source_target_pairs={{0,16},{16,0},{1,17},{17,1},{2,18},{18,2},{3,19},{19,3},{4,20},{20... | collective-permute-start | bytes 786440 | tf_op jit(solution)/shard_map/ppermute | solution.py:309
  11.4 2.2 collective-permute-done
  13.5 1.0 pad_maximum_fusion.refs_0_
  14.5 1.0 collective-permute-start.1
  15.5 7.3 %fusion = f32[64,1024]{1,0:T(8,128)S(1)} fusion(f32[64,2048]{1,0:T(8,128)S(1)} %copy-done, f32[1024,2048]{1,0:T(8,128)} %param.10), kind=kOutput, calls=%fused_computation.4 | convolution fusion | flops 805306368 | bytes 9175040 | tf_op jit(solution)/shard_map/dot_general | solution.py:18
  22.8 6.5 %collective-permute-done.1.refs_1_ = f32[2,64,1024]{2,1,0:T(8,128)} collective-permute-done((f32[2,64,1024]{2,1,0:T(8,128)S(1)}, f32[2,64,1024]{2,1,0:T(8,128)}, u32[]{:S(2)}, u32[]{:S(2)}) %collective-permute-start.1) | collective-permute-done | bytes 524320 | tf_op jit(solution)/shard_map/ppermute | solution.py:307
  29.3 0.8 reshape.17
  30.1 6.9 %all-to-all-start = ((f32[16,4,1024]{2,1,0:T(4,128)}), f32[16,4,1024]{2,1,0:T(4,128)}, u32[]{:S(2)}, u32[]{:S(2)}) async-start(f32[16,4,1024]{2,1,0:T(4,128)} %reshape.17), calls=%async_computation | async-start | bytes 524288 | tf_op jit(solution)/shard_map/all_to_all | solution.py:28
  37.0 11.4 %shard_map.95 = (bf16[1024,1024]{1,0:T(8,128)(2,1)S(1)}, bf16[1024,1024]{1,0:T(8,128)(2,1)S(1)}) custom-call(f32[1024,1024]{1,0:T(8,128)} %bitcast.23, f32[8192,128]{1,0:T(8,128)} %bitcast.25), custom_call_target="tpu_custom_call" | custom-call | tf_op jit(solution)/shard_map/pallas_call | solution.py:143
  48.4 1.3 copy-done.1
  49.8 0.9 collective-permute-start.3
  50.7 0.8 constant_dynamic-slice_fusion.rhs_ref
  51.4 1.0 reduce_sum.9.past_ref
  52.4 2.8 %shard_map.96 = f32[4,1024]{1,0:T(4,128)S(1)} custom-call(f32[4,1024]{1,0:T(4,128)S(1)} %constant_dynamic-slice_fusion.rhs_ref, f32[4,1024]{1,0:T(4,128)S(1)} %reduce_sum.9.past_ref, f32[1024,1024]{1,0:T(8,128)} %bitcast.24), custom_call_target="tpu_custom_call" | custom-call | tf_op jit(solution)/shard_map/pallas_call | solution.py:177
  55.3 13.9 %all_to_all.20.pieces_ref = f32[16,4,1024]{2,1,0:T(4,128)S(1)} all-to-all(f32[16,4,1024]{2,1,0:T(4,128)S(1)} %broadcast_in_dim.8), channel_id=1, replica_groups=mesh['prow_0'=4,'prow_1'=2,'pcol_0'=4,'pcol_1'=4] {'pcol_0','pcol_1'}, dimensions={0} | all-to-all | bytes 524288 | tf_op jit(solution)/shard_map/all_to_all | solution.py:28
  69.3 8.3 %collective-permute-start.4 = (f32[64,1024]{1,0:T(8,128)S(1)}, f32[64,1024]{1,0:T(8,128)}, u32[]{:S(2)}, u32[]{:S(2)}) collective-permute-start(f32[64,1024]{1,0:T(8,128)S(1)} %shard_map.97.before_ref.total_ref), channel_id=1, source_target_pairs={{0,16},{1,32},{3,96},{4,64}} | collective-permute-start | bytes 786440 | tf_op jit(solution)/shard_map/ppermute | solution.py:40
  77.6 2.7 %collective-permute-done.4.refs_0_ = f32[64,1024]{1,0:T(8,128)} collective-permute-done((f32[64,1024]{1,0:T(8,128)S(1)}, f32[64,1024]{1,0:T(8,128)}, u32[]{:S(2)}, u32[]{:S(2)}) %collective-permute-start.4) | collective-permute-done | bytes 262176 | tf_op jit(solution)/shard_map/ppermute | solution.py:40
  80.3 11.5 %collective-permute-start.5 = (f32[64,1024]{1,0:T(8,128)}, f32[64,1024]{1,0:T(8,128)}, u32[]{:S(2)}, u32[]{:S(2)}) collective-permute-start(f32[64,1024]{1,0:T(8,128)} %collective-permute-done.4.refs_0_), channel_id=1, source_target_pairs={{32,48},{64,80},{96,112}} | collective-permute-start | bytes 786440 | tf_op jit(solution)/shard_map/ppermute | solution.py:40
  91.9 1.6 copy-done.2
  93.5 1.9 shard_map.98
  95.4 2.1 collective-permute-start.7
  97.5 0.7 collective-permute-start.13
  98.2 3.0 %collective-permute-start.6 = (f32[64,1024]{1,0:T(8,128)S(1)}, f32[64,1024]{1,0:T(8,128)S(1)}, u32[]{:S(2)}, u32[]{:S(2)}) collective-permute-start(f32[64,1024]{1,0:T(8,128)S(1)} %get-tuple-element.32.before_ref), channel_id=1, source_target_pairs={{16,33}} | collective-permute-start | bytes 786440 | tf_op jit(solution)/shard_map/ppermute | solution.py:40
  101.2 0.7 collective-permute-start.10
  101.9 0.7 collective-permute-start.11
  102.6 0.7 collective-permute-start.12
  103.3 0.7 collective-permute-start.8
  104.0 1.1 collective-permute-done.6.refs_0_
  105.0 0.7 collective-permute-start.9
  106.4 0.7 collective-permute-start.15
  107.1 19.5 %collective-permute-start.20 = (f32[64,1024]{1,0:T(8,128)S(1)}, f32[64,1024]{1,0:T(8,128)S(1)}, u32[]{:S(2)}, u32[]{:S(2)}) collective-permute-start(f32[64,1024]{1,0:T(8,128)S(1)} %get-tuple-element.32.before_ref), channel_id=1, source_target_pairs={{48,50},{64,67},{80,84},{96,101},{112,118}} | collective-permute-start | bytes 786440 | tf_op jit(solution)/shard_map/ppermute | solution.py:40
  126.6 0.7 collective-permute-start.14
  127.3 0.9 collective-permute-start.21
  128.2 0.7 collective-permute-start.16
  128.9 0.7 collective-permute-start.17
  129.6 0.7 collective-permute-start.18
  130.3 0.7 collective-permute-start.19
  131.6 0.7 collective-permute-start.23
  132.3 25.2 %collective-permute-start.27 = (f32[64,1024]{1,0:T(8,128)S(1)}, f32[64,1024]{1,0:T(8,128)S(1)}, u32[]{:S(2)}, u32[]{:S(2)}) collective-permute-start(f32[64,1024]{1,0:T(8,128)S(1)} %get-tuple-element.34.before_ref), channel_id=1, source_target_pairs={{65,67},{81,84},{97,101},{113,118}} | collective-permute-start | bytes 786440 | tf_op jit(solution)/shard_map/ppermute | solution.py:40
  157.5 0.7 collective-permute-start.22
  158.2 0.7 collective-permute-start.28
  158.9 0.7 collective-permute-start.24
  159.6 0.7 collective-permute-start.25
  160.3 0.7 collective-permute-start.26
  161.7 0.7 collective-permute-start.30
  162.3 21.1 %collective-permute-start.33 = (f32[64,1024]{1,0:T(8,128)S(1)}, f32[64,1024]{1,0:T(8,128)S(1)}, u32[]{:S(2)}, u32[]{:S(2)}) collective-permute-start(f32[64,1024]{1,0:T(8,128)S(1)} %get-tuple-element.36.before_ref), channel_id=1, source_target_pairs={{82,84},{98,101},{114,118}} | collective-permute-start | bytes 786440 | tf_op jit(solution)/shard_map/ppermute | solution.py:40
  183.4 0.7 collective-permute-start.29
  184.1 0.7 collective-permute-start.34
  184.8 0.7 collective-permute-start.31
  185.5 0.7 collective-permute-start.32
  186.9 0.7 collective-permute-start.36
  187.5 0.7 collective-permute-start.38
  188.2 0.7 collective-permute-start.35
  188.9 0.7 collective-permute-start.39
  189.6 0.7 collective-permute-start.37
  190.3 0.7 collective-permute-start.41
  191.6 0.7 collective-permute-start.40
  192.3 0.7 collective-permute-start.42
  193.0 1.3 shard_map.104
  194.4 0.7 copy-done.4
  195.1 6.7 %all-to-all-start.2 = ((f32[16,8,512]{2,1,0:T(8,128)}), f32[16,8,512]{2,1,0:T(8,128)S(1)}, u32[]{:S(2)}, u32[]{:S(2)}) async-start(f32[16,8,512]{2,1,0:T(8,128)} %bitcast.20), calls=%async_computation.2 | async-start | bytes 524288 | tf_op jit(solution)/shard_map/all_to_all | solution.py:28
  201.8 8.1 %all-to-all-done.2 = f32[16,8,512]{2,1,0:T(8,128)S(1)} async-done(((f32[16,8,512]{2,1,0:T(8,128)}), f32[16,8,512]{2,1,0:T(8,128)S(1)}, u32[]{:S(2)}, u32[]{:S(2)}) %all-to-all-start.2) | async-done | bytes 262176 | tf_op jit(solution)/shard_map/all_to_all | solution.py:28
  210.2 58.5 %all_to_all.21.pieces_ref = f32[128,8,512]{2,1,0:T(8,128)S(1)} all-to-all(f32[128,8,512]{2,1,0:T(8,128)S(1)} %broadcast_in_dim.19), channel_id=1, replica_groups=mesh['prow_0'=4,'prow_1'=2,'pcol_0'=4,'pcol_1'=4] {'prow_0','prow_1','pc..., dimensions={0} | all-to-all | bytes 4194304 | tf_op jit(solution)/shard_map/all_to_all | solution.py:28
  268.7 2.9 %shard_map.105 = (f32[64,1024]{1,0:T(8,128)}, f32[2,64,128]{2,1,0:T(8,128)}) custom-call(s32[2]{0:T(128)S(1)} %bitcast.22, s32[2,8]{1,0:T(2,128)S(1)} %bitcast.21, s32[2]{0:T(128)S(1)} %pad_add_fusion.where_ref.row_ref, f32[128,8,512]{2,1,0:T(8,128)S(1)} %all_to_all.21.pieces_ref, f32[2,64,1024]{2,1,0:T(8,128)S(1)} %pad_maximum_fusion.refs_0_, ...), custom_call_target="tpu_custom_call" | custom-call | tf_op jit(solution)/shard_map/pallas_call | solution.py:278
  (62 shorter events, 3.6 us)
Async XLA Ops:
  0.6 14.9 %copy-start = (f32[64,2048]{1,0:T(8,128)S(1)}, f32[64,2048]{1,0:T(8,128)}, u32[]{:S(2)}) copy-start(f32[64,2048]{1,0:T(8,128)} %param.9) | copy-start | bytes 1572868
  0.6 12.9 %collective-permute-start = (f32[64,1024]{1,0:T(8,128)}, f32[64,1024]{1,0:T(8,128)S(1)}, u32[]{:S(2)}, u32[]{:S(2)}) collective-permute-start(f32[64,1024]{1,0:T(8,128)} %param.8), channel_id=1, source_target_pairs={{0,16},{16,0},{1,17},{17,1},{2,18},{18,2},{3,19},{19,3},{4,20},{20... | collective-permute-start | bytes 786440 | tf_op jit(solution)/shard_map/ppermute | solution.py:309
  14.5 14.8 %collective-permute-start.1 = (f32[2,64,1024]{2,1,0:T(8,128)S(1)}, f32[2,64,1024]{2,1,0:T(8,128)}, u32[]{:S(2)}, u32[]{:S(2)}) collective-permute-start(f32[2,64,1024]{2,1,0:T(8,128)S(1)} %pad_maximum_fusion.refs_0_), channel_id=1, source_target_pairs={{0,32},{32,64},{64,96},{96,0},{1,33},{33,65},{65,97},{97,1},{2,34}... | collective-permute-start | bytes 1572872 | tf_op jit(solution)/shard_map/ppermute | solution.py:307
  29.3 20.4 %collective-permute-start.2 = (f32[2,64,1024]{2,1,0:T(8,128)}, f32[2,64,1024]{2,1,0:T(8,128)}, u32[]{:S(2)}, u32[]{:S(2)}) collective-permute-start(f32[2,64,1024]{2,1,0:T(8,128)} %collective-permute-done.1.refs_1_), channel_id=1, source_target_pairs={{0,32},{32,64},{64,96},{96,0},{1,33},{33,65},{65,97},{97,1},{2,34}... | collective-permute-start | bytes 1572872 | tf_op jit(solution)/shard_map/ppermute | solution.py:307
  30.1 19.6 %all-to-all-start = ((f32[16,4,1024]{2,1,0:T(4,128)}), f32[16,4,1024]{2,1,0:T(4,128)}, u32[]{:S(2)}, u32[]{:S(2)}) async-start(f32[16,4,1024]{2,1,0:T(4,128)} %reshape.17), calls=%async_computation | async-start | bytes 524288 | tf_op jit(solution)/shard_map/all_to_all | solution.py:28
  48.4 1.4 copy-start.1
  49.8 19.5 %collective-permute-start.3 = (f32[2,64,1024]{2,1,0:T(8,128)}, f32[2,64,1024]{2,1,0:T(8,128)}, u32[]{:S(2)}, u32[]{:S(2)}) collective-permute-start(f32[2,64,1024]{2,1,0:T(8,128)} %collective-permute-done.2.refs_2_), channel_id=1, source_target_pairs={{0,32},{32,64},{64,96},{96,0},{1,33},{33,65},{65,97},{97,1},{2,34}... | collective-permute-start | bytes 1572872 | tf_op jit(solution)/shard_map/ppermute | solution.py:307
  69.3 11.0 %collective-permute-start.4 = (f32[64,1024]{1,0:T(8,128)S(1)}, f32[64,1024]{1,0:T(8,128)}, u32[]{:S(2)}, u32[]{:S(2)}) collective-permute-start(f32[64,1024]{1,0:T(8,128)S(1)} %shard_map.97.before_ref.total_ref), channel_id=1, source_target_pairs={{0,16},{1,32},{3,96},{4,64}} | collective-permute-start | bytes 786440 | tf_op jit(solution)/shard_map/ppermute | solution.py:40
  80.3 11.6 %collective-permute-start.5 = (f32[64,1024]{1,0:T(8,128)}, f32[64,1024]{1,0:T(8,128)}, u32[]{:S(2)}, u32[]{:S(2)}) collective-permute-start(f32[64,1024]{1,0:T(8,128)} %collective-permute-done.4.refs_0_), channel_id=1, source_target_pairs={{32,48},{64,80},{96,112}} | collective-permute-start | bytes 786440 | tf_op jit(solution)/shard_map/ppermute | solution.py:40
  91.9 1.6 copy-start.2
  95.4 5.8 %collective-permute-start.7 = (f32[64,1024]{1,0:T(8,128)S(1)}, f32[64,1024]{1,0:T(8,128)S(1)}, u32[]{:S(2)}, u32[]{:S(2)}) collective-permute-start(f32[64,1024]{1,0:T(8,128)S(1)} %get-tuple-element.32.before_ref), channel_id=1, source_target_pairs={{16,0}} | collective-permute-start | bytes 786440 | tf_op jit(solution)/shard_map/ppermute | solution.py:40
  97.5 5.8 %collective-permute-start.13 = (f32[64,1024]{1,0:T(8,128)S(1)}, f32[64,1024]{1,0:T(8,128)S(1)}, u32[]{:S(2)}, u32[]{:S(2)}) collective-permute-start(f32[64,1024]{1,0:T(8,128)S(1)} %get-tuple-element.32.before_ref), channel_id=1, source_target_pairs={{32,33}} | collective-permute-start | bytes 786440 | tf_op jit(solution)/shard_map/ppermute | solution.py:40
  98.2 6.9 %collective-permute-start.6 = (f32[64,1024]{1,0:T(8,128)S(1)}, f32[64,1024]{1,0:T(8,128)S(1)}, u32[]{:S(2)}, u32[]{:S(2)}) collective-permute-start(f32[64,1024]{1,0:T(8,128)S(1)} %get-tuple-element.32.before_ref), channel_id=1, source_target_pairs={{16,33}} | collective-permute-start | bytes 786440 | tf_op jit(solution)/shard_map/ppermute | solution.py:40
  101.2 4.5 %collective-permute-start.10 = (f32[64,1024]{1,0:T(8,128)S(1)}, f32[64,1024]{1,0:T(8,128)S(1)}, u32[]{:S(2)}, u32[]{:S(2)}) collective-permute-start(f32[64,1024]{1,0:T(8,128)S(1)} %collective-permute-done.7), channel_id=1, source_target_pairs={{0,81}} | collective-permute-start | bytes 786440 | tf_op jit(solution)/shard_map/ppermute | solution.py:40
  101.9 3.8 %collective-permute-start.11 = (f32[64,1024]{1,0:T(8,128)S(1)}, f32[64,1024]{1,0:T(8,128)S(1)}, u32[]{:S(2)}, u32[]{:S(2)}) collective-permute-start(f32[64,1024]{1,0:T(8,128)S(1)} %collective-permute-done.7), channel_id=1, source_target_pairs={{0,97}} | collective-permute-start | bytes 786440 | tf_op jit(solution)/shard_map/ppermute | solution.py:40
  102.6 3.2 %collective-permute-start.12 = (f32[64,1024]{1,0:T(8,128)S(1)}, f32[64,1024]{1,0:T(8,128)S(1)}, u32[]{:S(2)}, u32[]{:S(2)}) collective-permute-start(f32[64,1024]{1,0:T(8,128)S(1)} %collective-permute-done.7), channel_id=1, source_target_pairs={{0,113}} | collective-permute-start | bytes 786440 | tf_op jit(solution)/shard_map/ppermute | solution.py:40
  103.3 2.5 collective-permute-start.8
  105.0 0.7 collective-permute-start.9
  106.4 21.8 %collective-permute-start.15 = (f32[64,1024]{1,0:T(8,128)S(1)}, f32[64,1024]{1,0:T(8,128)S(1)}, u32[]{:S(2)}, u32[]{:S(2)}) collective-permute-start(f32[64,1024]{1,0:T(8,128)S(1)} %get-tuple-element.34.before_ref), channel_id=1, source_target_pairs={{33,49}} | collective-permute-start | bytes 786440 | tf_op jit(solution)/shard_map/ppermute | solution.py:40
  107.1 22.5 %collective-permute-start.20 = (f32[64,1024]{1,0:T(8,128)S(1)}, f32[64,1024]{1,0:T(8,128)S(1)}, u32[]{:S(2)}, u32[]{:S(2)}) collective-permute-start(f32[64,1024]{1,0:T(8,128)S(1)} %get-tuple-element.32.before_ref), channel_id=1, source_target_pairs={{48,50},{64,67},{80,84},{96,101},{112,118}} | collective-permute-start | bytes 786440 | tf_op jit(solution)/shard_map/ppermute | solution.py:40
  126.6 3.7 %collective-permute-start.14 = (f32[64,1024]{1,0:T(8,128)S(1)}, f32[64,1024]{1,0:T(8,128)S(1)}, u32[]{:S(2)}, u32[]{:S(2)}) collective-permute-start(f32[64,1024]{1,0:T(8,128)S(1)} %get-tuple-element.34.before_ref), channel_id=1, source_target_pairs={{33,50}} | collective-permute-start | bytes 786440 | tf_op jit(solution)/shard_map/ppermute | solution.py:40
  127.3 3.7 %collective-permute-start.21 = (f32[64,1024]{1,0:T(8,128)S(1)}, f32[64,1024]{1,0:T(8,128)S(1)}, u32[]{:S(2)}, u32[]{:S(2)}) collective-permute-start(f32[64,1024]{1,0:T(8,128)S(1)} %get-tuple-element.34.before_ref), channel_id=1, source_target_pairs={{49,50}} | collective-permute-start | bytes 786440 | tf_op jit(solution)/shard_map/ppermute | solution.py:40
  128.2 2.8 %collective-permute-start.16 = (f32[64,1024]{1,0:T(8,128)S(1)}, f32[64,1024]{1,0:T(8,128)S(1)}, u32[]{:S(2)}, u32[]{:S(2)}) collective-permute-start(f32[64,1024]{1,0:T(8,128)S(1)} %collective-permute-done.15), channel_id=1, source_target_pairs={{49,66}} | collective-permute-start | bytes 786440 | tf_op jit(solution)/shard_map/ppermute | solution.py:40
  128.9 2.1 collective-permute-start.17
  129.6 1.4 collective-permute-start.18
  130.3 0.7 collective-permute-start.19
  131.6 27.3 %collective-permute-start.23 = (f32[64,1024]{1,0:T(8,128)S(1)}, f32[64,1024]{1,0:T(8,128)S(1)}, u32[]{:S(2)}, u32[]{:S(2)}) collective-permute-start(f32[64,1024]{1,0:T(8,128)S(1)} %get-tuple-element.36.before_ref), channel_id=1, source_target_pairs={{50,34}} | collective-permute-start | bytes 786440 | tf_op jit(solution)/shard_map/ppermute | solution.py:40
  132.3 28.0 %collective-permute-start.27 = (f32[64,1024]{1,0:T(8,128)S(1)}, f32[64,1024]{1,0:T(8,128)S(1)}, u32[]{:S(2)}, u32[]{:S(2)}) collective-permute-start(f32[64,1024]{1,0:T(8,128)S(1)} %get-tuple-element.34.before_ref), channel_id=1, source_target_pairs={{65,67},{81,84},{97,101},{113,118}} | collective-permute-start | bytes 786440 | tf_op jit(solution)/shard_map/ppermute | solution.py:40
  157.5 3.5 %collective-permute-start.22 = (f32[64,1024]{1,0:T(8,128)S(1)}, f32[64,1024]{1,0:T(8,128)S(1)}, u32[]{:S(2)}, u32[]{:S(2)}) collective-permute-start(f32[64,1024]{1,0:T(8,128)S(1)} %get-tuple-element.36.before_ref), channel_id=1, source_target_pairs={{50,67}} | collective-permute-start | bytes 786440 | tf_op jit(solution)/shard_map/ppermute | solution.py:40
  158.2 2.8 %collective-permute-start.28 = (f32[64,1024]{1,0:T(8,128)S(1)}, f32[64,1024]{1,0:T(8,128)S(1)}, u32[]{:S(2)}, u32[]{:S(2)}) collective-permute-start(f32[64,1024]{1,0:T(8,128)S(1)} %get-tuple-element.36.before_ref), channel_id=1, source_target_pairs={{66,67}} | collective-permute-start | bytes 786440 | tf_op jit(solution)/shard_map/ppermute | solution.py:40
  158.9 2.1 collective-permute-start.24
  159.6 1.4 collective-permute-start.25
  160.3 0.7 collective-permute-start.26
  161.7 23.1 %collective-permute-start.30 = (f32[64,1024]{1,0:T(8,128)S(1)}, f32[64,1024]{1,0:T(8,128)S(1)}, u32[]{:S(2)}, u32[]{:S(2)}) collective-permute-start(f32[64,1024]{1,0:T(8,128)S(1)} %get-tuple-element.38.before_ref), channel_id=1, source_target_pairs={{67,83}} | collective-permute-start | bytes 786440 | tf_op jit(solution)/shard_map/ppermute | solution.py:40
  162.3 23.8 %collective-permute-start.33 = (f32[64,1024]{1,0:T(8,128)S(1)}, f32[64,1024]{1,0:T(8,128)S(1)}, u32[]{:S(2)}, u32[]{:S(2)}) collective-permute-start(f32[64,1024]{1,0:T(8,128)S(1)} %get-tuple-element.36.before_ref), channel_id=1, source_target_pairs={{82,84},{98,101},{114,118}} | collective-permute-start | bytes 786440 | tf_op jit(solution)/shard_map/ppermute | solution.py:40
  183.4 2.8 %collective-permute-start.29 = (f32[64,1024]{1,0:T(8,128)S(1)}, f32[64,1024]{1,0:T(8,128)S(1)}, u32[]{:S(2)}, u32[]{:S(2)}) collective-permute-start(f32[64,1024]{1,0:T(8,128)S(1)} %get-tuple-element.38.before_ref), channel_id=1, source_target_pairs={{67,84}} | collective-permute-start | bytes 786440 | tf_op jit(solution)/shard_map/ppermute | solution.py:40
  184.1 2.1 collective-permute-start.34
  184.8 1.4 collective-permute-start.31
  185.5 0.7 collective-permute-start.32
  186.9 2.7 %collective-permute-start.36 = (f32[64,1024]{1,0:T(8,128)S(1)}, f32[64,1024]{1,0:T(8,128)S(1)}, u32[]{:S(2)}, u32[]{:S(2)}) collective-permute-start(f32[64,1024]{1,0:T(8,128)S(1)} %get-tuple-element.40.before_ref), channel_id=1, source_target_pairs={{84,68}} | collective-permute-start | bytes 786440 | tf_op jit(solution)/shard_map/ppermute | solution.py:40
  187.5 3.4 %collective-permute-start.38 = (f32[64,1024]{1,0:T(8,128)S(1)}, f32[64,1024]{1,0:T(8,128)S(1)}, u32[]{:S(2)}, u32[]{:S(2)}) collective-permute-start(f32[64,1024]{1,0:T(8,128)S(1)} %get-tuple-element.38.before_ref), channel_id=1, source_target_pairs={{99,101},{115,118}} | collective-permute-start | bytes 786440 | tf_op jit(solution)/shard_map/ppermute | solution.py:40
  188.2 2.8 %collective-permute-start.35 = (f32[64,1024]{1,0:T(8,128)S(1)}, f32[64,1024]{1,0:T(8,128)S(1)}, u32[]{:S(2)}, u32[]{:S(2)}) collective-permute-start(f32[64,1024]{1,0:T(8,128)S(1)} %get-tuple-element.40.before_ref), channel_id=1, source_target_pairs={{84,101}} | collective-permute-start | bytes 786440 | tf_op jit(solution)/shard_map/ppermute | solution.py:40
  188.9 2.1 collective-permute-start.39
  189.6 1.4 collective-permute-start.37
  190.3 2.7 %collective-permute-start.41 = (f32[64,1024]{1,0:T(8,128)S(1)}, f32[64,1024]{1,0:T(8,128)S(1)}, u32[]{:S(2)}, u32[]{:S(2)}) collective-permute-start(f32[64,1024]{1,0:T(8,128)S(1)} %get-tuple-element.40.before_ref), channel_id=1, source_target_pairs={{116,118}} | collective-permute-start | bytes 786440 | tf_op jit(solution)/shard_map/ppermute | solution.py:40
  191.6 1.4 collective-permute-start.40
  192.3 0.7 collective-permute-start.42
  194.4 0.7 copy-start.4
  194.4 74.3 %copy-start.3 = (f32[1,2,8,128,128]{4,3,2,1,0:T(8,128)S(1)}, f32[1,2,8,128,128]{4,3,2,1,0:T(8,128)}, u32[]{:S(2)}) copy-start(f32[1,2,8,128,128]{4,3,2,1,0:T(8,128)} %param.15) | copy-start | bytes 3145732
  194.4 74.3 %copy-start.5 = (s32[1,2,8]{2,1,0:T(2,128)S(1)}, s32[1,2,8]{2,1,0:T(2,128)}, u32[]{:S(2)}) copy-start(s32[1,2,8]{2,1,0:T(2,128)} %param.14) | copy-start | bytes 196
  194.4 74.3 %copy-start.6 = (s32[1,2]{1,0:T(1,128)S(1)}, s32[1,2]{1,0:T(1,128)}, u32[]{:S(2)}) copy-start(s32[1,2]{1,0:T(1,128)} %param.13) | copy-start | bytes 28
  195.1 14.8 %all-to-all-start.2 = ((f32[16,8,512]{2,1,0:T(8,128)}), f32[16,8,512]{2,1,0:T(8,128)S(1)}, u32[]{:S(2)}, u32[]{:S(2)}) async-start(f32[16,8,512]{2,1,0:T(8,128)} %bitcast.20), calls=%async_computation.2 | async-start | bytes 524288 | tf_op jit(solution)/shard_map/all_to_all | solution.py:28

commit v6 on v4

--- a/solution.py
+++ b/solution.py
@@ -200,12 +200,20 @@
         def _():
             out_ref[...] = before_ref[...]
 
-        @pl.when(turn)
+        @pl.when(jnp.logical_and(turn, row == step + 1))
+        def _():
+            out_ref[...] = known_refs[0][...]
+
+        @pl.when(jnp.logical_and(turn, row > step + 1))
         def _():
             known = known_refs[0][...]
             for ref in known_refs[1:]:
                 known = known + ref[...]
-            out_ref[...] = sum_ref[...] - three_pass(known, high_ref[...], low_ref[...], ALONG)
+            out_ref[...] = known
+
+        @pl.when(turn)
+        def _():
+            out_ref[...] = sum_ref[...] - three_pass(out_ref[...], high_ref[...], low_ref[...], ALONG)
 
     extras = [] if extra is None else [extra]
     like = jax.ShapeDtypeStruct(before.shape, jnp.float32)
@@ -216,6 +224,21 @@
         out_shape=(like, like),
         compiler_params=room(3),
     )(where, before, total, *knowns, *extras, high, low)
+
+
+def assemble_kernel(pieces_ref, out_ref):
+    for i in range(COLS):
+        out_ref[pl.ds(i * 4, 4), :] = pieces_ref[i]
+
+
+def assemble(pieces):
+    return pl.pallas_call(
+        assemble_kernel,
+        in_specs=[VMEM],
+        out_specs=VMEM,
+        out_shape=jax.ShapeDtypeStruct((64, 1024), jnp.float32),
+        compiler_params=room(2),
+    )(pieces)
 
 
 def finish_kernel(tiles_ref, near_ref, row_ref, pieces_ref, rhs_ref, force_ref, solution_ref, residual_ref):
@@ -274,7 +297,7 @@
     past_rows, high = lax.optimization_barrier((past_rows, high))
     rhs_rows = lax.dynamic_slice_in_dim(window_rhs, col * 4, 4, 0)
     start_rows = start_product(rhs_rows, past_rows, inverse)
-    start = to_everyone(start_rows, PCOL, COLS).reshape(64, 1024)
+    start = assemble(to_everyone(start_rows, PCOL, COLS))
 
     arrived = send(start, [(place(0, k - 1), place(k, 0)) for k in range(1, ROWS)])
     current, total = fire(0, where, start, start, None, [arrived], high, low)

time: 218 us -> 218 us (level)
  no operation moved by 1% of the time
where the time goes in v6:
time: 218 us; the launch traced here: 217 us
  starting transfers between devices  104 us (48%)
  waiting for transfers between devices  42.5 us (19%)
  Pallas kernels  22.2 us (10%)
  between operations  14.7 us (7%)
  blocking collectives  14 us (6%)
  local copies, waits for them, and re-layouts  11.6 us (5%)
  matrix products  7.31 us (3%)
    all_to_all x3, starting transfers between devices, exchange(): return lax.all_to_all(pieces, axes, 0, 0, tiled=True)  79.6 us
    all_to_all x3, waiting for transfers between devices, exchange(): return lax.all_to_all(pieces, axes, 0, 0, tiled=True)  37.2 us
    ppermute x33, starting transfers between devices, send(): return lax.ppermute(x, EVERY, pairs)  24.2 us
    all_to_all x1, blocking collectives, exchange(): return lax.all_to_all(pieces, axes, 0, 0, tiled=True)  14 us
    pallas_call x1, Pallas kernels, form(): pl.pallas_call(form_kernel, in_specs=[hbm, hbm], out_specs=(VMEM,) * 2, o...  11.4 us
    unnamed x16, local copies, waits for them, and re-layouts  8.38 us
    dot_general x1, matrix products, product(): lax.dot_general(left, right, (((left_dim,), (right_dim,)), ((), ())), pre...  7.31 us
    pallas_call x7, Pallas kernels, fire(): pl.pallas_call(kernel, in_specs=[SMEM] + [VMEM] * (len(knowns) + len(extr...  6.03 us
  transfers between devices with their start and end apart: 37, of which 4 were waited for; matrix products, arithmetic and copies ran while one was open for 1% of the time, Pallas kernels for 6%

profile of v6, /device:TPU:1, one launch (start us, length us, event | category | flops | bytes accessed | tf_op | source)
XLA Modules:
  0.0 216.5 jit_solution(10275214547142235315)
XLA Ops:
  7.2 1.0 copy-done
  8.2 7.3 %fusion = f32[64,1024]{1,0:T(8,128)S(1)} fusion(f32[64,2048]{1,0:T(8,128)S(1)} %copy-done, f32[1024,2048]{1,0:T(8,128)} %param.10), kind=kOutput, calls=%fused_computation.3 | convolution fusion | flops 805306368 | bytes 9175040 | tf_op jit(solution)/shard_map/dot_general | solution.py:18
  15.5 0.8 reshape.17
  16.3 7.6 %all-to-all-start = ((f32[16,4,1024]{2,1,0:T(4,128)}), f32[16,4,1024]{2,1,0:T(4,128)S(1)}, u32[]{:S(2)}, u32[]{:S(2)}) async-start(f32[16,4,1024]{2,1,0:T(4,128)} %reshape.17), calls=%async_computation | async-start | bytes 524288 | tf_op jit(solution)/shard_map/all_to_all | solution.py:28
  23.9 0.2 all-gather.3.cloned.1.call-start
  24.1 11.4 %shard_map.95 = (bf16[1024,1024]{1,0:T(8,128)(2,1)S(1)}, bf16[1024,1024]{1,0:T(8,128)(2,1)S(1)}) custom-call(f32[1024,1024]{1,0:T(8,128)} %bitcast.22, f32[8192,128]{1,0:T(8,128)} %bitcast.24), custom_call_target="tpu_custom_call" | custom-call | tf_op jit(solution)/shard_map/pallas_call | solution.py:143
  35.5 1.3 copy-done.1
  36.9 0.8 constant_dynamic-slice_fusion.rhs_ref
  37.6 0.1 reduce_sum.9.past_ref
  37.7 2.8 %shard_map.96 = f32[4,1024]{1,0:T(4,128)S(1)} custom-call(f32[4,1024]{1,0:T(4,128)S(1)} %constant_dynamic-slice_fusion.rhs_ref, f32[4,1024]{1,0:T(4,128)S(1)} %reduce_sum.9.past_ref, f32[1024,1024]{1,0:T(8,128)} %bitcast.23), custom_call_target="tpu_custom_call" | custom-call | tf_op jit(solution)/shard_map/pallas_call | solution.py:177
  40.6 14.0 %all_to_all.20.pieces_ref = f32[16,4,1024]{2,1,0:T(4,128)S(1)} all-to-all(f32[16,4,1024]{2,1,0:T(4,128)S(1)} %broadcast_in_dim.8), channel_id=1, replica_groups=mesh['prow_0'=4,'prow_1'=2,'pcol_0'=4,'pcol_1'=4] {'pcol_0','pcol_1'}, dimensions={0} | all-to-all | bytes 524288 | tf_op jit(solution)/shard_map/all_to_all | solution.py:28
  54.6 1.3 collective-permute-start
  55.9 0.1 pad_add_fusion.where_ref.row_ref
  56.0 3.6 %collective-permute-done.refs_0_ = f32[64,1024]{1,0:T(8,128)S(1)} collective-permute-done((f32[64,1024]{1,0:T(8,128)S(1)}, f32[64,1024]{1,0:T(8,128)S(1)}, u32[]{:S(2)}, u32[]{:S(2)}) %collective-permute-start) | collective-permute-done | bytes 262176 | tf_op jit(solution)/shard_map/ppermute | solution.py:40
  59.6 1.6 copy-done.2
  61.2 1.4 shard_map.98
  62.6 1.3 collective-permute-start.2
  63.9 1.3 collective-permute-start.1
  65.2 0.7 collective-permute-start.8
  65.9 0.7 collective-permute-start.3
  66.6 0.7 collective-permute-start.4
  67.3 0.7 collective-permute-start.5
  67.9 1.6 collective-permute-done.1.refs_0_
  69.5 0.7 collective-permute-start.6
  70.2 0.7 collective-permute-start.7
  71.0 0.6 shard_map.99
  71.6 0.7 collective-permute-start.10
  72.3 0.7 collective-permute-start.15
  72.9 0.7 collective-permute-start.9
  73.6 0.7 collective-permute-start.11
  74.3 0.7 collective-permute-start.12
  75.0 0.7 collective-permute-start.13
  75.7 0.7 collective-permute-start.14
  76.4 0.8 shard_map.100
  77.3 0.7 collective-permute-start.17
  78.0 0.7 collective-permute-start.16
  78.7 0.7 collective-permute-start.21
  79.4 0.7 collective-permute-start.18
  80.0 0.7 collective-permute-start.19
  80.7 0.7 collective-permute-start.20
  81.5 0.6 shard_map.101
  82.1 0.7 collective-permute-start.23
  82.8 0.7 collective-permute-start.22
  83.5 0.7 collective-permute-start.26
  84.2 0.7 collective-permute-start.24
  84.8 0.7 collective-permute-start.25
  85.6 1.6 copy-done.3
  87.2 0.6 shard_map.102
  87.8 0.7 collective-permute-start.28
  88.5 0.7 collective-permute-start.27
  89.2 0.7 collective-permute-start.30
  89.8 0.7 collective-permute-start.29
  90.6 0.6 shard_map.103
  91.2 0.7 collective-permute-start.31
  91.9 0.7 collective-permute-start.32
  92.6 1.4 shard_map.104
  94.0 3.7 %all-to-all-start.2 = ((f32[16,8,512]{2,1,0:T(8,128)}), f32[16,8,512]{2,1,0:T(8,128)S(1)}, u32[]{:S(2)}, u32[]{:S(2)}) async-start(f32[16,8,512]{2,1,0:T(8,128)} %bitcast.8), calls=%async_computation.2 | async-start | bytes 524288 | tf_op jit(solution)/shard_map/all_to_all | solution.py:28
  97.7 7.5 %all-to-all-done.2 = f32[16,8,512]{2,1,0:T(8,128)S(1)} async-done(((f32[16,8,512]{2,1,0:T(8,128)}), f32[16,8,512]{2,1,0:T(8,128)S(1)}, u32[]{:S(2)}, u32[]{:S(2)}) %all-to-all-start.2) | async-done | bytes 262176 | tf_op jit(solution)/shard_map/all_to_all | solution.py:28
  105.2 1.6 broadcast_in_dim.19
  106.8 68.4 %all-to-all-start.3 = ((f32[128,8,512]{2,1,0:T(8,128)}), f32[128,8,512]{2,1,0:T(8,128)S(1)}, u32[]{:S(2)}, u32[]{:S(2)}) async-start(f32[128,8,512]{2,1,0:T(8,128)} %broadcast_in_dim.19), calls=%async_computation.3 | async-start | bytes 4194304 | tf_op jit(solution)/shard_map/all_to_all | solution.py:28
  175.2 29.7 %all-to-all-done.3.pieces_ref = f32[128,8,512]{2,1,0:T(8,128)S(1)} async-done(((f32[128,8,512]{2,1,0:T(8,128)}), f32[128,8,512]{2,1,0:T(8,128)S(1)}, u32[]{:S(2)}, u32[]{:S(2)}) %all-to-all-start.3) | async-done | bytes 2097184 | tf_op jit(solution)/shard_map/all_to_all | solution.py:28
  204.9 1.6 copy-done.4
  206.5 1.2 copy-done.5
  207.7 2.0 shard_map.105
  (47 shorter events, 0.2 us)
Async XLA Ops:
  7.2 1.0 copy-start
  16.3 21.3 %all-to-all-start = ((f32[16,4,1024]{2,1,0:T(4,128)}), f32[16,4,1024]{2,1,0:T(4,128)S(1)}, u32[]{:S(2)}, u32[]{:S(2)}) async-start(f32[16,4,1024]{2,1,0:T(4,128)} %reshape.17), calls=%async_computation | async-start | bytes 524288 | tf_op jit(solution)/shard_map/all_to_all | solution.py:28
  23.9 151.3 %all-gather.3.cloned.1.call-start = ((), (), s32[]{:S(2)}) async-start(), calls=%async_computation.4 | async-start | bytes 2359296 | tf_op jit(solution)/shard_map/all_gather | solution.py:293
  35.5 1.4 copy-start.1
  54.6 5.0 %collective-permute-start = (f32[64,1024]{1,0:T(8,128)S(1)}, f32[64,1024]{1,0:T(8,128)S(1)}, u32[]{:S(2)}, u32[]{:S(2)}) collective-permute-start(f32[64,1024]{1,0:T(8,128)S(1)} %shard_map.97.before_ref.total_ref), channel_id=1, source_target_pairs={{0,16},{1,32},{2,48},{3,64},{4,80},{5,96},{6,112}} | collective-permute-start | bytes 786440 | tf_op jit(solution)/shard_map/ppermute | solution.py:40
  59.6 1.6 copy-start.2
  62.6 3.3 %collective-permute-start.2 = (f32[64,1024]{1,0:T(8,128)S(1)}, f32[64,1024]{1,0:T(8,128)S(1)}, u32[]{:S(2)}, u32[]{:S(2)}) collective-permute-start(f32[64,1024]{1,0:T(8,128)S(1)} %get-tuple-element.25.before_ref), channel_id=1, source_target_pairs={{16,0}} | collective-permute-start | bytes 786440 | tf_op jit(solution)/shard_map/ppermute | solution.py:40
  63.9 5.7 %collective-permute-start.1 = (f32[64,1024]{1,0:T(8,128)S(1)}, f32[64,1024]{1,0:T(8,128)S(1)}, u32[]{:S(2)}, u32[]{:S(2)}) collective-permute-start(f32[64,1024]{1,0:T(8,128)S(1)} %get-tuple-element.25.before_ref), channel_id=1, source_target_pairs={{16,33}} | collective-permute-start | bytes 786440 | tf_op jit(solution)/shard_map/ppermute | solution.py:40
  65.2 5.0 %collective-permute-start.8 = (f32[64,1024]{1,0:T(8,128)S(1)}, f32[64,1024]{1,0:T(8,128)S(1)}, u32[]{:S(2)}, u32[]{:S(2)}) collective-permute-start(f32[64,1024]{1,0:T(8,128)S(1)} %get-tuple-element.25.before_ref), channel_id=1, source_target_pairs={{32,33},{48,50},{64,67},{80,84},{96,101},{112,118}} | collective-permute-start | bytes 786440 | tf_op jit(solution)/shard_map/ppermute | solution.py:40
  65.9 5.0 %collective-permute-start.3 = (f32[64,1024]{1,0:T(8,128)S(1)}, f32[64,1024]{1,0:T(8,128)S(1)}, u32[]{:S(2)}, u32[]{:S(2)}) collective-permute-start(f32[64,1024]{1,0:T(8,128)S(1)} %collective-permute-done.2), channel_id=1, source_target_pairs={{0,49}} | collective-permute-start | bytes 786440 | tf_op jit(solution)/shard_map/ppermute | solution.py:40
  66.6 4.4 %collective-permute-start.4 = (f32[64,1024]{1,0:T(8,128)S(1)}, f32[64,1024]{1,0:T(8,128)S(1)}, u32[]{:S(2)}, u32[]{:S(2)}) collective-permute-start(f32[64,1024]{1,0:T(8,128)S(1)} %collective-permute-done.2), channel_id=1, source_target_pairs={{0,65}} | collective-permute-start | bytes 786440 | tf_op jit(solution)/shard_map/ppermute | solution.py:40
  67.3 3.7 %collective-permute-start.5 = (f32[64,1024]{1,0:T(8,128)S(1)}, f32[64,1024]{1,0:T(8,128)S(1)}, u32[]{:S(2)}, u32[]{:S(2)}) collective-permute-start(f32[64,1024]{1,0:T(8,128)S(1)} %collective-permute-done.2), channel_id=1, source_target_pairs={{0,81}} | collective-permute-start | bytes 786440 | tf_op jit(solution)/shard_map/ppermute | solution.py:40
  69.5 1.4 collective-permute-start.6
  70.2 0.7 collective-permute-start.7
  71.6 2.1 collective-permute-start.10
  72.3 3.4 %collective-permute-start.15 = (f32[64,1024]{1,0:T(8,128)S(1)}, f32[64,1024]{1,0:T(8,128)S(1)}, u32[]{:S(2)}, u32[]{:S(2)}) collective-permute-start(f32[64,1024]{1,0:T(8,128)S(1)} %get-tuple-element.27.before_ref), channel_id=1, source_target_pairs={{49,50},{65,67},{81,84},{97,101},{113,118}} | collective-permute-start | bytes 786440 | tf_op jit(solution)/shard_map/ppermute | solution.py:40
  72.9 3.5 %collective-permute-start.9 = (f32[64,1024]{1,0:T(8,128)S(1)}, f32[64,1024]{1,0:T(8,128)S(1)}, u32[]{:S(2)}, u32[]{:S(2)}) collective-permute-start(f32[64,1024]{1,0:T(8,128)S(1)} %get-tuple-element.27.before_ref), channel_id=1, source_target_pairs={{33,50}} | collective-permute-start | bytes 786440 | tf_op jit(solution)/shard_map/ppermute | solution.py:40
  73.6 2.8 %collective-permute-start.11 = (f32[64,1024]{1,0:T(8,128)S(1)}, f32[64,1024]{1,0:T(8,128)S(1)}, u32[]{:S(2)}, u32[]{:S(2)}) collective-permute-start(f32[64,1024]{1,0:T(8,128)S(1)} %collective-permute-done.10), channel_id=1, source_target_pairs={{49,66}} | collective-permute-start | bytes 786440 | tf_op jit(solution)/shard_map/ppermute | solution.py:40
  74.3 2.1 collective-permute-start.12
  75.0 1.4 collective-permute-start.13
  75.7 0.7 collective-permute-start.14
  77.3 2.1 collective-permute-start.17
  78.0 3.4 %collective-permute-start.16 = (f32[64,1024]{1,0:T(8,128)S(1)}, f32[64,1024]{1,0:T(8,128)S(1)}, u32[]{:S(2)}, u32[]{:S(2)}) collective-permute-start(f32[64,1024]{1,0:T(8,128)S(1)} %get-tuple-element.29.before_ref), channel_id=1, source_target_pairs={{50,67}} | collective-permute-start | bytes 786440 | tf_op jit(solution)/shard_map/ppermute | solution.py:40
  78.7 2.8 %collective-permute-start.21 = (f32[64,1024]{1,0:T(8,128)S(1)}, f32[64,1024]{1,0:T(8,128)S(1)}, u32[]{:S(2)}, u32[]{:S(2)}) collective-permute-start(f32[64,1024]{1,0:T(8,128)S(1)} %get-tuple-element.29.before_ref), channel_id=1, source_target_pairs={{66,67},{82,84},{98,101},{114,118}} | collective-permute-start | bytes 786440 | tf_op jit(solution)/shard_map/ppermute | solution.py:40
  79.4 2.1 collective-permute-start.18
  80.0 1.4 collective-permute-start.19
  80.7 0.7 collective-permute-start.20
  82.1 2.1 collective-permute-start.23
  82.8 2.8 %collective-permute-start.22 = (f32[64,1024]{1,0:T(8,128)S(1)}, f32[64,1024]{1,0:T(8,128)S(1)}, u32[]{:S(2)}, u32[]{:S(2)}) collective-permute-start(f32[64,1024]{1,0:T(8,128)S(1)} %get-tuple-element.31.before_ref), channel_id=1, source_target_pairs={{67,84}} | collective-permute-start | bytes 786440 | tf_op jit(solution)/shard_map/ppermute | solution.py:40
  83.5 2.1 collective-permute-start.26
  84.2 1.4 collective-permute-start.24
  84.8 0.7 collective-permute-start.25
  85.6 1.6 copy-start.3
  87.8 2.1 collective-permute-start.28
  88.5 2.1 collective-permute-start.27
  89.2 1.4 collective-permute-start.30
  89.8 0.7 collective-permute-start.29
  91.2 1.4 collective-permute-start.31
  91.9 0.7 collective-permute-start.32
  94.0 110.9 %copy-start.6 = (s32[1,2,8]{2,1,0:T(2,128)S(1)}, s32[1,2,8]{2,1,0:T(2,128)}, u32[]{:S(2)}) copy-start(s32[1,2,8]{2,1,0:T(2,128)} %param.14) | copy-start | bytes 196
  94.0 110.9 %copy-start.7 = (s32[1,2]{1,0:T(1,128)S(1)}, s32[1,2]{1,0:T(1,128)}, u32[]{:S(2)}) copy-start(s32[1,2]{1,0:T(1,128)} %param.13) | copy-start | bytes 28
  94.0 11.2 %all-to-all-start.2 = ((f32[16,8,512]{2,1,0:T(8,128)}), f32[16,8,512]{2,1,0:T(8,128)S(1)}, u32[]{:S(2)}, u32[]{:S(2)}) async-start(f32[16,8,512]{2,1,0:T(8,128)} %bitcast.8), calls=%async_computation.2 | async-start | bytes 524288 | tf_op jit(solution)/shard_map/all_to_all | solution.py:28
  106.8 98.1 %all-to-all-start.3 = ((f32[128,8,512]{2,1,0:T(8,128)}), f32[128,8,512]{2,1,0:T(8,128)S(1)}, u32[]{:S(2)}, u32[]{:S(2)}) async-start(f32[128,8,512]{2,1,0:T(8,128)} %broadcast_in_dim.19), calls=%async_computation.3 | async-start | bytes 4194304 | tf_op jit(solution)/shard_map/all_to_all | solution.py:28
  204.9 1.6 copy-start.4
  206.5 1.2 copy-start.5
Sparse Core Ops, SparseCore 0:
  82.9 57.6 all-gather.2

commit v7 on v6

--- a/solution.py
+++ b/solution.py
@@ -184,17 +184,12 @@
     )(rhs, past, in_hbm(inverse))
 
 
-def fire(step, where, before, total, extra, knowns, high, low):
-    def kernel(where_ref, before_ref, total_ref, *refs):
+def fire(step, where, before, base, knowns, high, low):
+    def kernel(where_ref, before_ref, base_ref, *refs):
+        known_refs = refs[:-3]
+        high_ref, low_ref, out_ref = refs[-3:]
         row, col = where_ref[0], where_ref[1]
         turn = jnp.logical_and(col == step, row > step)
-        known_refs = refs[: len(knowns)]
-        extra_refs = refs[len(knowns) : -4]
-        high_ref, low_ref, out_ref, sum_ref = refs[-4:]
-        if extra_refs:
-            sum_ref[...] = total_ref[...] + extra_refs[0][...]
-        else:
-            sum_ref[...] = jnp.where(row == col + 1, total_ref[...], 0.0)
 
         @pl.when(jnp.logical_not(turn))
         def _():
@@ -213,17 +208,15 @@
 
         @pl.when(turn)
         def _():
-            out_ref[...] = sum_ref[...] - three_pass(out_ref[...], high_ref[...], low_ref[...], ALONG)
-
-    extras = [] if extra is None else [extra]
-    like = jax.ShapeDtypeStruct(before.shape, jnp.float32)
+            out_ref[...] = base_ref[...] - three_pass(out_ref[...], high_ref[...], low_ref[...], ALONG)
+
     return pl.pallas_call(
         kernel,
-        in_specs=[SMEM] + [VMEM] * (len(knowns) + len(extras) + 4),
-        out_specs=(VMEM, VMEM),
-        out_shape=(like, like),
+        in_specs=[SMEM] + [VMEM] * (len(knowns) + 4),
+        out_specs=VMEM,
+        out_shape=jax.ShapeDtypeStruct(before.shape, jnp.float32),
         compiler_params=room(3),
-    )(where, before, total, *knowns, *extras, high, low)
+    )(where, before, base, *knowns, high, low)
 
 
 def assemble_kernel(pieces_ref, out_ref):
@@ -300,16 +293,12 @@
     start = assemble(to_everyone(start_rows, PCOL, COLS))
 
     arrived = send(start, [(place(0, k - 1), place(k, 0)) for k in range(1, ROWS)])
-    current, total = fire(0, where, start, start, None, [arrived], high, low)
+    current = fire(0, where, start, start, [arrived], high, low)
     for step in range(1, ROWS - 1):
         source = place(step, step - 1)
-        beside = place(step ^ 1, step - 1)
-        knowns = [send(current, [(source, place(step + 1, step))])]
-        if step + 2 < ROWS:
-            relayed = send(current, [(source, beside)])
-            knowns += [send(relayed, [(beside, place(k, step))]) for k in range(step + 2, ROWS)]
-        extra = send(current, [(place(k, step - 1), place(k, k - 1)) for k in range(step + 1, ROWS)])
-        current, total = fire(step, where, current, total, extra, knowns, high, low)
+        knowns = [send(current, [(source, place(k, step))]) for k in range(step + 1, ROWS)]
+        partial = send(current, [(place(k, step - 1), place(k, step)) for k in range(step + 1, ROWS)])
+        current = fire(step, where, current, partial, knowns, high, low)
 
     pieces = current.reshape(8, 8, 2, 512).transpose(0, 2, 1, 3).reshape(COLS, 8, 512)
     spread = exchange(pieces, PCOL)

time: 218 us -> 213 us (0.977)
  starting transfers between devices: 104 us -> 96.5 us
  waiting for transfers between devices: 42.5 us -> 45.6 us
    all_to_all x3, starting transfers between devices: 79.6 us -> 53.4 us  [exchange(): return lax.all_to_all(pieces, axes, 0, 0, tiled=True)]
    ppermute x33 -> x28, starting transfers between devices: 24.2 us -> 42.8 us  [send(): return lax.ppermute(x, EVERY, pairs)]
    ppermute x33 -> x28, waiting for transfers between devices: 5.27 us -> 8.39 us  [send(): return lax.ppermute(x, EVERY, pairs)]
  transfers between devices with their start and end apart: 37 -> 32, of which waited for: 4 -> 5; matrix products, arithmetic and copies ran while one was open for 1% -> 1% of each run, Pallas kernels for 6% -> 7%
where the time goes in v7:
time: 213 us; the launch traced here: 212 us
  starting transfers between devices  96.5 us (45%)
  waiting for transfers between devices  45.6 us (21%)
  Pallas kernels  22.6 us (11%)
  between operations  14.6 us (7%)
  blocking collectives  14 us (7%)
  local copies, waits for them, and re-layouts  11.5 us (5%)
  matrix products  7.31 us (3%)
    all_to_all x3, starting transfers between devices, exchange(): return lax.all_to_all(pieces, axes, 0, 0, tiled=True)  53.4 us
    ppermute x28, starting transfers between devices, send(): return lax.ppermute(x, EVERY, pairs)  42.8 us
    all_to_all x3, waiting for transfers between devices, exchange(): return lax.all_to_all(pieces, axes, 0, 0, tiled=True)  37.2 us
    all_to_all x1, blocking collectives, exchange(): return lax.all_to_all(pieces, axes, 0, 0, tiled=True)  14 us
    pallas_call x1, Pallas kernels, form(): pl.pallas_call(form_kernel, in_specs=[hbm, hbm], out_specs=(VMEM,) * 2, o...  11.4 us
    ppermute x28, waiting for transfers between devices, send(): return lax.ppermute(x, EVERY, pairs)  8.39 us
    unnamed x16, local copies, waits for them, and re-layouts  8.35 us
    dot_general x1, matrix products, product(): lax.dot_general(left, right, (((left_dim,), (right_dim,)), ((), ())), pre...  7.31 us
  transfers between devices with their start and end apart: 32, of which 5 were waited for; matrix products, arithmetic and copies ran while one was open for 1% of the time, Pallas kernels for 7%

profile of v7, /device:TPU:1, one launch (start us, length us, event | category | flops | bytes accessed | tf_op | source)
XLA Modules:
  0.0 212.3 jit_solution(7118729905093979116)
XLA Ops:
  7.2 0.0 copy-start
  7.2 1.0 copy-done
  8.2 7.3 %fusion = f32[64,1024]{1,0:T(8,128)S(1)} fusion(f32[64,2048]{1,0:T(8,128)S(1)} %copy-done, f32[1024,2048]{1,0:T(8,128)} %param.10), kind=kOutput, calls=%fused_computation.3 | convolution fusion | flops 805306368 | bytes 9175040 | tf_op jit(solution)/shard_map/dot_general | solution.py:18
  15.5 0.8 reshape.17
  16.3 7.6 %all-to-all-start = ((f32[16,4,1024]{2,1,0:T(4,128)}), f32[16,4,1024]{2,1,0:T(4,128)S(1)}, u32[]{:S(2)}, u32[]{:S(2)}) async-start(f32[16,4,1024]{2,1,0:T(4,128)} %reshape.17), calls=%async_computation | async-start | bytes 524288 | tf_op jit(solution)/shard_map/all_to_all | solution.py:28
  23.9 0.2 all-gather.3.cloned.1.call-start
  24.1 11.4 %shard_map.95 = (bf16[1024,1024]{1,0:T(8,128)(2,1)S(1)}, bf16[1024,1024]{1,0:T(8,128)(2,1)S(1)}) custom-call(f32[1024,1024]{1,0:T(8,128)} %bitcast.22, f32[8192,128]{1,0:T(8,128)} %bitcast.24), custom_call_target="tpu_custom_call" | custom-call | tf_op jit(solution)/shard_map/pallas_call | solution.py:143
  35.5 1.3 copy-done.1
  36.8 0.8 constant_dynamic-slice_fusion.rhs_ref
  37.6 0.0 all-to-all-done
  37.6 0.1 reduce_sum.9.past_ref
  37.6 2.8 %shard_map.96 = f32[4,1024]{1,0:T(4,128)S(1)} custom-call(f32[4,1024]{1,0:T(4,128)S(1)} %constant_dynamic-slice_fusion.rhs_ref, f32[4,1024]{1,0:T(4,128)S(1)} %reduce_sum.9.past_ref, f32[1024,1024]{1,0:T(8,128)} %bitcast.23), custom_call_target="tpu_custom_call" | custom-call | tf_op jit(solution)/shard_map/pallas_call | solution.py:177
  40.5 14.0 %all_to_all.20.pieces_ref = f32[16,4,1024]{2,1,0:T(4,128)S(1)} all-to-all(f32[16,4,1024]{2,1,0:T(4,128)S(1)} %broadcast_in_dim.8), channel_id=1, replica_groups=mesh['prow_0'=4,'prow_1'=2,'pcol_0'=4,'pcol_1'=4] {'pcol_0','pcol_1'}, dimensions={0} | all-to-all | bytes 524288 | tf_op jit(solution)/shard_map/all_to_all | solution.py:28
  54.6 1.3 collective-permute-start
  55.9 0.1 pad_add_fusion.where_ref.row_ref
  56.0 3.6 %collective-permute-done.refs_0_ = f32[64,1024]{1,0:T(8,128)S(1)} collective-permute-done((f32[64,1024]{1,0:T(8,128)S(1)}, f32[64,1024]{1,0:T(8,128)S(1)}, u32[]{:S(2)}, u32[]{:S(2)}) %collective-permute-start) | collective-permute-done | bytes 262176 | tf_op jit(solution)/shard_map/ppermute | solution.py:40
  59.6 1.6 copy-done.2
  61.1 1.3 shard_map.98.before_ref
  62.5 0.7 collective-permute-start.1
  63.2 1.8 collective-permute-start.2
  65.0 1.3 collective-permute-start.3
  66.3 2.0 collective-permute-start.4
  68.3 1.3 collective-permute-start.5
  69.6 16.8 %collective-permute-start.6 = (f32[64,1024]{1,0:T(8,128)S(1)}, f32[64,1024]{1,0:T(8,128)S(1)}, u32[]{:S(2)}, u32[]{:S(2)}) collective-permute-start(f32[64,1024]{1,0:T(8,128)S(1)} %shard_map.98.before_ref), channel_id=1, source_target_pairs={{16,97}} | collective-permute-start | bytes 786440 | tf_op jit(solution)/shard_map/ppermute | solution.py:40
  86.5 1.3 collective-permute-start.7
  87.8 1.9 collective-permute-done.6.refs_4_
  89.7 2.8 %collective-permute-done.7.refs_5_ = f32[64,1024]{1,0:T(8,128)S(1)} collective-permute-done((f32[64,1024]{1,0:T(8,128)S(1)}, f32[64,1024]{1,0:T(8,128)S(1)}, u32[]{:S(2)}, u32[]{:S(2)}) %collective-permute-start.7) | collective-permute-done | bytes 262176 | tf_op jit(solution)/shard_map/ppermute | solution.py:40
  92.5 0.6 shard_map.99.before_ref
  93.1 0.7 collective-permute-start.10
  93.8 0.7 collective-permute-start.11
  94.5 1.4 collective-permute-start.12
  95.9 1.4 collective-permute-start.13
  97.3 1.4 collective-permute-start.8
  98.7 1.4 collective-permute-start.9
  100.0 0.0 all-gather.3.cloned.1.call-update
  100.1 1.6 copy-done.3
  101.7 1.5 shard_map.100.before_ref
  103.1 0.7 collective-permute-start.14
  103.8 0.7 collective-permute-start.15
  104.5 0.7 collective-permute-start.16
  105.2 0.7 collective-permute-start.17
  105.9 0.7 collective-permute-start.18
  106.6 0.6 shard_map.101.before_ref
  107.2 0.7 collective-permute-start.19
  107.9 0.7 collective-permute-start.20
  108.6 0.7 collective-permute-start.21
  109.3 0.7 collective-permute-start.22
  110.0 0.6 shard_map.102.before_ref
  110.6 0.7 collective-permute-start.23
  111.3 0.7 collective-permute-start.24
  111.9 0.7 collective-permute-start.25
  112.7 0.6 shard_map.103.before_ref
  113.3 0.7 collective-permute-start.26
  113.9 0.7 collective-permute-start.27
  114.6 1.3 shard_map.104
  115.9 3.7 %all-to-all-start.2 = ((f32[16,8,512]{2,1,0:T(8,128)}), f32[16,8,512]{2,1,0:T(8,128)S(1)}, u32[]{:S(2)}, u32[]{:S(2)}) async-start(f32[16,8,512]{2,1,0:T(8,128)} %bitcast.8), calls=%async_computation.2 | async-start | bytes 524288 | tf_op jit(solution)/shard_map/all_to_all | solution.py:28
  119.6 7.5 %all-to-all-done.2 = f32[16,8,512]{2,1,0:T(8,128)S(1)} async-done(((f32[16,8,512]{2,1,0:T(8,128)}), f32[16,8,512]{2,1,0:T(8,128)S(1)}, u32[]{:S(2)}, u32[]{:S(2)}) %all-to-all-start.2) | async-done | bytes 262176 | tf_op jit(solution)/shard_map/all_to_all | solution.py:28
  127.1 1.6 broadcast_in_dim.19
  128.7 42.2 %all-to-all-start.3 = ((f32[128,8,512]{2,1,0:T(8,128)}), f32[128,8,512]{2,1,0:T(8,128)S(1)}, u32[]{:S(2)}, u32[]{:S(2)}) async-start(f32[128,8,512]{2,1,0:T(8,128)} %broadcast_in_dim.19), calls=%async_computation.3 | async-start | bytes 4194304 | tf_op jit(solution)/shard_map/all_to_all | solution.py:28
  170.9 0.0 all-gather.3.cloned.1.call-done
  170.9 29.7 %all-to-all-done.3.pieces_ref = f32[128,8,512]{2,1,0:T(8,128)S(1)} async-done(((f32[128,8,512]{2,1,0:T(8,128)}), f32[128,8,512]{2,1,0:T(8,128)S(1)}, u32[]{:S(2)}, u32[]{:S(2)}) %all-to-all-start.3) | async-done | bytes 2097184 | tf_op jit(solution)/shard_map/all_to_all | solution.py:28
  200.6 1.6 copy-done.4
  202.2 1.2 copy-done.5
  203.4 2.0 shard_map.105
  (37 shorter events, 0.2 us)
Async XLA Ops:
  7.2 1.0 copy-start
  16.3 21.3 %all-to-all-start = ((f32[16,4,1024]{2,1,0:T(4,128)}), f32[16,4,1024]{2,1,0:T(4,128)S(1)}, u32[]{:S(2)}, u32[]{:S(2)}) async-start(f32[16,4,1024]{2,1,0:T(4,128)} %reshape.17), calls=%async_computation | async-start | bytes 524288 | tf_op jit(solution)/shard_map/all_to_all | solution.py:28
  23.9 147.0 %all-gather.3.cloned.1.call-start = ((), (), s32[]{:S(2)}) async-start(), calls=%async_computation.4 | async-start | bytes 2359296 | tf_op jit(solution)/shard_map/all_gather | solution.py:286
  35.5 1.3 copy-start.1
  54.6 5.0 %collective-permute-start = (f32[64,1024]{1,0:T(8,128)S(1)}, f32[64,1024]{1,0:T(8,128)S(1)}, u32[]{:S(2)}, u32[]{:S(2)}) collective-permute-start(f32[64,1024]{1,0:T(8,128)S(1)} %shard_map.97.before_ref.base_ref), channel_id=1, source_target_pairs={{0,16},{1,32},{2,48},{3,64},{4,80},{5,96},{6,112}} | collective-permute-start | bytes 786440 | tf_op jit(solution)/shard_map/ppermute | solution.py:40
  59.6 1.6 copy-start.2
  62.5 7.1 %collective-permute-start.1 = (f32[64,1024]{1,0:T(8,128)S(1)}, f32[64,1024]{1,0:T(8,128)S(1)}, u32[]{:S(2)}, u32[]{:S(2)}) collective-permute-start(f32[64,1024]{1,0:T(8,128)S(1)} %shard_map.98.before_ref), channel_id=1, source_target_pairs={{32,33},{48,49},{64,65},{80,81},{96,97},{112,113}} | collective-permute-start | bytes 786440 | tf_op jit(solution)/shard_map/ppermute | solution.py:40
  63.2 23.3 %collective-permute-start.2 = (f32[64,1024]{1,0:T(8,128)S(1)}, f32[64,1024]{1,0:T(8,128)S(1)}, u32[]{:S(2)}, u32[]{:S(2)}) collective-permute-start(f32[64,1024]{1,0:T(8,128)S(1)} %shard_map.98.before_ref), channel_id=1, source_target_pairs={{16,33}} | collective-permute-start | bytes 786440 | tf_op jit(solution)/shard_map/ppermute | solution.py:40
  65.0 22.8 %collective-permute-start.3 = (f32[64,1024]{1,0:T(8,128)S(1)}, f32[64,1024]{1,0:T(8,128)S(1)}, u32[]{:S(2)}, u32[]{:S(2)}) collective-permute-start(f32[64,1024]{1,0:T(8,128)S(1)} %shard_map.98.before_ref), channel_id=1, source_target_pairs={{16,49}} | collective-permute-start | bytes 786440 | tf_op jit(solution)/shard_map/ppermute | solution.py:40
  66.3 21.5 %collective-permute-start.4 = (f32[64,1024]{1,0:T(8,128)S(1)}, f32[64,1024]{1,0:T(8,128)S(1)}, u32[]{:S(2)}, u32[]{:S(2)}) collective-permute-start(f32[64,1024]{1,0:T(8,128)S(1)} %shard_map.98.before_ref), channel_id=1, source_target_pairs={{16,65}} | collective-permute-start | bytes 786440 | tf_op jit(solution)/shard_map/ppermute | solution.py:40
  68.3 19.5 %collective-permute-start.5 = (f32[64,1024]{1,0:T(8,128)S(1)}, f32[64,1024]{1,0:T(8,128)S(1)}, u32[]{:S(2)}, u32[]{:S(2)}) collective-permute-start(f32[64,1024]{1,0:T(8,128)S(1)} %shard_map.98.before_ref), channel_id=1, source_target_pairs={{16,81}} | collective-permute-start | bytes 786440 | tf_op jit(solution)/shard_map/ppermute | solution.py:40
  69.6 20.1 %collective-permute-start.6 = (f32[64,1024]{1,0:T(8,128)S(1)}, f32[64,1024]{1,0:T(8,128)S(1)}, u32[]{:S(2)}, u32[]{:S(2)}) collective-permute-start(f32[64,1024]{1,0:T(8,128)S(1)} %shard_map.98.before_ref), channel_id=1, source_target_pairs={{16,97}} | collective-permute-start | bytes 786440 | tf_op jit(solution)/shard_map/ppermute | solution.py:40
  86.5 6.1 %collective-permute-start.7 = (f32[64,1024]{1,0:T(8,128)S(1)}, f32[64,1024]{1,0:T(8,128)S(1)}, u32[]{:S(2)}, u32[]{:S(2)}) collective-permute-start(f32[64,1024]{1,0:T(8,128)S(1)} %shard_map.98.before_ref), channel_id=1, source_target_pairs={{16,113}} | collective-permute-start | bytes 786440 | tf_op jit(solution)/shard_map/ppermute | solution.py:40
  93.1 5.5 %collective-permute-start.10 = (f32[64,1024]{1,0:T(8,128)S(1)}, f32[64,1024]{1,0:T(8,128)S(1)}, u32[]{:S(2)}, u32[]{:S(2)}) collective-permute-start(f32[64,1024]{1,0:T(8,128)S(1)} %shard_map.99.before_ref), channel_id=1, source_target_pairs={{33,66}} | collective-permute-start | bytes 786440 | tf_op jit(solution)/shard_map/ppermute | solution.py:40
  93.8 6.2 %collective-permute-start.11 = (f32[64,1024]{1,0:T(8,128)S(1)}, f32[64,1024]{1,0:T(8,128)S(1)}, u32[]{:S(2)}, u32[]{:S(2)}) collective-permute-start(f32[64,1024]{1,0:T(8,128)S(1)} %shard_map.99.before_ref), channel_id=1, source_target_pairs={{33,82}} | collective-permute-start | bytes 786440 | tf_op jit(solution)/shard_map/ppermute | solution.py:40
  94.5 5.5 %collective-permute-start.12 = (f32[64,1024]{1,0:T(8,128)S(1)}, f32[64,1024]{1,0:T(8,128)}, u32[]{:S(2)}, u32[]{:S(2)}) collective-permute-start(f32[64,1024]{1,0:T(8,128)S(1)} %shard_map.99.before_ref), channel_id=1, source_target_pairs={{33,98}} | collective-permute-start | bytes 786440 | tf_op jit(solution)/shard_map/ppermute | solution.py:40
  95.9 4.2 %collective-permute-start.13 = (f32[64,1024]{1,0:T(8,128)S(1)}, f32[64,1024]{1,0:T(8,128)}, u32[]{:S(2)}, u32[]{:S(2)}) collective-permute-start(f32[64,1024]{1,0:T(8,128)S(1)} %shard_map.99.before_ref), channel_id=1, source_target_pairs={{33,114}} | collective-permute-start | bytes 786440 | tf_op jit(solution)/shard_map/ppermute | solution.py:40
  97.3 2.8 %collective-permute-start.8 = (f32[64,1024]{1,0:T(8,128)S(1)}, f32[64,1024]{1,0:T(8,128)}, u32[]{:S(2)}, u32[]{:S(2)}) collective-permute-start(f32[64,1024]{1,0:T(8,128)S(1)} %shard_map.99.before_ref), channel_id=1, source_target_pairs={{49,50},{65,66},{81,82},{97,98},{113,114}} | collective-permute-start | bytes 786440 | tf_op jit(solution)/shard_map/ppermute | solution.py:40
  98.7 1.4 collective-permute-start.9
  100.1 1.6 copy-start.3
  103.1 3.4 %collective-permute-start.14 = (f32[64,1024]{1,0:T(8,128)S(1)}, f32[64,1024]{1,0:T(8,128)S(1)}, u32[]{:S(2)}, u32[]{:S(2)}) collective-permute-start(f32[64,1024]{1,0:T(8,128)S(1)} %shard_map.100.before_ref), channel_id=1, source_target_pairs={{66,67},{82,83},{98,99},{114,115}} | collective-permute-start | bytes 786440 | tf_op jit(solution)/shard_map/ppermute | solution.py:40
  103.8 2.8 %collective-permute-start.15 = (f32[64,1024]{1,0:T(8,128)S(1)}, f32[64,1024]{1,0:T(8,128)S(1)}, u32[]{:S(2)}, u32[]{:S(2)}) collective-permute-start(f32[64,1024]{1,0:T(8,128)S(1)} %shard_map.100.before_ref), channel_id=1, source_target_pairs={{50,67}} | collective-permute-start | bytes 786440 | tf_op jit(solution)/shard_map/ppermute | solution.py:40
  104.5 2.1 collective-permute-start.16
  105.2 1.4 collective-permute-start.17
  105.9 0.7 collective-permute-start.18
  107.2 2.7 %collective-permute-start.19 = (f32[64,1024]{1,0:T(8,128)S(1)}, f32[64,1024]{1,0:T(8,128)S(1)}, u32[]{:S(2)}, u32[]{:S(2)}) collective-permute-start(f32[64,1024]{1,0:T(8,128)S(1)} %shard_map.101.before_ref), channel_id=1, source_target_pairs={{83,84},{99,100},{115,116}} | collective-permute-start | bytes 786440 | tf_op jit(solution)/shard_map/ppermute | solution.py:40
  107.9 2.1 collective-permute-start.20
  108.6 1.4 collective-permute-start.21
  109.3 0.7 collective-permute-start.22
  110.6 2.1 collective-permute-start.23
  111.3 1.4 collective-permute-start.24
  111.9 0.7 collective-permute-start.25
  113.3 1.4 collective-permute-start.26
  113.9 0.7 collective-permute-start.27
  115.9 84.7 %copy-start.6 = (s32[1,2,8]{2,1,0:T(2,128)S(1)}, s32[1,2,8]{2,1,0:T(2,128)}, u32[]{:S(2)}) copy-start(s32[1,2,8]{2,1,0:T(2,128)} %param.14) | copy-start | bytes 196
  115.9 84.7 %copy-start.7 = (s32[1,2]{1,0:T(1,128)S(1)}, s32[1,2]{1,0:T(1,128)}, u32[]{:S(2)}) copy-start(s32[1,2]{1,0:T(1,128)} %param.13) | copy-start | bytes 28
  115.9 11.2 %all-to-all-start.2 = ((f32[16,8,512]{2,1,0:T(8,128)}), f32[16,8,512]{2,1,0:T(8,128)S(1)}, u32[]{:S(2)}, u32[]{:S(2)}) async-start(f32[16,8,512]{2,1,0:T(8,128)} %bitcast.8), calls=%async_computation.2 | async-start | bytes 524288 | tf_op jit(solution)/shard_map/all_to_all | solution.py:28
  128.7 71.9 %all-to-all-start.3 = ((f32[128,8,512]{2,1,0:T(8,128)}), f32[128,8,512]{2,1,0:T(8,128)S(1)}, u32[]{:S(2)}, u32[]{:S(2)}) async-start(f32[128,8,512]{2,1,0:T(8,128)} %broadcast_in_dim.19), calls=%async_computation.3 | async-start | bytes 4194304 | tf_op jit(solution)/shard_map/all_to_all | solution.py:28
  200.6 1.6 copy-start.4
  202.2 1.2 copy-start.5
Sparse Core Ops, SparseCore 0:
  100.2 24.2 all-gather.2

commit v8 on v7

--- a/solution.py
+++ b/solution.py
@@ -299,6 +299,8 @@
         knowns = [send(current, [(source, place(k, step))]) for k in range(step + 1, ROWS)]
         partial = send(current, [(place(k, step - 1), place(k, step)) for k in range(step + 1, ROWS)])
         current = fire(step, where, current, partial, knowns, high, low)
+        if step == 3:
+            current, full_rhs = lax.optimization_barrier((current, full_rhs))
 
     pieces = current.reshape(8, 8, 2, 512).transpose(0, 2, 1, 3).reshape(COLS, 8, 512)
     spread = exchange(pieces, PCOL)

time: 213 us -> 206 us (0.967)
  blocking collectives: 14 us -> 86.9 us
  starting transfers between devices: 96.5 us -> 51.5 us
  waiting for transfers between devices: 45.6 us -> 16.6 us
  local copies, waits for them, and re-layouts: 11.5 us -> 6.66 us
    all_to_all x1 -> x2, blocking collectives: 14 us -> 86.9 us  [exchange(): return lax.all_to_all(pieces, axes, 0, 0, tiled=True)]
    all_to_all x3 -> x2, starting transfers between devices: 53.4 us -> 11.3 us  [exchange(): return lax.all_to_all(pieces, axes, 0, 0, tiled=True)]
    all_to_all x3 -> x2, waiting for transfers between devices: 37.2 us -> 7.5 us  [exchange(): return lax.all_to_all(pieces, axes, 0, 0, tiled=True)]
    unnamed x16, local copies, waits for them, and re-layouts: 8.35 us -> 4.82 us
    ppermute x28, starting transfers between devices: 42.8 us -> 40.2 us  [send(): return lax.ppermute(x, EVERY, pairs)]
  transfers between devices with their start and end apart: 32 -> 31, of which waited for: 5 -> 4; matrix products, arithmetic and copies ran while one was open for 1% -> 4% of each run, Pallas kernels for 7% -> 8%
where the time goes in v8:
time: 206 us
  blocking collectives  86.9 us (42%)
  starting transfers between devices  51.5 us (25%)
  Pallas kernels  21.9 us (11%)
  waiting for transfers between devices  16.6 us (8%)
  between operations  14.6 us (7%)
  matrix products  7.31 us (4%)
  local copies, waits for them, and re-layouts  6.66 us (3%)
    all_to_all x2, blocking collectives, exchange(): return lax.all_to_all(pieces, axes, 0, 0, tiled=True)  86.9 us
    ppermute x28, starting transfers between devices, send(): return lax.ppermute(x, EVERY, pairs)  40.2 us
    all_to_all x2, starting transfers between devices, exchange(): return lax.all_to_all(pieces, axes, 0, 0, tiled=True)  11.3 us
    pallas_call x1, Pallas kernels, form(): pl.pallas_call(form_kernel, in_specs=[hbm, hbm], out_specs=(VMEM,) * 2, o...  11.2 us
    ppermute x28, waiting for transfers between devices, send(): return lax.ppermute(x, EVERY, pairs)  8.38 us
    all_to_all x2, waiting for transfers between devices, exchange(): return lax.all_to_all(pieces, axes, 0, 0, tiled=True)  7.5 us
    dot_general x1, matrix products, product(): lax.dot_general(left, right, (((left_dim,), (right_dim,)), ((), ())), pre...  7.31 us
    pallas_call x7, Pallas kernels, fire(): pl.pallas_call(kernel, in_specs=[SMEM] + [VMEM] * (len(knowns) + 4), out_...  5.75 us
  transfers between devices with their start and end apart: 31, of which 4 were waited for; matrix products, arithmetic and copies ran while one was open for 4% of the time, Pallas kernels for 8%

profile of v8, /device:TPU:1, one launch (start us, length us, event | category | flops | bytes accessed | tf_op | source)
XLA Modules:
  0.0 205.5 jit_solution(2504863626005955128)
XLA Ops:
  7.2 0.0 copy-start
  7.2 0.0 all-gather.3.cloned.1.call-start
  7.2 0.7 all-gather.3.cloned.1.call-update
  7.9 0.3 copy-done
  8.2 7.3 %fusion = f32[64,1024]{1,0:T(8,128)S(1)} fusion(f32[64,2048]{1,0:T(8,128)S(1)} %copy-done, f32[1024,2048]{1,0:T(8,128)} %param.10), kind=kOutput, calls=%fused_computation.3 | convolution fusion | flops 805306368 | bytes 9175040 | tf_op jit(solution)/shard_map/dot_general | solution.py:18
  15.5 0.8 reshape.17
  16.3 7.6 %all-to-all-start = ((f32[16,4,1024]{2,1,0:T(4,128)}), f32[16,4,1024]{2,1,0:T(4,128)S(1)}, u32[]{:S(2)}, u32[]{:S(2)}) async-start(f32[16,4,1024]{2,1,0:T(4,128)} %reshape.17), calls=%async_computation | async-start | bytes 524288 | tf_op jit(solution)/shard_map/all_to_all | solution.py:28
  23.9 11.2 %shard_map.95 = (bf16[1024,1024]{1,0:T(8,128)(2,1)S(1)}, bf16[1024,1024]{1,0:T(8,128)(2,1)S(1)}) custom-call(f32[1024,1024]{1,0:T(8,128)} %bitcast.22, f32[8192,128]{1,0:T(8,128)} %bitcast.24), custom_call_target="tpu_custom_call" | custom-call | tf_op jit(solution)/shard_map/pallas_call | solution.py:143
  35.2 1.3 copy-done.1
  36.5 0.8 constant_dynamic-slice_fusion.rhs_ref
  37.3 0.1 reduce_sum.9.past_ref
  37.3 2.8 %shard_map.96 = f32[4,1024]{1,0:T(4,128)S(1)} custom-call(f32[4,1024]{1,0:T(4,128)S(1)} %constant_dynamic-slice_fusion.rhs_ref, f32[4,1024]{1,0:T(4,128)S(1)} %reduce_sum.9.past_ref, f32[1024,1024]{1,0:T(8,128)} %bitcast.23), custom_call_target="tpu_custom_call" | custom-call | tf_op jit(solution)/shard_map/pallas_call | solution.py:177
  40.2 14.0 %all_to_all.20.pieces_ref = f32[16,4,1024]{2,1,0:T(4,128)S(1)} all-to-all(f32[16,4,1024]{2,1,0:T(4,128)S(1)} %broadcast_in_dim.8), channel_id=1, replica_groups=mesh['prow_0'=4,'prow_1'=2,'pcol_0'=4,'pcol_1'=4] {'pcol_0','pcol_1'}, dimensions={0} | all-to-all | bytes 524288 | tf_op jit(solution)/shard_map/all_to_all | solution.py:28
  54.2 1.3 collective-permute-start
  55.6 0.1 pad_add_fusion.where_ref.row_ref
  55.6 3.6 %collective-permute-done.refs_0_ = f32[64,1024]{1,0:T(8,128)S(1)} collective-permute-done((f32[64,1024]{1,0:T(8,128)S(1)}, f32[64,1024]{1,0:T(8,128)S(1)}, u32[]{:S(2)}, u32[]{:S(2)}) %collective-permute-start) | collective-permute-done | bytes 262176 | tf_op jit(solution)/shard_map/ppermute | solution.py:40
  59.2 1.6 copy-done.2
  60.8 1.4 shard_map.98.before_ref
  62.2 0.7 collective-permute-start.1
  62.9 1.8 collective-permute-start.2
  64.7 1.3 collective-permute-start.3
  66.0 2.0 collective-permute-start.4
  68.0 1.3 collective-permute-start.5
  69.4 0.0 collective-permute-done.1.base_ref
  69.4 16.9 %collective-permute-start.6 = (f32[64,1024]{1,0:T(8,128)S(1)}, f32[64,1024]{1,0:T(8,128)S(1)}, u32[]{:S(2)}, u32[]{:S(2)}) collective-permute-start(f32[64,1024]{1,0:T(8,128)S(1)} %shard_map.98.before_ref), channel_id=1, source_target_pairs={{16,97}} | collective-permute-start | bytes 786440 | tf_op jit(solution)/shard_map/ppermute | solution.py:40
  86.2 0.0 collective-permute-done.2.refs_0_
  86.3 1.3 collective-permute-start.7
  87.6 0.0 collective-permute-done.5.refs_3_
  87.6 1.9 collective-permute-done.6.refs_4_
  89.5 2.8 %collective-permute-done.7.refs_5_ = f32[64,1024]{1,0:T(8,128)S(1)} collective-permute-done((f32[64,1024]{1,0:T(8,128)S(1)}, f32[64,1024]{1,0:T(8,128)S(1)}, u32[]{:S(2)}, u32[]{:S(2)}) %collective-permute-start.7) | collective-permute-done | bytes 262176 | tf_op jit(solution)/shard_map/ppermute | solution.py:40
  92.3 0.6 shard_map.99.before_ref
  92.9 0.7 collective-permute-start.10
  93.6 0.7 collective-permute-start.11
  94.3 0.7 collective-permute-start.12
  95.0 0.7 collective-permute-start.13
  95.7 0.7 collective-permute-start.8
  96.4 0.0 collective-permute-done.10.refs_1_
  96.4 0.7 collective-permute-start.9
  97.1 0.8 shard_map.100.before_ref
  97.9 0.7 collective-permute-start.14
  98.6 0.7 collective-permute-start.15
  99.3 0.7 collective-permute-start.16
  100.0 0.7 collective-permute-start.17
  100.6 0.7 collective-permute-start.18
  101.4 0.6 shard_map.101.before_ref
  102.0 0.0 all-gather.3.cloned.1.call-done
  102.0 0.7 collective-permute-start.19
  102.7 0.7 collective-permute-start.20
  103.4 0.7 collective-permute-start.21
  104.1 0.7 collective-permute-start.22
  104.8 1.6 copy-done.3
  106.4 0.6 shard_map.102.before_ref
  107.0 0.7 collective-permute-start.23
  107.6 0.7 collective-permute-start.24
  108.3 0.7 collective-permute-start.25
  109.0 0.6 shard_map.103.before_ref
  109.6 0.7 collective-permute-start.26
  110.3 0.7 collective-permute-start.27
  111.0 1.3 shard_map.104
  112.3 3.7 %all-to-all-start.2 = ((f32[16,8,512]{2,1,0:T(8,128)}), f32[16,8,512]{2,1,0:T(8,128)S(1)}, u32[]{:S(2)}, u32[]{:S(2)}) async-start(f32[16,8,512]{2,1,0:T(8,128)} %bitcast.9), calls=%async_computation.2 | async-start | bytes 524288 | tf_op jit(solution)/shard_map/all_to_all | solution.py:28
  116.0 7.5 %all-to-all-done.2 = f32[16,8,512]{2,1,0:T(8,128)S(1)} async-done(((f32[16,8,512]{2,1,0:T(8,128)}), f32[16,8,512]{2,1,0:T(8,128)S(1)}, u32[]{:S(2)}, u32[]{:S(2)}) %all-to-all-start.2) | async-done | bytes 262176 | tf_op jit(solution)/shard_map/all_to_all | solution.py:28
  123.5 0.3 broadcast_in_dim.19
  123.8 72.9 %all_to_all.21.pieces_ref = f32[128,8,512]{2,1,0:T(8,128)S(1)} all-to-all(f32[128,8,512]{2,1,0:T(8,128)S(1)} %broadcast_in_dim.19), channel_id=1, replica_groups=mesh['prow_0'=4,'prow_1'=2,'pcol_0'=4,'pcol_1'=4] {'prow_0','prow_1','pc..., dimensions={0} | all-to-all | bytes 4194304 | tf_op jit(solution)/shard_map/all_to_all | solution.py:28
  196.7 2.0 shard_map.105
  (36 shorter events, 0.2 us)
Async XLA Ops:
  7.2 1.0 copy-start
  7.2 94.8 %all-gather.3.cloned.1.call-start = ((), (), s32[]{:S(2)}) async-start(), calls=%async_computation.4 | async-start | bytes 2359296 | tf_op jit(solution)/shard_map/all_gather | solution.py:286
  16.3 21.0 %all-to-all-start = ((f32[16,4,1024]{2,1,0:T(4,128)}), f32[16,4,1024]{2,1,0:T(4,128)S(1)}, u32[]{:S(2)}, u32[]{:S(2)}) async-start(f32[16,4,1024]{2,1,0:T(4,128)} %reshape.17), calls=%async_computation | async-start | bytes 524288 | tf_op jit(solution)/shard_map/all_to_all | solution.py:28
  35.2 1.3 copy-start.1
  54.2 5.0 %collective-permute-start = (f32[64,1024]{1,0:T(8,128)S(1)}, f32[64,1024]{1,0:T(8,128)S(1)}, u32[]{:S(2)}, u32[]{:S(2)}) collective-permute-start(f32[64,1024]{1,0:T(8,128)S(1)} %shard_map.97.before_ref.base_ref), channel_id=1, source_target_pairs={{0,16},{1,32},{2,48},{3,64},{4,80},{5,96},{6,112}} | collective-permute-start | bytes 786440 | tf_op jit(solution)/shard_map/ppermute | solution.py:40
  59.2 1.6 copy-start.2
  62.2 7.2 %collective-permute-start.1 = (f32[64,1024]{1,0:T(8,128)S(1)}, f32[64,1024]{1,0:T(8,128)S(1)}, u32[]{:S(2)}, u32[]{:S(2)}) collective-permute-start(f32[64,1024]{1,0:T(8,128)S(1)} %shard_map.98.before_ref), channel_id=1, source_target_pairs={{32,33},{48,49},{64,65},{80,81},{96,97},{112,113}} | collective-permute-start | bytes 786440 | tf_op jit(solution)/shard_map/ppermute | solution.py:40
  62.9 23.4 %collective-permute-start.2 = (f32[64,1024]{1,0:T(8,128)S(1)}, f32[64,1024]{1,0:T(8,128)S(1)}, u32[]{:S(2)}, u32[]{:S(2)}) collective-permute-start(f32[64,1024]{1,0:T(8,128)S(1)} %shard_map.98.before_ref), channel_id=1, source_target_pairs={{16,33}} | collective-permute-start | bytes 786440 | tf_op jit(solution)/shard_map/ppermute | solution.py:40
  64.7 22.9 %collective-permute-start.3 = (f32[64,1024]{1,0:T(8,128)S(1)}, f32[64,1024]{1,0:T(8,128)S(1)}, u32[]{:S(2)}, u32[]{:S(2)}) collective-permute-start(f32[64,1024]{1,0:T(8,128)S(1)} %shard_map.98.before_ref), channel_id=1, source_target_pairs={{16,49}} | collective-permute-start | bytes 786440 | tf_op jit(solution)/shard_map/ppermute | solution.py:40
  66.0 21.6 %collective-permute-start.4 = (f32[64,1024]{1,0:T(8,128)S(1)}, f32[64,1024]{1,0:T(8,128)S(1)}, u32[]{:S(2)}, u32[]{:S(2)}) collective-permute-start(f32[64,1024]{1,0:T(8,128)S(1)} %shard_map.98.before_ref), channel_id=1, source_target_pairs={{16,65}} | collective-permute-start | bytes 786440 | tf_op jit(solution)/shard_map/ppermute | solution.py:40
  68.0 19.6 %collective-permute-start.5 = (f32[64,1024]{1,0:T(8,128)S(1)}, f32[64,1024]{1,0:T(8,128)S(1)}, u32[]{:S(2)}, u32[]{:S(2)}) collective-permute-start(f32[64,1024]{1,0:T(8,128)S(1)} %shard_map.98.before_ref), channel_id=1, source_target_pairs={{16,81}} | collective-permute-start | bytes 786440 | tf_op jit(solution)/shard_map/ppermute | solution.py:40
  69.4 20.2 %collective-permute-start.6 = (f32[64,1024]{1,0:T(8,128)S(1)}, f32[64,1024]{1,0:T(8,128)S(1)}, u32[]{:S(2)}, u32[]{:S(2)}) collective-permute-start(f32[64,1024]{1,0:T(8,128)S(1)} %shard_map.98.before_ref), channel_id=1, source_target_pairs={{16,97}} | collective-permute-start | bytes 786440 | tf_op jit(solution)/shard_map/ppermute | solution.py:40
  86.3 6.1 %collective-permute-start.7 = (f32[64,1024]{1,0:T(8,128)S(1)}, f32[64,1024]{1,0:T(8,128)S(1)}, u32[]{:S(2)}, u32[]{:S(2)}) collective-permute-start(f32[64,1024]{1,0:T(8,128)S(1)} %shard_map.98.before_ref), channel_id=1, source_target_pairs={{16,113}} | collective-permute-start | bytes 786440 | tf_op jit(solution)/shard_map/ppermute | solution.py:40
  92.9 3.4 %collective-permute-start.10 = (f32[64,1024]{1,0:T(8,128)S(1)}, f32[64,1024]{1,0:T(8,128)S(1)}, u32[]{:S(2)}, u32[]{:S(2)}) collective-permute-start(f32[64,1024]{1,0:T(8,128)S(1)} %shard_map.99.before_ref), channel_id=1, source_target_pairs={{33,66}} | collective-permute-start | bytes 786440 | tf_op jit(solution)/shard_map/ppermute | solution.py:40
  93.6 3.4 %collective-permute-start.11 = (f32[64,1024]{1,0:T(8,128)S(1)}, f32[64,1024]{1,0:T(8,128)S(1)}, u32[]{:S(2)}, u32[]{:S(2)}) collective-permute-start(f32[64,1024]{1,0:T(8,128)S(1)} %shard_map.99.before_ref), channel_id=1, source_target_pairs={{33,82}} | collective-permute-start | bytes 786440 | tf_op jit(solution)/shard_map/ppermute | solution.py:40
  94.3 2.8 %collective-permute-start.12 = (f32[64,1024]{1,0:T(8,128)S(1)}, f32[64,1024]{1,0:T(8,128)S(1)}, u32[]{:S(2)}, u32[]{:S(2)}) collective-permute-start(f32[64,1024]{1,0:T(8,128)S(1)} %shard_map.99.before_ref), channel_id=1, source_target_pairs={{33,98}} | collective-permute-start | bytes 786440 | tf_op jit(solution)/shard_map/ppermute | solution.py:40
  95.0 2.1 %collective-permute-start.13 = (f32[64,1024]{1,0:T(8,128)S(1)}, f32[64,1024]{1,0:T(8,128)S(1)}, u32[]{:S(2)}, u32[]{:S(2)}) collective-permute-start(f32[64,1024]{1,0:T(8,128)S(1)} %shard_map.99.before_ref), channel_id=1, source_target_pairs={{33,114}} | collective-permute-start | bytes 786440 | tf_op jit(solution)/shard_map/ppermute | solution.py:40
  95.7 1.4 collective-permute-start.8
  96.4 0.7 collective-permute-start.9
  97.9 3.4 %collective-permute-start.14 = (f32[64,1024]{1,0:T(8,128)S(1)}, f32[64,1024]{1,0:T(8,128)S(1)}, u32[]{:S(2)}, u32[]{:S(2)}) collective-permute-start(f32[64,1024]{1,0:T(8,128)S(1)} %shard_map.100.before_ref), channel_id=1, source_target_pairs={{66,67},{82,83},{98,99},{114,115}} | collective-permute-start | bytes 786440 | tf_op jit(solution)/shard_map/ppermute | solution.py:40
  98.6 2.8 %collective-permute-start.15 = (f32[64,1024]{1,0:T(8,128)S(1)}, f32[64,1024]{1,0:T(8,128)S(1)}, u32[]{:S(2)}, u32[]{:S(2)}) collective-permute-start(f32[64,1024]{1,0:T(8,128)S(1)} %shard_map.100.before_ref), channel_id=1, source_target_pairs={{50,67}} | collective-permute-start | bytes 786440 | tf_op jit(solution)/shard_map/ppermute | solution.py:40
  99.3 2.1 %collective-permute-start.16 = (f32[64,1024]{1,0:T(8,128)S(1)}, f32[64,1024]{1,0:T(8,128)S(1)}, u32[]{:S(2)}, u32[]{:S(2)}) collective-permute-start(f32[64,1024]{1,0:T(8,128)S(1)} %shard_map.100.before_ref), channel_id=1, source_target_pairs={{50,83}} | collective-permute-start | bytes 786440 | tf_op jit(solution)/shard_map/ppermute | solution.py:40
  100.0 1.4 collective-permute-start.17
  100.6 0.7 collective-permute-start.18
  102.0 2.7 %collective-permute-start.19 = (f32[64,1024]{1,0:T(8,128)S(1)}, f32[64,1024]{1,0:T(8,128)S(1)}, u32[]{:S(2)}, u32[]{:S(2)}) collective-permute-start(f32[64,1024]{1,0:T(8,128)S(1)} %shard_map.101.before_ref), channel_id=1, source_target_pairs={{83,84},{99,100},{115,116}} | collective-permute-start | bytes 786440 | tf_op jit(solution)/shard_map/ppermute | solution.py:40
  102.7 2.1 %collective-permute-start.20 = (f32[64,1024]{1,0:T(8,128)S(1)}, f32[64,1024]{1,0:T(8,128)S(1)}, u32[]{:S(2)}, u32[]{:S(2)}) collective-permute-start(f32[64,1024]{1,0:T(8,128)S(1)} %shard_map.101.before_ref), channel_id=1, source_target_pairs={{67,84}} | collective-permute-start | bytes 786440 | tf_op jit(solution)/shard_map/ppermute | solution.py:40
  103.4 1.4 collective-permute-start.21
  104.1 0.7 collective-permute-start.22
  104.8 1.6 copy-start.3
  107.0 2.1 %collective-permute-start.23 = (f32[64,1024]{1,0:T(8,128)S(1)}, f32[64,1024]{1,0:T(8,128)S(1)}, u32[]{:S(2)}, u32[]{:S(2)}) collective-permute-start(f32[64,1024]{1,0:T(8,128)S(1)} %shard_map.102.before_ref), channel_id=1, source_target_pairs={{100,101},{116,117}} | collective-permute-start | bytes 786440 | tf_op jit(solution)/shard_map/ppermute | solution.py:40
  107.6 1.4 collective-permute-start.24
  108.3 0.7 collective-permute-start.25
  109.6 1.4 collective-permute-start.26
  110.3 0.7 collective-permute-start.27
  112.3 84.4 %copy-start.4 = (f32[512,1024]{1,0:T(8,128)S(1)}, f32[512,1024]{1,0:T(8,128)}, u32[]{:S(2)}) copy-start(f32[512,1024]{1,0:T(8,128)} %all-gather.3.cloned.1.call-done) | copy-start | bytes 6291460
  112.3 84.4 %copy-start.6 = (s32[1,2,8]{2,1,0:T(2,128)S(1)}, s32[1,2,8]{2,1,0:T(2,128)}, u32[]{:S(2)}) copy-start(s32[1,2,8]{2,1,0:T(2,128)} %param.14) | copy-start | bytes 196
  112.3 84.4 %copy-start.7 = (s32[1,2]{1,0:T(1,128)S(1)}, s32[1,2]{1,0:T(1,128)}, u32[]{:S(2)}) copy-start(s32[1,2]{1,0:T(1,128)} %param.13) | copy-start | bytes 28
  112.3 11.2 %all-to-all-start.2 = ((f32[16,8,512]{2,1,0:T(8,128)}), f32[16,8,512]{2,1,0:T(8,128)S(1)}, u32[]{:S(2)}, u32[]{:S(2)}) async-start(f32[16,8,512]{2,1,0:T(8,128)} %bitcast.9), calls=%async_computation.2 | async-start | bytes 524288 | tf_op jit(solution)/shard_map/all_to_all | solution.py:28
  123.5 73.2 %copy-start.5 = (f32[1,2,8,128,128]{4,3,2,1,0:T(8,128)S(1)}, f32[1,2,8,128,128]{4,3,2,1,0:T(8,128)}, u32[]{:S(2)}) copy-start(f32[1,2,8,128,128]{4,3,2,1,0:T(8,128)} %param.15) | copy-start | bytes 3145732
Sparse Core Ops, SparseCore 0:
  9.7 29.0 all-gather.2
